TPU v7x, 32 devices: a whole 2x2x4 slice. The times are simulated.
32 devices in a mesh: tok: 8 (over z, core), voc: 4 (over y, x).
Axes of the slice: x: 2, y: 2, z: 4, core: 2. Of those that a mesh axis runs over, the one named last changes fastest.
Arguments:
- hidden: bfloat16 [4096, 1024], P('tok'), may hold values from -64 to 64
- head_weight: bfloat16 [1024, 16384], P('tok', 'voc'), may hold values from -1 to 1
- target_logits: bfloat16 [4096, 16384], P('tok', 'voc'), may hold values from -320 to 320
- token_ids: int32 [4096], P('tok'), may hold values from 0 to 16383
Outputs:
- loss: float32 [], replicated
- grad_hidden: float32 [4096, 1024], P('tok', 'voc')
- grad_head: float32 [1024, 16384], P('tok', 'voc')
All inputs are finite; a program needn't handle non-finite values.
Results may differ from a plain program's by a relative error of at most 0.015.
Values may be sent and summed in bfloat16 or wider, within the bound.
No kernel may reach another device: no remote copies, remote signals or barrier semaphores. Data moves between devices by JAX's collectives and lax.ppermute only.
A program may use at most 128 MiB of HBM per device.

v0:
```python
import jax
import jax.numpy as jnp
from jax import lax
from jax.sharding import PartitionSpec as P

ce_weight = 0.5


def body(hidden, head_weight, target_logits, token_ids):
    rows = hidden.shape[0]
    share = head_weight.shape[1]
    vocab_start = lax.axis_index("voc") * share
    whole = lax.all_gather(head_weight, "tok", axis=0, tiled=True)
    draft = jnp.dot(hidden, whole, preferred_element_type=jnp.float32)
    target = target_logits.astype(jnp.float32)
    target_max, draft_max = lax.pmax((jnp.max(target, axis=1), jnp.max(draft, axis=1)), "voc")
    target_exp = jnp.exp(target - target_max[:, None])
    draft_exp = jnp.exp(draft - draft_max[:, None])
    target_sum, draft_sum = lax.psum(
        (jnp.sum(target_exp, axis=1), jnp.sum(draft_exp, axis=1)), "voc"
    )
    probs_p = target_exp / target_sum[:, None]
    probs_q = draft_exp / draft_sum[:, None]
    lse_t = target_max + jnp.log(target_sum)
    lse_z = draft_max + jnp.log(draft_sum)
    column = lax.broadcasted_iota(jnp.int32, (rows, share), 1) + vocab_start
    own = (column == token_ids[:, None]).astype(jnp.float32)
    voc_count = lax.axis_size("voc")
    per_token = jnp.sum(probs_p * (target - draft) - ce_weight * own * draft, axis=1)
    per_token = per_token + ((1.0 + ce_weight) * lse_z - lse_t) / voc_count
    total = lax.psum(jnp.sum(per_token), ("tok", "voc"))
    loss = total / (rows * lax.axis_size("tok"))
    slope = ((1.0 + ce_weight) * probs_q - probs_p - ce_weight * own).astype(jnp.bfloat16)
    partial_grad = lax.dot_general(
        slope, whole, (((1,), (1,)), ((), ())), preferred_element_type=jnp.float32
    )
    grad_hidden = lax.psum_scatter(
        partial_grad.astype(jnp.bfloat16), "voc", scatter_dimension=1, tiled=True
    ).astype(jnp.float32)
    grad_head = lax.psum_scatter(
        lax.dot_general(
            hidden, slope, (((0,), (0,)), ((), ())), preferred_element_type=jnp.float32
        ).astype(jnp.bfloat16),
        "tok",
        scatter_dimension=0,
        tiled=True,
    ).astype(jnp.float32)
    return (loss, grad_hidden, grad_head)


def solution(mesh):
    placed = (P("tok", None), P("tok", "voc"), P("tok", "voc"), P("tok"))
    return jax.shard_map(
        body,
        mesh=mesh,
        in_specs=placed,
        out_specs=(P(), P("tok", "voc"), P("tok", "voc")),
        check_vma=False,
    )
```

profile of v0, /device:TPU:0, one launch (start us, length us, event | category | flops | bytes accessed | tf_op | source)
XLA Modules:
  0.0 290.3 jit_solution(11293099033932415413)
XLA Ops:
  7.2 0.0 all-gather.2.cloned.1.call-start
  7.2 0.7 all-gather.2.cloned.1.call-update
  7.9 0.0 reduce-scatter.5.cloned.1.call-start
  8.0 2.8 reduce_max.23
  10.8 83.6 %all-gather.2.cloned.1.call-done = bf16[1024,4096]{1,0:T(8,128)(2,1)} async-done(((bf16[128,4096]{1,0:T(8,128)(2,1)}), bf16[1024,4096]{1,0:T(8,128)(2,1)}) %all-gather.2.cloned.1.call-update) | async-done | bytes 8388624 | tf_op jit(solution)/shard_map/all_gather | solution.py:13
  94.4 10.1 %fusion.8 = (f32[512]{0:T(512)S(1)}, f32[512,4096]{1,0:T(8,128)}) fusion(bf16[512,1024]{1,0:T(8,128)(2,1)S(1)} %copy-done, bf16[1024,4096]{1,0:T(8,128)(2,1)} %all-gather.2.cloned.1.call-done), kind=kOutput, calls=%fused_computation.17 | convolution fusion | flops 4297063936 | bytes 17827840 | tf_op jit(solution)/shard_map/dot_general | solution.py:14
  104.5 9.8 %all-reduce = (f32[512]{0:T(512)S(1)}, f32[512]{0:T(512)S(1)}) all-reduce(f32[512]{0:T(512)S(1)} %get-tuple-element.13, bf16[512]{0:T(512)(128)(2,1)S(1)} %reduce_max.23), channel_id=1, replica_groups=mesh['tok'=8,'voc'=4] {'voc'}, use_global_device_ids=true, to_apply=%region_6.0 | all-reduce | flops 1024 | bytes 7168 | tf_op jit(solution)/shard_map/pmax | solution.py:16
  114.3 3.7 %fusion.2 = f32[512]{0:T(512)S(1)} fusion(bf16[512,4096]{1,0:T(8,128)(2,1)} %param.6, f32[512]{0:T(512)S(1)} %get-tuple-element.12), kind=kLoop, calls=%fused_computation.6 | loop fusion | flops 6290944 | bytes 4198400 | tf_op jit(solution)/shard_map/reduce_sum | solution.py:20
  118.0 8.0 %psum.21 = f32[512]{0:T(512)S(1)} all-reduce(f32[512]{0:T(512)S(1)} %fusion.2), channel_id=1, replica_groups=mesh['tok'=8,'voc'=4] {'voc'}, use_global_device_ids=true, to_apply=%region_3.0 | all-reduce | flops 512 | bytes 4096 | tf_op jit(solution)/shard_map/psum | solution.py:19
  126.0 7.6 %fusion.7 = (f32[512]{0:T(512)S(1)}, f32[512]{0:T(512)S(1)}) fusion(f32[512,4096]{1,0:T(8,128)} %get-tuple-element.14, f32[512]{0:T(512)S(1)} %get-tuple-element.11, s32[512]{0:T(512)S(1)} %copy-done.2, s32[4096]{0:T(1024)S(1)} %iota_add_fusion, f32[512]{0:T(512)S(1)} %psum.21, f32[512]{0:T(512)S(1)} %get-tuple-element.12, bf16[512,4096]{1,0:T(8,128)(2,1)} %param.6), kind=kLoop, calls=%fused_computation.13 | loop fusion | flops 25164800 | bytes 12611584 | tf_op jit(solution)/shard_map/reduce_sum | solution.py:20
  133.6 9.2 %psum.22 = f32[512]{0:T(512)S(1)} all-reduce(f32[512]{0:T(512)S(1)} %get-tuple-element.9), channel_id=1, replica_groups=mesh['tok'=8,'voc'=4] {'voc'}, use_global_device_ids=true, to_apply=%region_8.0 | all-reduce | flops 512 | bytes 4096 | tf_op jit(solution)/shard_map/psum | solution.py:19
  142.7 8.1 %fusion.6 = bf16[512,4096]{1,0:T(8,128)(2,1)S(1)} fusion(f32[512,4096]{1,0:T(8,128)} %get-tuple-element.14, bf16[512,4096]{1,0:T(8,128)(2,1)} %param.6, f32[512]{0:T(512)S(1)} %psum.22, f32[512]{0:T(512)S(1)} %get-tuple-element.11, s32[4096]{0:T(1024)S(1)} %iota_add_fusion, f32[512]{0:T(512)S(1)} %psum.21, f32[512]{0:T(512)S(1)} %get-tuple-element.12, ...), kind=kLoop, calls=%fused_computation.10 | loop fusion | flops 23068672 | bytes 16803840 | tf_op jit(solution)/shard_map/convert_element_type | solution.py:33
  150.8 2.0 copy-done.1
  152.8 8.0 %convolution_convert_fusion = bf16[512,1024]{1,0:T(8,128)(2,1)} fusion(bf16[512,4096]{1,0:T(8,128)(2,1)S(1)} %fusion.6, bf16[1024,4096]{1,0:T(8,128)(2,1)} %all-gather.2.cloned.1.call-done), kind=kOutput, calls=%fused_computation.14 | convolution fusion | flops 4295491584 | bytes 13631488 | tf_op jit(solution)/shard_map/dot_general | solution.py:34
  160.9 0.0 reduce-scatter.7.cloned.1.call-start
  160.9 9.0 %convert_bitcast_fusion = bf16[1024,4096]{0,1:T(8,128)(2,1)} fusion(bf16[512,4096]{1,0:T(8,128)(2,1)} %copy-done.1, bf16[512,1024]{1,0:T(8,128)(2,1)S(1)} %copy-done), kind=kOutput, calls=%fused_computation.11 | convolution fusion | flops 4299161600 | bytes 13631488 | tf_op jit(solution)/shard_map/dot_general | solution.py:41
  169.9 11.3 %copy.9 = bf16[1024,4096]{1,0:T(8,128)(2,1)} copy(bf16[1024,4096]{0,1:T(8,128)(2,1)} %convert_bitcast_fusion) | data formatting | bytes 16777216
  181.3 0.6 add_reduce_fusion
  181.9 39.5 %psum.23 = f32[]{:T(128)} all-reduce(f32[]{:T(128)} %add_reduce_fusion), channel_id=1, replica_groups=mesh['tok'=8,'voc'=4] {'tok','voc'}, use_global_device_ids=true, to_apply=%region_10.0 | all-reduce | flops 1 | bytes 8 | tf_op jit(solution)/shard_map/psum | solution.py:31
  222.1 0.0 reduce-scatter.5.cloned.1.call-done
  222.1 1.8 convert_element_type.25
  223.9 55.5 %reduce-scatter.7.cloned.1.call-done = bf16[128,4096]{1,0:T(8,128)(2,1)} async-done(((bf16[1024,4096]{1,0:T(8,128)(2,1)}), bf16[128,4096]{1,0:T(8,128)(2,1)}) %reduce-scatter.7.cloned.1.call-update) | async-done | bytes 1048592
  279.4 1.6 copy.10
  281.0 1.6 copy.8
  (8 shorter events, 0.1 us)
Async XLA Ops:
  7.2 87.2 %copy-start = (bf16[512,1024]{1,0:T(8,128)(2,1)S(1)}, bf16[512,1024]{1,0:T(8,128)(2,1)}, u32[]{:S(2)}) copy-start(bf16[512,1024]{1,0:T(8,128)(2,1)} %param.4) | copy-start | bytes 3145732
  7.2 87.2 %all-gather.2.cloned.1.call-start = ((), (), s32[]{:S(2)}) async-start(), calls=%async_computation.2 | async-start | bytes 9437184 | tf_op jit(solution)/shard_map/all_gather | solution.py:13
  7.9 214.2 %reduce-scatter.5.cloned.1.call-start = ((), (), s32[]{:S(2)}) async-start(), calls=%async_computation.3 | async-start | bytes 1310720 | tf_op jit(solution)/shard_map/reduce_scatter | solution.py:37
  10.8 115.2 %copy-start.2 = (s32[512]{0:T(512)S(1)}, s32[512]{0:T(512)}, u32[]{:S(2)}) copy-start(s32[512]{0:T(512)} %param.7) | copy-start | bytes 6148
  150.8 2.0 copy-start.1
  160.9 118.5 %reduce-scatter.7.cloned.1.call-start = ((), (), s32[]{:S(2)}) async-start(), calls=%async_computation.4 | async-start | bytes 9437184
Sparse Core Ops, SparseCore 0:
  9.6 84.7 all-gather.1
  161.0 25.4 reduce-scatter.4
  188.8 90.5 reduce-scatter.6
where the time goes:
time: 291 us; the launch traced here: 290 us
  waiting for transfers between devices  140 us (48%)
  blocking collectives  66.4 us (23%)
  matrix products  27.2 us (9%)
  other arithmetic  24.6 us (8%)
  local copies, waits for them, and re-layouts  16.5 us (6%)
  between operations  15.6 us (5%)
    all_gather x1, waiting for transfers between devices, body(): whole = lax.all_gather(head_weight, 'tok', axis=0, tiled=True)  83.6 us
    unnamed x4, waiting for transfers between devices  56.3 us
    psum x1, blocking collectives, body(): total = lax.psum(jnp.sum(per_token), ('tok', 'voc'))  39.5 us
    psum x2, blocking collectives, body(): lax.psum((jnp.sum(target_exp, axis=1), jnp.sum(draft_exp, axis=1)), 'voc')  17.1 us
    unnamed x9, local copies, waits for them, and re-layouts  16.5 us
    dot_general x1, matrix products, body(): draft = jnp.dot(hidden, whole, preferred_element_type=jnp.float32)  10.1 us
    pmax x1, blocking collectives, body(): lax.pmax((jnp.max(target, axis=1), jnp.max(draft, axis=1)), 'voc')  9.81 us
    dot_general x1, matrix products, body(): lax.dot_general(hidden, slope, (((0,), (0,)), ((), ())), preferred_elemen...  9.02 us
  transfers between devices with their start and end apart: 3, of which 2 were waited for; matrix products, arithmetic and copies ran while one was open for 9% of the time, Pallas kernels for 0%

commit v1 on v0

v1 whole, which is shorter than its diff:
```python
import functools
import jax
import jax.numpy as jnp
from jax import lax
from jax.sharding import PartitionSpec as P

ce_weight = 0.5
PARTS = 2
f32, bf16 = jnp.float32, jnp.bfloat16


def dot(a, b):
    return lax.dot_general(a, b, (((1,), (0,)), ((), ())), preferred_element_type=f32)


def dot_nt(a, b):
    return lax.dot_general(a, b, (((1,), (1,)), ((), ())), preferred_element_type=f32)


def body(n_tok, n_voc, hidden, head, logits, ids):
    nz = n_tok // 2
    rows, dh = hidden.shape
    share = head.shape[1]
    half = share // 2
    piece = half // PARTS
    deep = 2 * head.shape[0]
    me = lax.axis_index("tok")
    core = lax.rem(me, 2)
    z = lax.div(me, 2)
    voc = lax.axis_index("voc")

    def swap(x):
        return lax.ppermute(x, "tok", [(i, i ^ 1) for i in range(n_tok)])

    def hop(x, pairs):
        return lax.ppermute(x, "tok", [(2 * a + k, 2 * b + k) for a, b in pairs for k in range(2)])

    def cols(x, which, size):
        return lax.dynamic_slice_in_dim(x, which * size, size, 1)

    def combine(fold, x):
        bits = n_voc.bit_length() - 1
        masks = [(k, v) for v in range(min(n_voc, 4)) for k in range(2)]
        rounds = [masks]
        done = 2
        while done < bits:
            wide = min(2, bits - done)
            rounds.append([(0, v << done) for v in range(1 << wide)])
            done += wide
        for masks in rounds:
            got = []
            turned = jnp.concatenate([x[:, rows:], x[:, :rows]], axis=1)
            for k, v in masks:
                if k == 0 and v == 0:
                    got.append(x)
                    continue
                perm = [
                    (t * n_voc + w, (t ^ k) * n_voc + (w ^ v))
                    for t in range(n_tok)
                    for w in range(n_voc)
                ]
                got.append(lax.ppermute(turned if k else x, ("tok", "voc"), perm))
            while len(got) > 1:
                got = [fold(got[j], got[j + 1]) for j in range(0, len(got), 2)]
            x = got[0]
        return x

    def fold_stats(a, b):
        top = jnp.maximum(a[0], b[0])
        total = a[1] * jnp.exp(a[0] - top) + b[1] * jnp.exp(b[0] - top)
        return jnp.concatenate([jnp.stack([top, total]), a[2:] + b[2:]])

    blocks = []
    for p in range(PARTS):
        keep = lax.dynamic_slice_in_dim(head, core * half + p * piece, piece, 1)
        send = lax.dynamic_slice_in_dim(head, (1 - core) * half + p * piece, piece, 1)
        other = swap(send)
        blocks.append(
            jnp.where(
                core == 0,
                jnp.concatenate([keep, other]),
                jnp.concatenate([other, keep]),
            )
        )

    up = [[b] for b in blocks]
    down = [[b] for b in blocks]
    for s in range(1, nz):
        for p in range(PARTS):
            u, d = up[p][-1], down[p][-1]
            up_pairs = [(a, a + 1) for a in range(s - 1, nz - 1)]
            down_pairs = [(a, a - 1) for a in range(1, nz - s + 1)]
            if set(b for _, b in up_pairs) & set(b for _, b in down_pairs) or set(
                a for a, _ in up_pairs
            ) & set(a for a, _ in down_pairs):
                up[p].append(hop(u, up_pairs))
                down[p].append(hop(d, down_pairs))
            else:
                both = hop(jnp.where(z >= s - 1, u, d), up_pairs + down_pairs)
                up[p].append(both)
                down[p].append(both)

    hid = jnp.concatenate([hidden, swap(hidden)])
    hid_t = hid.T
    tgt = jnp.concatenate([cols(logits, core, half), swap(cols(logits, 1 - core, half))])
    tok_ids = jnp.concatenate([ids, swap(ids)])
    target = tgt.astype(f32)
    t_max = jnp.max(target, axis=1)
    t_sum = jnp.sum(jnp.exp(target - t_max[:, None]), axis=1)
    t_top, t_total = combine(fold_stats, jnp.stack([t_max, t_sum]))
    lse_t = t_top + jnp.log(t_total)
    t_inv = 1.0 / t_total
    vocab_start = voc * share + core * half
    iota = lax.broadcasted_iota(jnp.int32, (2 * rows, piece), 1)

    def hid_cols(index):
        return lax.dynamic_slice_in_dim(hid, index * deep, deep, 1)

    draft, whole = [], []
    for p in range(PARTS):
        acc = dot(hid_cols(z), blocks[p])
        for s in range(1, nz):
            u, d = up[p][s], down[p][s]
            if 2 * s < nz:
                acc = acc + dot(hid_cols(jnp.maximum(z - s, 0)), u)
                acc = acc + dot(hid_cols(jnp.minimum(z + s, nz - 1)), d)
            else:
                one = u if u is d else jnp.where(z >= s, u, d)
                index = jnp.where(z >= s, z - s, jnp.minimum(z + s, nz - 1))
                live = jnp.logical_or(z >= s, z + s < nz)
                acc = acc + jnp.where(live, 1.0, 0.0) * dot(hid_cols(index), one)
        draft.append(acc)

    z_max = functools.reduce(jnp.maximum, [jnp.max(a, axis=1) for a in draft])
    z_sum, part_loss = 0.0, 0.0
    probs, owns = [], []
    for p in range(PARTS):
        z_sum = z_sum + jnp.sum(jnp.exp(draft[p] - z_max[:, None]), axis=1)
        t = target[:, p * piece:(p + 1) * piece]
        prob = jnp.exp(t - t_top[:, None]) * t_inv[:, None]
        own = (iota + (vocab_start + p * piece) == tok_ids[:, None]).astype(f32)
        part_loss = part_loss + jnp.sum(
            prob * (t - draft[p]) - ce_weight * own * draft[p], axis=1
        )
        probs.append(prob)
        owns.append(own)
    z_top, z_total, all_loss = combine(fold_stats, jnp.stack([z_max, z_sum, part_loss]))
    lse_z = z_top + jnp.log(z_total)
    scale = (1.0 + ce_weight) * jnp.exp(z_max - z_top) / z_total
    slope = [
        (
            jnp.exp(draft[p] - z_max[:, None]) * scale[:, None]
            - probs[p]
            - ce_weight * owns[p]
        ).astype(bf16)
        for p in range(PARTS)
    ]

    per_token = (all_loss + (1.0 + ce_weight) * lse_z - lse_t).reshape(2, rows)
    plane = jnp.sum(per_token, axis=1)
    plane = jnp.broadcast_to(plane[0] + plane[1], (8, 128))
    spot = lax.broadcasted_iota(jnp.int32, (nz, 1, 1), 0)
    every = jnp.where(spot == z, plane[None], 0.0)
    for k in range(1, nz):
        came = hop(plane, [(a, (a + k) % nz) for a in range(nz)])
        every = every + jnp.where(spot == lax.rem(z - k + nz, nz), came[None], 0.0)
    loss = jnp.sum(every[:, 0, 0]) / (rows * n_tok)

    def grad_rows(index, p):
        return dot(lax.dynamic_slice_in_dim(hid_t, index * deep, deep, 0), slope[p])

    zero = None
    got_up, got_down = [zero] * PARTS, [zero] * PARTS
    for s in range(1, nz):
        for p in range(PARTS):
            up_pairs = [(a, a + 1) for a in range(0, s)]
            down_pairs = [(a, a - 1) for a in range(nz - s, nz)]
            if 2 * s <= nz:
                index = jnp.where(z < s, jnp.minimum(z + nz - s, nz - 1), jnp.maximum(z - nz + s, 0))
                msg = grad_rows(index, p)
                if s > 1:
                    msg = msg + got_up[p].astype(f32)
                    if got_down[p] is not got_up[p]:
                        msg = msg + got_down[p].astype(f32)
                msg = msg.astype(bf16)
                if 2 * s < nz - 1:
                    got_up[p] = got_down[p] = hop(msg, up_pairs + down_pairs)
                else:
                    got_up[p] = hop(msg, up_pairs)
                    got_down[p] = hop(msg, down_pairs)
            else:
                msg_up = grad_rows(jnp.minimum(z + nz - s, nz - 1), p) + got_up[p].astype(f32)
                msg_down = grad_rows(jnp.maximum(z - nz + s, 0), p) + got_down[p].astype(f32)
                got_up[p] = hop(msg_up.astype(bf16), up_pairs)
                got_down[p] = hop(msg_down.astype(bf16), down_pairs)
    keeps, gives = [], []
    for p in range(PARTS):
        full = grad_rows(z, p) + got_up[p].astype(f32) + got_down[p].astype(f32)
        keeps.append(lax.dynamic_slice_in_dim(full, core * (deep // 2), deep // 2, 0))
        give = lax.dynamic_slice_in_dim(full, (1 - core) * (deep // 2), deep // 2, 0)
        gives.append(swap(give.astype(bf16)).astype(f32))
    mine = jnp.concatenate(keeps, axis=1)
    theirs = jnp.concatenate(gives, axis=1)
    grad_head = jnp.where(
        core == 0,
        jnp.concatenate([mine, theirs], axis=1),
        jnp.concatenate([theirs, mine], axis=1),
    )

    part = 0.0
    for p in range(PARTS):
        full = jnp.zeros((dh, piece), bf16)
        for s in range(nz):
            if s == 0:
                block = blocks[p]
            else:
                block = jnp.where(z >= s, up[p][s], down[p][nz - s])
            full = lax.dynamic_update_slice_in_dim(full, block, lax.rem(z - s + nz, nz) * deep, 0)
        part = part + dot_nt(slope[p], full)
    own_part = part[:rows] + swap(part[rows:].astype(bf16)).astype(f32)
    width = dh // n_voc
    grad_hidden = lax.dynamic_slice_in_dim(own_part, voc * width, width, 1)
    for v in range(1, n_voc):
        give = lax.dynamic_slice_in_dim(own_part, (voc ^ v) * width, width, 1).astype(bf16)
        came = lax.ppermute(give, "voc", [(w, w ^ v) for w in range(n_voc)])
        grad_hidden = grad_hidden + came.astype(f32)
    return loss, grad_hidden, grad_head


def solution(mesh):
    placed = (P("tok", None), P("tok", "voc"), P("tok", "voc"), P("tok"))
    return jax.shard_map(
        functools.partial(body, mesh.shape["tok"], mesh.shape["voc"]),
        mesh=mesh,
        in_specs=placed,
        out_specs=(P(), P("tok", "voc"), P("tok", "voc")),
        check_vma=False,
    )
```

time: 291 us -> 232 us (0.80)
  waiting for transfers between devices: 140 us -> 50.4 us
  starting transfers between devices: 0.12 us -> 68.4 us
  blocking collectives: 66.4 us -> 0 us
  matrix products: 27.2 us -> 42.2 us
  other arithmetic: 24.6 us -> 37.4 us
  between operations: 15.6 us -> 4.72 us
  local copies, waits for them, and re-layouts: 16.5 us -> 27.1 us
    all_gather x1 -> x0, waiting for transfers between devices: 83.6 us -> none  [body(): whole = lax.all_gather(head_weight, 'tok', axis=0, tiled=True)]
    ppermute x0 -> x48, starting transfers between devices: none -> 68.4 us  [the longest x23 49.9 us: hop(): lax.ppermute(x, 'tok', [(2 * a + k, 2 * b + k) for a, b in pairs for k in...]
    psum x3 -> x0, blocking collectives: 56.6 us -> none  [the longest x1 39.5 us: body(): total = lax.psum(jnp.sum(per_token), ('tok', 'voc'))]
    unnamed x4 -> x0, waiting for transfers between devices: 56.3 us -> none
    ppermute x0 -> x48, waiting for transfers between devices: none -> 50.4 us  [the longest x23 44.7 us: hop(): lax.ppermute(x, 'tok', [(2 * a + k, 2 * b + k) for a, b in pairs for k in...]
    dot_general x3 -> x22, matrix products: 27.2 us -> 42.2 us  [the longest x20 34.2 us: dot(): lax.dot_general(a, b, (((1,), (0,)), ((), ())), preferred_element_type=f32)]
    dynamic_update_slice x0 -> x6, other arithmetic: none -> 10.1 us  [body(): lax.dynamic_update_slice_in_dim(full, block, lax.rem(z - s + nz, nz) * de...]
    pmax x1 -> x0, blocking collectives: 9.81 us -> none  [body(): lax.pmax((jnp.max(target, axis=1), jnp.max(draft, axis=1)), 'voc')]
  transfers between devices with their start and end apart: 3 -> 48, of which waited for: 2 -> 17; matrix products, arithmetic and copies ran while one was open for 9% -> 35% of each run, Pallas kernels for 0% -> 0%
where the time goes in v1:
time: 232 us; the launch traced here: 230 us
  starting transfers between devices  68.4 us (29%)
  waiting for transfers between devices  50.4 us (22%)
  matrix products  42.2 us (18%)
  other arithmetic  37.4 us (16%)
  local copies, waits for them, and re-layouts  27.1 us (12%)
  between operations  4.72 us (2%)
    ppermute x23, starting transfers between devices, hop(): lax.ppermute(x, 'tok', [(2 * a + k, 2 * b + k) for a, b in pairs for k in...  49.9 us
    ppermute x23, waiting for transfers between devices, hop(): lax.ppermute(x, 'tok', [(2 * a + k, 2 * b + k) for a, b in pairs for k in...  44.7 us
    dot_general x20, matrix products, dot(): lax.dot_general(a, b, (((1,), (0,)), ((), ())), preferred_element_type=f32)  34.2 us
    ppermute x14, starting transfers between devices, combine(): got.append(lax.ppermute(turned if k else x, ('tok', 'voc'), perm))  14.1 us
    unnamed x33, local copies, waits for them, and re-layouts  10.5 us
    dynamic_update_slice x6, other arithmetic, body(): lax.dynamic_update_slice_in_dim(full, block, lax.rem(z - s + nz, nz) * de...  10.1 us
    dot_general x2, matrix products, dot_nt(): lax.dot_general(a, b, (((1,), (1,)), ((), ())), preferred_element_type=f32)  7.99 us
    convert_element_type x1, other arithmetic, body(): slope = [(jnp.exp(draft[p] - z_max[:, None]) * scale[:, None] - probs[p]...  7.77 us
  transfers between devices with their start and end apart: 48, of which 17 were waited for; matrix products, arithmetic and copies ran while one was open for 35% of the time, Pallas kernels for 0%

profile of v1, /device:TPU:0, one launch (start us, length us, event | category | flops | bytes accessed | tf_op | source)
XLA Modules:
  0.0 230.2 jit_solution(10411174613364658485)
XLA Ops:
  3.1 4.0 %constant_dynamic-slice_fusion.7 = (bf16[512,2048]{1,0:T(8,128)(2,1)S(1)}, bf16[512,2048]{1,0:T(8,128)(2,1)}) fusion(bf16[512,4096]{1,0:T(8,128)(2,1)} %param.6, s32[]{:T(128)S(6)} %select_n.182, s32[]{:T(128)S(6)} %select_n.183), kind=kLoop, calls=%fused_computation.125 | loop fusion | bytes 8388616 | tf_op jit(solution)/shard_map/dynamic_slice | solution.py:39
  9.8 5.7 %collective-permute-start.10 = (bf16[256,1024]{1,0:T(8,128)(2,1)}, bf16[256,1024]{1,0:T(8,128)(2,1)}, u32[]{:S(2)}, u32[]{:S(2)}) collective-permute-start(bf16[256,1024]{1,0:T(8,128)(2,1)} %get-tuple-element.37), channel_id=1, source_target_pairs={{0,8},{4,12},{8,16},{12,20},{16,24},{20,28},{1,9},{5,13},{9,17},{1... | collective-permute-start | bytes 1572872 | tf_op jit(solution)/shard_map/ppermute | solution.py:36
  20.7 5.4 %collective-permute-start.17 = (bf16[256,1024]{1,0:T(8,128)(2,1)}, bf16[256,1024]{1,0:T(8,128)(2,1)}, u32[]{:S(2)}, u32[]{:S(2)}) collective-permute-start(bf16[256,1024]{1,0:T(8,128)(2,1)} %get-tuple-element.39), channel_id=1, source_target_pairs={{0,8},{4,12},{8,16},{12,20},{16,24},{20,28},{1,9},{5,13},{9,17},{1... | collective-permute-start | bytes 1572872 | tf_op jit(solution)/shard_map/ppermute | solution.py:36
  27.5 3.9 %copy.12 = bf16[512,2048]{0,1:T(8,128)(2,1)} copy(bf16[512,2048]{1,0:T(8,128)(2,1)} %get-tuple-element.50) | data formatting | bytes 4194304
  39.0 3.6 %collective-permute-done.18 = bf16[256,1024]{1,0:T(8,128)(2,1)} collective-permute-done((bf16[256,1024]{1,0:T(8,128)(2,1)}, bf16[256,1024]{1,0:T(8,128)(2,1)}, u32[]{:S(2)}, u32[]{:S(2)}) %collective-permute-start.18) | collective-permute-done | bytes 524320 | tf_op jit(solution)/shard_map/ppermute | solution.py:36
  58.0 8.1 %collective-permute-done.20 = bf16[256,1024]{1,0:T(8,128)(2,1)S(1)} collective-permute-done((bf16[256,1024]{1,0:T(8,128)(2,1)}, bf16[256,1024]{1,0:T(8,128)(2,1)S(1)}, u32[]{:S(2)}, u32[]{:S(2)}) %collective-permute-start.20) | collective-permute-done | bytes 524320 | tf_op jit(solution)/shard_map/ppermute | solution.py:36
  68.4 8.9 %collective-permute-done.14 = bf16[256,1024]{1,0:T(8,128)(2,1)S(1)} collective-permute-done((bf16[256,1024]{1,0:T(8,128)(2,1)S(1)}, bf16[256,1024]{1,0:T(8,128)(2,1)S(1)}, u32[]{:S(2)}, u32[]{:S(2)}) %collective-permute-start.14) | collective-permute-done | bytes 524320 | tf_op jit(solution)/shard_map/ppermute | solution.py:36
  78.2 2.7 %fusion.24 = f32[1024,1024]{0,1:T(8,128)} fusion(bf16[256,1024]{1,0:T(8,128)(2,1)S(1)} %collective-permute-done.14, bf16[1024,1024]{1,0:T(8,128)(2,1)S(1)} %constant_dynamic-update-slice_fusion.4, s32[]{:T(128)S(6)} %select_n.196), kind=kOutput, calls=%fused_computation.64 | convolution fusion | flops 536870912 | bytes 5242884 | tf_op jit(solution)/shard_map/dot_general | solution.py:13
  80.8 3.7 %fusion.126 = (f32[1024]{0:T(1024)S(1)}, f32[1024,1024]{0,1:T(8,128)S(1)}) fusion(f32[1024,1024]{0,1:T(8,128)} %fusion.24, f32[]{:T(128)S(6)} %select_n.194, bf16[256,1024]{1,0:T(8,128)(2,1)S(1)} %broadcast_select_fusion.1, bf16[1024,1024]{1,0:T(8,128)(2,1)S(1)} %constant_dynamic-update-slice_fusion.4, s32[]{:T(128)S(6)} %select_n.191, f32[]{:T(128)S(6)} %select_n.189, ...), kind=kOutput, calls=%fused_computation.253 | convolution fusion | flops 544209920 | bytes 22024204 | tf_op jit(solution)/shard_map/dot_general | solution.py:13
  84.6 3.3 %collective-permute-done.21 = bf16[256,1024]{1,0:T(8,128)(2,1)} collective-permute-done((bf16[256,1024]{1,0:T(8,128)(2,1)}, bf16[256,1024]{1,0:T(8,128)(2,1)}, u32[]{:S(2)}, u32[]{:S(2)}) %collective-permute-start.21) | collective-permute-done | bytes 524320 | tf_op jit(solution)/shard_map/ppermute | solution.py:36
  100.6 2.7 %fusion.9 = (f32[1024,2048]{0,1:T(8,128)S(1)}, bf16[1024]{0:T(1024)(128)(2,1)S(1)}) fusion(bf16[512,2048]{0,1:T(8,128)(2,1)} %collective-permute-done, bf16[512,2048]{0,1:T(8,128)(2,1)S(1)} %copy-done.3), kind=kLoop, calls=%fused_computation.21 | loop fusion | flops 12581888 | bytes 12584960 | tf_op jit(solution)/shard_map/convert_element_type | solution.py:107
  103.3 3.9 %exponential_reduce_fusion = f32[1024]{0:T(1024)S(1)} fusion(f32[1024]{0:T(1024)S(1)} %reduce_max.41, bf16[512,2048]{0,1:T(8,128)(2,1)} %collective-permute-done, bf16[512,2048]{0,1:T(8,128)(2,1)S(1)} %copy-done.3), kind=kLoop, calls=%fused_computation | loop fusion | flops 12581888 | bytes 4202496 | tf_op jit(solution)/shard_map/reduce_sum | solution.py:109
  117.9 4.8 %fusion.4 = (f32[1024]{0:T(1024)S(1)}, f32[1024]{0:T(1024)S(1)}, f32[1024]{0:T(1024)S(1)}, f32[1024]{0:T(1024)S(1)}) fusion(f32[1024,1024]{0,1:T(8,128)S(1)} %get-tuple-element.95, f32[1024,2048]{0,1:T(8,128)S(1)} %get-tuple-element.47, s32[1024]{0:T(1024)S(1)} %pad_add_fusion, f32[1024]{0:T(1024)S(1)} %add_divide_fusion.1, f32[1024]{0:T(1024)S(1)} %get-tuple-element.40, ...), kind=kLoop, calls=%fused_computation.9 | loop fusion | flops 23064576 | bytes 16818176 | tf_op jit(solution)/shard_map/reduce_sum | solution.py:142
  133.4 7.8 %fusion.2 = (bf16[1024,1024]{0,1:T(8,128)(2,1)S(1)}, bf16[1024,1024]{0,1:T(8,128)(2,1)S(1)}) fusion(f32[1024,2048]{0,1:T(8,128)} %copy-done, f32[1024,1024]{0,1:T(8,128)} %copy-done.1, f32[1024]{0:T(1024)S(1)} %add_divide_fusion, f32[1024]{0:T(1024)S(1)} %max.267, s32[1024]{0:T(1024)S(1)} %pad_add_fusion, f32[1024]{0:T(1024)S(1)} %add_divide_fusion.1, ...), kind=kLoop, calls=%fused_computation.7 | loop fusion | flops 18874368 | bytes 21000192 | tf_op jit(solution)/shard_map/convert_element_type | solution.py:155
  143.3 2.9 %collective-permute-start.36 = (bf16[256,1024]{1,0:T(8,128)(2,1)}, bf16[256,1024]{1,0:T(8,128)(2,1)S(1)}, u32[]{:S(2)}, u32[]{:S(2)}) collective-permute-start(bf16[256,1024]{1,0:T(8,128)(2,1)} %convolution_convert_fusion.1), channel_id=1, source_target_pairs={{0,8},{4,12},{24,16},{28,20},{1,9},{5,13},{25,17},{29,21},{2,10},{... | collective-permute-start | bytes 1572872 | tf_op jit(solution)/shard_map/ppermute | solution.py:36
  146.2 4.0 %fusion.128 = f32[1024,1024]{1,0:T(8,128)S(1)} fusion(bf16[1024,1024]{0,1:T(8,128)(2,1)S(1)} %get-tuple-element.46, bf16[1024,1024]{1,0:T(8,128)(2,1)} %select_dynamic-update-slice_fusion), kind=kOutput, calls=%fused_computation.255 | convolution fusion | flops 2147483648 | bytes 8388608 | tf_op jit(solution)/shard_map/dot_general | solution.py:17
  150.2 4.0 %convolution_add_fusion = f32[1024,1024]{1,0:T(8,128)S(1)} fusion(f32[1024,1024]{1,0:T(8,128)S(1)} %fusion.128, bf16[1024,1024]{0,1:T(8,128)(2,1)S(1)} %get-tuple-element.45, bf16[1024,1024]{1,0:T(8,128)(2,1)} %select_dynamic-update-slice_fusion.2), kind=kOutput, calls=%fused_computation.25 | convolution fusion | flops 2148532224 | bytes 12582912 | tf_op jit(solution)/shard_map/dot_general | solution.py:17
  166.1 3.2 %collective-permute-start.41 = (bf16[256,1024]{1,0:T(8,128)(2,1)S(1)}, bf16[256,1024]{1,0:T(8,128)(2,1)}, u32[]{:S(2)}, u32[]{:S(2)}) collective-permute-start(bf16[256,1024]{1,0:T(8,128)(2,1)S(1)} %convolution_convert_fusion), channel_id=1, source_target_pairs={{0,8},{4,12},{24,16},{28,20},{1,9},{5,13},{25,17},{29,21},{2,10},{... | collective-permute-start | bytes 1572872 | tf_op jit(solution)/shard_map/ppermute | solution.py:36
  182.6 4.7 %collective-permute-start.42 = (bf16[256,1024]{1,0:T(8,128)(2,1)S(1)}, bf16[256,1024]{1,0:T(8,128)(2,1)S(1)}, u32[]{:S(2)}, u32[]{:S(2)}) collective-permute-start(bf16[256,1024]{1,0:T(8,128)(2,1)S(1)} %fusion.16), channel_id=1, source_target_pairs={{0,8},{4,12},{8,16},{12,20},{1,9},{5,13},{9,17},{13,21},{2,10},{6,... | collective-permute-start | bytes 1572872 | tf_op jit(solution)/shard_map/ppermute | solution.py:36
  192.8 4.4 %collective-permute-start.38 = (bf16[256,1024]{1,0:T(8,128)(2,1)S(1)}, bf16[256,1024]{1,0:T(8,128)(2,1)S(1)}, u32[]{:S(2)}, u32[]{:S(2)}) collective-permute-start(bf16[256,1024]{1,0:T(8,128)(2,1)S(1)} %fusion.12), channel_id=1, source_target_pairs={{0,8},{4,12},{8,16},{12,20},{16,24},{20,28},{1,9},{5,13},{9,17},{1... | collective-permute-start | bytes 1572872 | tf_op jit(solution)/shard_map/ppermute | solution.py:36
  199.3 3.9 %collective-permute-done.42 = bf16[256,1024]{1,0:T(8,128)(2,1)S(1)} collective-permute-done((bf16[256,1024]{1,0:T(8,128)(2,1)S(1)}, bf16[256,1024]{1,0:T(8,128)(2,1)S(1)}, u32[]{:S(2)}, u32[]{:S(2)}) %collective-permute-start.42) | collective-permute-done | bytes 524320 | tf_op jit(solution)/shard_map/ppermute | solution.py:36
  204.0 4.4 %collective-permute-start.43 = (bf16[256,1024]{1,0:T(8,128)(2,1)S(1)}, bf16[256,1024]{1,0:T(8,128)(2,1)S(1)}, u32[]{:S(2)}, u32[]{:S(2)}) collective-permute-start(bf16[256,1024]{1,0:T(8,128)(2,1)S(1)} %fusion.15), channel_id=1, source_target_pairs={{0,8},{4,12},{8,16},{12,20},{16,24},{20,28},{1,9},{5,13},{9,17},{1... | collective-permute-start | bytes 1572872 | tf_op jit(solution)/shard_map/ppermute | solution.py:36
  211.6 2.9 %collective-permute-done.38 = bf16[256,1024]{1,0:T(8,128)(2,1)S(1)} collective-permute-done((bf16[256,1024]{1,0:T(8,128)(2,1)S(1)}, bf16[256,1024]{1,0:T(8,128)(2,1)S(1)}, u32[]{:S(2)}, u32[]{:S(2)}) %collective-permute-start.38) | collective-permute-done | bytes 524320 | tf_op jit(solution)/shard_map/ppermute | solution.py:36
  217.4 7.3 %collective-permute-done.43 = bf16[256,1024]{1,0:T(8,128)(2,1)S(1)} collective-permute-done((bf16[256,1024]{1,0:T(8,128)(2,1)S(1)}, bf16[256,1024]{1,0:T(8,128)(2,1)S(1)}, u32[]{:S(2)}, u32[]{:S(2)}) %collective-permute-start.43) | collective-permute-done | bytes 524320 | tf_op jit(solution)/shard_map/ppermute | solution.py:36
  (231 shorter events, 115.3 us)
Async XLA Ops:
  2.5 40.8 %collective-permute-start.8 = (bf16[512,1024]{1,0:T(8,128)(2,1)}, bf16[512,1024]{1,0:T(8,128)(2,1)}, u32[]{:S(2)}, u32[]{:S(2)}) collective-permute-start(bf16[512,1024]{1,0:T(8,128)(2,1)} %param.4), channel_id=1, source_target_pairs={{0,4},{4,0},{8,12},{12,8},{16,20},{20,16},{24,28},{28,24},{1,5},{5... | collective-permute-start | bytes 3145736 | tf_op jit(solution)/shard_map/ppermute | solution.py:33
  3.0 23.0 %collective-permute-start.15 = (s32[512]{0:T(512)S(1)}, s32[512]{0:T(512)S(1)}, u32[]{:S(2)}, u32[]{:S(2)}) collective-permute-start(s32[512]{0:T(512)S(1)} %copy-done.14), channel_id=1, source_target_pairs={{0,4},{4,0},{8,12},{12,8},{16,20},{20,16},{24,28},{28,24},{1,5},{5... | collective-permute-start | bytes 6152 | tf_op jit(solution)/shard_map/ppermute | solution.py:33
  9.8 25.4 %collective-permute-start.10 = (bf16[256,1024]{1,0:T(8,128)(2,1)}, bf16[256,1024]{1,0:T(8,128)(2,1)}, u32[]{:S(2)}, u32[]{:S(2)}) collective-permute-start(bf16[256,1024]{1,0:T(8,128)(2,1)} %get-tuple-element.37), channel_id=1, source_target_pairs={{0,8},{4,12},{8,16},{12,20},{16,24},{20,28},{1,9},{5,13},{9,17},{1... | collective-permute-start | bytes 1572872 | tf_op jit(solution)/shard_map/ppermute | solution.py:36
  15.6 19.7 %collective-permute-start.11 = (bf16[256,1024]{1,0:T(8,128)(2,1)}, bf16[256,1024]{1,0:T(8,128)(2,1)S(1)}, u32[]{:S(2)}, u32[]{:S(2)}) collective-permute-start(bf16[256,1024]{1,0:T(8,128)(2,1)} %get-tuple-element.37), channel_id=1, source_target_pairs={{8,0},{12,4},{16,8},{20,12},{24,16},{28,20},{9,1},{13,5},{17,9},{2... | collective-permute-start | bytes 1572872 | tf_op jit(solution)/shard_map/ppermute | solution.py:36
  20.7 17.1 %collective-permute-start.17 = (bf16[256,1024]{1,0:T(8,128)(2,1)}, bf16[256,1024]{1,0:T(8,128)(2,1)}, u32[]{:S(2)}, u32[]{:S(2)}) collective-permute-start(bf16[256,1024]{1,0:T(8,128)(2,1)} %get-tuple-element.39), channel_id=1, source_target_pairs={{0,8},{4,12},{8,16},{12,20},{16,24},{20,28},{1,9},{5,13},{9,17},{1... | collective-permute-start | bytes 1572872 | tf_op jit(solution)/shard_map/ppermute | solution.py:36
  26.0 16.6 %collective-permute-start.18 = (bf16[256,1024]{1,0:T(8,128)(2,1)}, bf16[256,1024]{1,0:T(8,128)(2,1)}, u32[]{:S(2)}, u32[]{:S(2)}) collective-permute-start(bf16[256,1024]{1,0:T(8,128)(2,1)} %get-tuple-element.39), channel_id=1, source_target_pairs={{8,0},{12,4},{16,8},{20,12},{24,16},{28,20},{9,1},{13,5},{17,9},{2... | collective-permute-start | bytes 1572872 | tf_op jit(solution)/shard_map/ppermute | solution.py:36
  35.2 65.4 %collective-permute-start = (bf16[512,2048]{0,1:T(8,128)(2,1)}, bf16[512,2048]{0,1:T(8,128)(2,1)}, u32[]{:S(2)}, u32[]{:S(2)}) collective-permute-start(bf16[512,2048]{0,1:T(8,128)(2,1)} %copy.12), channel_id=1, source_target_pairs={{0,4},{4,0},{8,12},{12,8},{16,20},{20,16},{24,28},{28,24},{1,5},{5... | collective-permute-start | bytes 6291464 | tf_op jit(solution)/shard_map/ppermute | solution.py:33
  35.3 18.6 %collective-permute-start.12 = (bf16[256,1024]{1,0:T(8,128)(2,1)}, bf16[256,1024]{1,0:T(8,128)(2,1)S(1)}, u32[]{:S(2)}, u32[]{:S(2)}) collective-permute-start(bf16[256,1024]{1,0:T(8,128)(2,1)} %collective-permute-done.10), channel_id=1, source_target_pairs={{8,16},{12,20},{16,24},{20,28},{9,17},{13,21},{17,25},{21,29},{10,... | collective-permute-start | bytes 1572872 | tf_op jit(solution)/shard_map/ppermute | solution.py:36
  37.7 17.1 %collective-permute-start.13 = (bf16[256,1024]{1,0:T(8,128)(2,1)S(1)}, bf16[256,1024]{1,0:T(8,128)(2,1)S(1)}, u32[]{:S(2)}, u32[]{:S(2)}) collective-permute-start(bf16[256,1024]{1,0:T(8,128)(2,1)S(1)} %collective-permute-done.11), channel_id=1, source_target_pairs={{8,0},{12,4},{16,8},{20,12},{9,1},{13,5},{17,9},{21,13},{10,2},{14... | collective-permute-start | bytes 1572872 | tf_op jit(solution)/shard_map/ppermute | solution.py:36
  42.6 15.4 %collective-permute-start.19 = (bf16[256,1024]{1,0:T(8,128)(2,1)}, bf16[256,1024]{1,0:T(8,128)(2,1)S(1)}, u32[]{:S(2)}, u32[]{:S(2)}) collective-permute-start(bf16[256,1024]{1,0:T(8,128)(2,1)} %collective-permute-done.17), channel_id=1, source_target_pairs={{8,16},{12,20},{16,24},{20,28},{9,17},{13,21},{17,25},{21,29},{10,... | collective-permute-start | bytes 1572872 | tf_op jit(solution)/shard_map/ppermute | solution.py:36
  43.3 22.8 %collective-permute-start.20 = (bf16[256,1024]{1,0:T(8,128)(2,1)}, bf16[256,1024]{1,0:T(8,128)(2,1)S(1)}, u32[]{:S(2)}, u32[]{:S(2)}) collective-permute-start(bf16[256,1024]{1,0:T(8,128)(2,1)} %collective-permute-done.18), channel_id=1, source_target_pairs={{8,0},{12,4},{16,8},{20,12},{9,1},{13,5},{17,9},{21,13},{10,2},{14... | collective-permute-start | bytes 1572872 | tf_op jit(solution)/shard_map/ppermute | solution.py:36
  54.9 22.4 %collective-permute-start.14 = (bf16[256,1024]{1,0:T(8,128)(2,1)S(1)}, bf16[256,1024]{1,0:T(8,128)(2,1)S(1)}, u32[]{:S(2)}, u32[]{:S(2)}) collective-permute-start(bf16[256,1024]{1,0:T(8,128)(2,1)S(1)} %broadcast_select_fusion.1), channel_id=1, source_target_pairs={{16,24},{20,28},{8,0},{12,4},{17,25},{21,29},{9,1},{13,5},{18,26},... | collective-permute-start | bytes 1572872 | tf_op jit(solution)/shard_map/ppermute | solution.py:36
  67.0 20.9 %collective-permute-start.21 = (bf16[256,1024]{1,0:T(8,128)(2,1)}, bf16[256,1024]{1,0:T(8,128)(2,1)}, u32[]{:S(2)}, u32[]{:S(2)}) collective-permute-start(bf16[256,1024]{1,0:T(8,128)(2,1)} %broadcast_select_fusion), channel_id=1, source_target_pairs={{16,24},{20,28},{8,0},{12,4},{17,25},{21,29},{9,1},{13,5},{18,26},... | collective-permute-start | bytes 1572872 | tf_op jit(solution)/shard_map/ppermute | solution.py:36
  143.3 30.7 %collective-permute-start.36 = (bf16[256,1024]{1,0:T(8,128)(2,1)}, bf16[256,1024]{1,0:T(8,128)(2,1)S(1)}, u32[]{:S(2)}, u32[]{:S(2)}) collective-permute-start(bf16[256,1024]{1,0:T(8,128)(2,1)} %convolution_convert_fusion.1), channel_id=1, source_target_pairs={{0,8},{4,12},{24,16},{28,20},{1,9},{5,13},{25,17},{29,21},{2,10},{... | collective-permute-start | bytes 1572872 | tf_op jit(solution)/shard_map/ppermute | solution.py:36
  157.3 30.7 %collective-permute-start.32 = (bf16[512,1024]{1,0:T(8,128)(2,1)}, bf16[512,1024]{1,0:T(8,128)(2,1)}, u32[]{:S(2)}, u32[]{:S(2)}) collective-permute-start(bf16[512,1024]{1,0:T(8,128)(2,1)} %slice.326), channel_id=1, source_target_pairs={{0,4},{4,0},{8,12},{12,8},{16,20},{20,16},{24,28},{28,24},{1,5},{5... | collective-permute-start | bytes 3145736 | tf_op jit(solution)/shard_map/ppermute | solution.py:33
  176.6 15.4 %collective-permute-start.37 = (bf16[256,1024]{1,0:T(8,128)(2,1)S(1)}, bf16[256,1024]{1,0:T(8,128)(2,1)S(1)}, u32[]{:S(2)}, u32[]{:S(2)}) collective-permute-start(bf16[256,1024]{1,0:T(8,128)(2,1)S(1)} %fusion.13), channel_id=1, source_target_pairs={{0,8},{4,12},{8,16},{12,20},{1,9},{5,13},{9,17},{13,21},{2,10},{6,... | collective-permute-start | bytes 1572872 | tf_op jit(solution)/shard_map/ppermute | solution.py:36
  178.3 18.9 %collective-permute-start.39 = (bf16[256,1024]{1,0:T(8,128)(2,1)S(1)}, bf16[256,1024]{1,0:T(8,128)(2,1)S(1)}, u32[]{:S(2)}, u32[]{:S(2)}) collective-permute-start(bf16[256,1024]{1,0:T(8,128)(2,1)S(1)} %fusion.13), channel_id=1, source_target_pairs={{16,8},{20,12},{24,16},{28,20},{17,9},{21,13},{25,17},{29,21},{18,... | collective-permute-start | bytes 1572872 | tf_op jit(solution)/shard_map/ppermute | solution.py:36
  182.6 20.6 %collective-permute-start.42 = (bf16[256,1024]{1,0:T(8,128)(2,1)S(1)}, bf16[256,1024]{1,0:T(8,128)(2,1)S(1)}, u32[]{:S(2)}, u32[]{:S(2)}) collective-permute-start(bf16[256,1024]{1,0:T(8,128)(2,1)S(1)} %fusion.16), channel_id=1, source_target_pairs={{0,8},{4,12},{8,16},{12,20},{1,9},{5,13},{9,17},{13,21},{2,10},{6,... | collective-permute-start | bytes 1572872 | tf_op jit(solution)/shard_map/ppermute | solution.py:36
  187.3 21.2 %collective-permute-start.44 = (bf16[256,1024]{1,0:T(8,128)(2,1)S(1)}, bf16[256,1024]{1,0:T(8,128)(2,1)S(1)}, u32[]{:S(2)}, u32[]{:S(2)}) collective-permute-start(bf16[256,1024]{1,0:T(8,128)(2,1)S(1)} %fusion.16), channel_id=1, source_target_pairs={{16,8},{20,12},{24,16},{28,20},{17,9},{21,13},{25,17},{29,21},{18,... | collective-permute-start | bytes 1572872 | tf_op jit(solution)/shard_map/ppermute | solution.py:36
  192.8 21.7 %collective-permute-start.38 = (bf16[256,1024]{1,0:T(8,128)(2,1)S(1)}, bf16[256,1024]{1,0:T(8,128)(2,1)S(1)}, u32[]{:S(2)}, u32[]{:S(2)}) collective-permute-start(bf16[256,1024]{1,0:T(8,128)(2,1)S(1)} %fusion.12), channel_id=1, source_target_pairs={{0,8},{4,12},{8,16},{12,20},{16,24},{20,28},{1,9},{5,13},{9,17},{1... | collective-permute-start | bytes 1572872 | tf_op jit(solution)/shard_map/ppermute | solution.py:36
  198.0 18.0 %collective-permute-start.40 = (bf16[256,1024]{1,0:T(8,128)(2,1)S(1)}, bf16[256,1024]{1,0:T(8,128)(2,1)S(1)}, u32[]{:S(2)}, u32[]{:S(2)}) collective-permute-start(bf16[256,1024]{1,0:T(8,128)(2,1)S(1)} %fusion.14), channel_id=1, source_target_pairs={{8,0},{12,4},{16,8},{20,12},{24,16},{28,20},{9,1},{13,5},{17,9},{2... | collective-permute-start | bytes 1572872 | tf_op jit(solution)/shard_map/ppermute | solution.py:36
  204.0 20.6 %collective-permute-start.43 = (bf16[256,1024]{1,0:T(8,128)(2,1)S(1)}, bf16[256,1024]{1,0:T(8,128)(2,1)S(1)}, u32[]{:S(2)}, u32[]{:S(2)}) collective-permute-start(bf16[256,1024]{1,0:T(8,128)(2,1)S(1)} %fusion.15), channel_id=1, source_target_pairs={{0,8},{4,12},{8,16},{12,20},{16,24},{20,28},{1,9},{5,13},{9,17},{1... | collective-permute-start | bytes 1572872 | tf_op jit(solution)/shard_map/ppermute | solution.py:36
  209.2 15.4 %collective-permute-start.45 = (bf16[256,1024]{1,0:T(8,128)(2,1)S(1)}, bf16[256,1024]{1,0:T(8,128)(2,1)S(1)}, u32[]{:S(2)}, u32[]{:S(2)}) collective-permute-start(bf16[256,1024]{1,0:T(8,128)(2,1)S(1)} %fusion.17), channel_id=1, source_target_pairs={{8,0},{12,4},{16,8},{20,12},{24,16},{28,20},{9,1},{13,5},{17,9},{2... | collective-permute-start | bytes 1572872 | tf_op jit(solution)/shard_map/ppermute | solution.py:36
  211.0 15.2 %collective-permute-start.33 = (bf16[512,256]{1,0:T(8,128)(2,1)S(1)}, bf16[512,256]{1,0:T(8,128)(2,1)S(1)}, u32[]{:S(2)}, u32[]{:S(2)}) collective-permute-start(bf16[512,256]{1,0:T(8,128)(2,1)S(1)} %get-tuple-element.51), channel_id=1, source_target_pairs={{0,1},{1,0},{2,3},{3,2},{4,5},{5,4},{6,7},{7,6},{8,9},{9,8},{10,11... | collective-permute-start | bytes 786440 | tf_op jit(solution)/shard_map/ppermute | solution.py:225
  (39 other events, 305.6 us)

commit v2 on v0

v2 whole, which is shorter than its diff:
```python
import functools
import jax
import jax.numpy as jnp
from jax import lax
from jax.experimental import pallas as pl
from jax.experimental.pallas import tpu as pltpu
from jax.sharding import PartitionSpec as P

ce_weight = 0.5
PARTS = 2
f32, bf16 = jnp.float32, jnp.bfloat16


def dot(a, b):
    return lax.dot_general(a, b, (((1,), (0,)), ((), ())), preferred_element_type=f32)


def dot_nt(a, b):
    return lax.dot_general(a, b, (((1,), (1,)), ((), ())), preferred_element_type=f32)


def lanes(columns, like):
    lane = lax.broadcasted_iota(jnp.int32, like, 1)
    out = jnp.zeros(like, f32)
    for k, c in enumerate(columns):
        out = jnp.where(lane == k, c, out)
    return out


def cost(flops, size, trans=0):
    return pl.CostEstimate(flops=flops, bytes_accessed=size, transcendentals=trans)


PARAMS = pltpu.CompilerParams(vmem_limit_bytes=48 << 20)


def target_kernel(t_ref, e_ref, stat_ref):
    t = t_ref[...].astype(f32)
    top = jnp.max(t, axis=1, keepdims=True)
    e = jnp.exp(t - top)
    e_ref[...] = e.astype(bf16)
    total = jnp.sum(e, axis=1, keepdims=True)
    first = jnp.sum(e * t, axis=1, keepdims=True)
    stat_ref[...] = lanes([top, total, first], stat_ref.shape)


def target_call(tgt, tile):
    n, half = tgt.shape
    return pl.pallas_call(
        target_kernel,
        grid=(n // tile,),
        in_specs=[pl.BlockSpec((tile, half), lambda i: (i, 0))],
        out_specs=[
            pl.BlockSpec((tile, half), lambda i: (i, 0)),
            pl.BlockSpec((tile, 128), lambda i: (i, 0)),
        ],
        out_shape=[
            jax.ShapeDtypeStruct((n, half), bf16),
            jax.ShapeDtypeStruct((n, 128), f32),
        ],
        compiler_params=PARAMS,
        cost_estimate=cost(8 * n * half, 4 * n * half, n * half),
        name="target_exps",
    )(tgt)


def partial_kernel(count, deep, idx_ref, h_ref, *refs):
    out_ref = refs[count]
    acc = None
    for k in range(count):
        at = pl.multiple_of(idx_ref[k] * deep, deep)
        term = dot(h_ref[:, pl.ds(at, deep)], refs[k][...])
        acc = term if acc is None else acc + term
    out_ref[...] = acc


def partial_call(index, hid, terms, tile):
    n, dh = hid.shape
    deep, piece = terms[0].shape
    count = len(terms)
    return pl.pallas_call(
        functools.partial(partial_kernel, count, deep),
        grid_spec=pltpu.PrefetchScalarGridSpec(
            num_scalar_prefetch=1,
            grid=(n // tile,),
            in_specs=[pl.BlockSpec((tile, dh), lambda i, s: (i, 0))]
            + [pl.BlockSpec((deep, piece), lambda i, s: (0, 0))] * count,
            out_specs=pl.BlockSpec((tile, piece), lambda i, s: (i, 0)),
        ),
        out_shape=jax.ShapeDtypeStruct((n, piece), f32),
        compiler_params=PARAMS,
        cost_estimate=cost(2 * n * deep * count * piece, 4 * n * piece + 2 * n * dh),
        name="partial_draft",
    )(index, hid, *terms)


def last_kernel(earlier, idx_ref, h_ref, w_ref, acc_ref, e_ref, id_ref, *refs):
    z = acc_ref[...] + dot(h_ref[...], w_ref[...])
    top = jnp.max(z, axis=1, keepdims=True)
    e = jnp.exp(z - top)
    total = jnp.sum(e, axis=1, keepdims=True)
    cross = jnp.sum(e_ref[...].astype(f32) * z, axis=1, keepdims=True)
    column = lax.broadcasted_iota(jnp.int32, z.shape, 1)
    own = jnp.sum(jnp.where(column == id_ref[...], z, 0.0), axis=1, keepdims=True)
    if earlier is None:
        ez_ref, stat_ref = refs
        ez_ref[...] = e.astype(bf16)
        stat_ref[...] = lanes([top, total, cross, own], stat_ref.shape)
        return
    t_ref = refs[0]
    stat_refs = refs[1:1 + earlier]
    ez_ref, send_ref, turn_ref, tops_ref = refs[1 + earlier:]
    ez_ref[...] = e.astype(bf16)
    tops, all_top = [top], top
    for r in stat_refs:
        tops.insert(len(tops) - 1, r[:, 0:1])
        all_top = jnp.maximum(all_top, r[:, 0:1])
    total = total * jnp.exp(top - all_top)
    for r in stat_refs:
        total = total + r[:, 1:2] * jnp.exp(r[:, 0:1] - all_top)
        cross = cross + r[:, 2:3]
        own = own + r[:, 3:4]
    t_top, t_total, t_first = t_ref[:, 0:1], t_ref[:, 1:2], t_ref[:, 2:3]
    like = t_ref.shape
    rows = lanes([t_top, t_total, t_first - cross, all_top, total, own], like).T[:8]
    send_ref[...] = rows
    turn_ref[...] = rows
    tops_ref[...] = lanes([t_top] + tops, like)


def last_call(index, hid, w, acc, e_t, part, ids, t_stat, stats, tile):
    n, dh = hid.shape
    deep, piece = w.shape
    grid = n // tile
    row = lambda i, s: (i, 0)
    in_specs = [
        pl.BlockSpec((tile, deep), lambda i, s: (i, s[0])),
        pl.BlockSpec((deep, piece), lambda i, s: (0, 0)),
        pl.BlockSpec((tile, piece), row),
        pl.BlockSpec((tile, piece), lambda i, s: (i, part)),
        pl.BlockSpec((tile, 1), row),
    ]
    args = [hid, w, acc, e_t, ids]
    out_specs = [pl.BlockSpec((tile, piece), row)]
    out_shape = [jax.ShapeDtypeStruct((n, piece), bf16)]
    earlier = None
    if stats is None:
        out_specs += [pl.BlockSpec((tile, 128), row)]
        out_shape += [jax.ShapeDtypeStruct((n, 128), f32)]
    else:
        earlier = len(stats)
        args += [t_stat] + stats
        in_specs += [pl.BlockSpec((tile, 128), row)] * (1 + earlier)
        out_specs += [
            pl.BlockSpec((8, tile), lambda i, s: (0, i)),
            pl.BlockSpec((8, tile), lambda i, s: (0, lax.rem(i + grid // 2, grid))),
            pl.BlockSpec((tile, 128), row),
        ]
        out_shape += [
            jax.ShapeDtypeStruct((8, n), f32),
            jax.ShapeDtypeStruct((8, n), f32),
            jax.ShapeDtypeStruct((n, 128), f32),
        ]
    return pl.pallas_call(
        functools.partial(last_kernel, earlier),
        grid_spec=pltpu.PrefetchScalarGridSpec(
            num_scalar_prefetch=1, grid=(grid,), in_specs=in_specs, out_specs=out_specs
        ),
        out_shape=out_shape,
        compiler_params=PARAMS,
        cost_estimate=cost(2 * n * deep * piece, 8 * n * piece, n * piece),
        name="last_draft",
    )(index, *args)


def fold_rows(a, b):
    t_top = jnp.maximum(a[0:1], b[0:1])
    fa, fb = jnp.exp(a[0:1] - t_top), jnp.exp(b[0:1] - t_top)
    z_top = jnp.maximum(a[3:4], b[3:4])
    ga, gb = jnp.exp(a[3:4] - z_top), jnp.exp(b[3:4] - z_top)
    rows = [
        t_top,
        a[1:2] * fa + b[1:2] * fb,
        a[2:3] * fa + b[2:3] * fb,
        z_top,
        a[4:5] * ga + b[4:5] * gb,
        a[5:6] + b[5:6],
    ]
    return jnp.concatenate(rows + [a[6:8]])


def slope_kernel(part, peers, idx_ref, *refs):
    step = pl.program_id(0)
    if peers:
        tops_ref = refs[peers]
        ez_ref, et_ref, id_ref, ht_ref = refs[peers + 1:peers + 5]
        slope_ref, msg_ref, coef_ref, loss_ref = refs[peers + 5:]

        @pl.when(step == 0)
        def _():
            got = [r[...] for r in refs[:peers]]
            while len(got) > 1:
                got = [fold_rows(got[j], got[j + 1]) for j in range(0, len(got), 2)]
            s = got[0]
            t_inv = 1.0 / s[1:2]
            lse_t = s[0:1] + jnp.log(s[1:2])
            lse_z = s[3:4] + jnp.log(s[4:5])
            n = s.shape[1]
            per_token = s[2:3] * t_inv - lse_t + (1.0 + ce_weight) * lse_z - ce_weight * s[5:6]
            plane = jnp.sum(per_token[:, :n // 2], axis=1, keepdims=True) + jnp.sum(
                per_token[:, n // 2:], axis=1, keepdims=True
            )
            loss_ref[...] = jnp.broadcast_to(plane, loss_ref.shape)
            z_inv = (1.0 + ce_weight) / s[4:5]
            flat = jnp.concatenate([s[0:1], t_inv, s[3:4], z_inv, jnp.zeros((124, n), f32)]).T
            tops = tops_ref[...]
            lane = lax.broadcasted_iota(jnp.int32, tops.shape, 1)
            base = jnp.where(lane == 0, flat[:, 0:1], flat[:, 2:3])
            gain = jnp.where(lane == 0, flat[:, 1:2], flat[:, 3:4])
            coef_ref[...] = jnp.where(lane <= PARTS, jnp.exp(tops - base) * gain, 0.0)

    else:
        coef_ref, ez_ref, et_ref, id_ref, ht_ref, slope_ref, msg_ref = refs
    b = coef_ref[:, 0:1]
    a = coef_ref[:, part + 1:part + 2]
    value = ez_ref[...].astype(f32) * a - et_ref[...].astype(f32) * b
    column = lax.broadcasted_iota(jnp.int32, value.shape, 1) + step * value.shape[1]
    value = jnp.where(column == id_ref[...], value - ce_weight, value)
    slope = value.astype(bf16)
    slope_ref[...] = slope
    msg_ref[...] = dot(ht_ref[...], slope).astype(bf16)


def slope_call(part, index, head_args, e_z, e_t, ids, hid_t, deep, tile):
    n, piece = e_z.shape
    peers = len(head_args) - 1
    steps = piece // tile
    fixed = lambda i, s: (0, 0)
    in_specs = [pl.BlockSpec(a.shape, fixed) for a in head_args] + [
        pl.BlockSpec((n, tile), lambda i, s: (0, i)),
        pl.BlockSpec((n, tile), lambda i, s: (0, part * steps + i)),
        pl.BlockSpec((n, 1), fixed),
        pl.BlockSpec((deep, n), lambda i, s: (s[0], 0)),
    ]
    out_specs = [
        pl.BlockSpec((n, tile), lambda i, s: (0, i)),
        pl.BlockSpec((deep, tile), lambda i, s: (0, i)),
    ]
    out_shape = [
        jax.ShapeDtypeStruct((n, piece), bf16),
        jax.ShapeDtypeStruct((deep, piece), bf16),
    ]
    if peers:
        out_specs += [pl.BlockSpec((n, 128), fixed), pl.BlockSpec((8, 128), fixed)]
        out_shape += [
            jax.ShapeDtypeStruct((n, 128), f32),
            jax.ShapeDtypeStruct((8, 128), f32),
        ]
    return pl.pallas_call(
        functools.partial(slope_kernel, part, peers),
        grid_spec=pltpu.PrefetchScalarGridSpec(
            num_scalar_prefetch=1, grid=(steps,), in_specs=in_specs, out_specs=out_specs
        ),
        out_shape=out_shape,
        compiler_params=PARAMS,
        cost_estimate=cost(2 * n * deep * piece, 6 * n * piece),
        name="slope",
    )(index, *head_args, e_z, e_t, ids, hid_t)


def body(n_tok, n_voc, hidden, head, logits, ids):
    nz = n_tok // 2
    rows, dh = hidden.shape
    own_rows, share = head.shape
    half = share // 2
    piece = half // PARTS
    deep = 2 * own_rows
    tile = min(256, rows)
    me = lax.axis_index("tok")
    core = lax.rem(me, 2)
    z = lax.div(me, 2)
    voc = lax.axis_index("voc")

    def swap(x):
        return lax.ppermute(x, "tok", [(i, i ^ 1) for i in range(n_tok)])

    def hop(x, pairs):
        return lax.ppermute(x, "tok", [(2 * a + k, 2 * b + k) for a, b in pairs for k in range(2)])

    def plane_swap(x, v):
        return lax.ppermute(x, "voc", [(w, w ^ v) for w in range(n_voc)])

    def mine(x, other=False):
        left, right = x[:, :half], x[:, half:]
        return jnp.where((core == 0) != other, left, right)

    def flip(x):
        parts = [x[:, (k ^ 1) * own_rows:((k ^ 1) + 1) * own_rows] for k in range(2 * nz)]
        return jnp.where(core == 0, x, jnp.concatenate(parts, axis=1))

    def scalar(x):
        return jnp.reshape(x, (1,)).astype(jnp.int32)

    keep, send = mine(head), mine(head, True)
    blocks = []
    for p in range(PARTS):
        cut = slice(p * piece, (p + 1) * piece)
        blocks.append(jnp.concatenate([keep[:, cut], swap(send[:, cut])]))

    up = [[b] for b in blocks]
    down = [[b] for b in blocks]
    merged = [None] * nz
    for s in range(1, nz):
        up_pairs = [(a, a + 1) for a in range(s - 1, nz - 1)]
        down_pairs = [(a, a - 1) for a in range(1, nz - s + 1)]
        for p in range(PARTS):
            u, d = up[p][-1], down[p][-1]
            if 2 * s > nz + 1:
                both = hop(jnp.where(z >= s - 1, u, d), up_pairs + down_pairs)
                up[p].append(both)
                down[p].append(both)
            else:
                up[p].append(hop(u, up_pairs))
                down[p].append(hop(d, down_pairs))

    def arrived(p, s):
        u, d = up[p][s], down[p][s]
        if u is d:
            return [(jnp.where(z >= s, nz - s, s), u)]
        if 2 * s >= nz:
            return [(jnp.where(z >= s, nz - s, s), jnp.where(z >= s, u, d))]
        return [(nz - s, u), (s, d)]

    hid = flip(jnp.concatenate([hidden, swap(hidden)]))
    hid = lax.dynamic_slice_in_dim(jnp.concatenate([hid, hid], axis=1), z * deep, dh, 1)
    hid_t = hid.T
    tgt = jnp.concatenate([mine(logits), swap(mine(logits, True))])
    local = jnp.concatenate([ids, swap(ids)]) - (voc * share + core * half)
    local = [(local - p * piece)[:, None] for p in range(PARTS)]
    e_t, t_stat = target_call(tgt, tile)

    stats, e_z = [], []
    for p in range(PARTS):
        terms = [(0, blocks[p])] + [x for s in range(1, nz - 1) for x in arrived(p, s)]
        index = jnp.stack([jnp.asarray(k, jnp.int32) for k, _ in terms])
        acc = partial_call(index, hid, [w for _, w in terms], tile)
        final = arrived(p, nz - 1)
        assert len(final) == 1
        at, w = final[0]
        at = scalar(jnp.minimum(at, nz - 1))
        if p < PARTS - 1:
            e, st = last_call(at, hid, w, acc, e_t, p, local[p], None, None, tile)
            stats.append(st)
        else:
            e, mine_rows, turned, tops = last_call(
                at, hid, w, acc, e_t, p, local[p], t_stat, stats, tile
            )
        e_z.append(e)

    x = fold_rows(mine_rows, swap(turned))
    bits = n_voc.bit_length() - 1
    done = 0
    while True:
        wide = min(2, bits - done)
        got = [x] + [plane_swap(x, v << done) for v in range(1, 1 << wide)]
        done += wide
        if done >= bits:
            break
        while len(got) > 1:
            got = [fold_rows(got[j], got[j + 1]) for j in range(0, len(got), 2)]
        x = got[0]

    def first_row(s):
        return jnp.where(z < s, nz - s, s)

    msgs, slope = [], []
    for p in range(PARTS):
        head_args = got + [tops] if p == 0 else [coef]
        outs = slope_call(
            p, scalar(first_row(1)), head_args, e_z[p], e_t, local[p], hid_t, deep, tile
        )
        slope.append(outs[0])
        msgs.append(outs[1])
        if p == 0:
            coef, plane = outs[2:]

    def grad_rows(index, p):
        return dot(lax.dynamic_slice_in_dim(hid_t, index * deep, deep, 0), slope[p])

    got_up, got_down = [None] * PARTS, [None] * PARTS
    for s in range(1, nz):
        up_pairs = [(a, a + 1) for a in range(0, s)]
        down_pairs = [(a, a - 1) for a in range(nz - s, nz)]
        for p in range(PARTS):
            if 2 * s <= nz:
                if s == 1:
                    msg = msgs[p]
                else:
                    msg = grad_rows(first_row(s), p) + got_up[p].astype(f32)
                    if got_down[p] is not got_up[p]:
                        msg = msg + got_down[p].astype(f32)
                    msg = msg.astype(bf16)
                if 2 * s < nz - 1:
                    got_up[p] = got_down[p] = hop(msg, up_pairs + down_pairs)
                else:
                    got_up[p] = hop(msg, up_pairs)
                    got_down[p] = hop(msg, down_pairs)
            else:
                msg_up = grad_rows(nz - s, p) + got_up[p].astype(f32)
                msg_down = grad_rows(s, p) + got_down[p].astype(f32)
                got_up[p] = hop(msg_up.astype(bf16), up_pairs)
                got_down[p] = hop(msg_down.astype(bf16), down_pairs)
    keeps, gives = [], []
    for p in range(PARTS):
        full = grad_rows(0, p) + got_up[p].astype(f32) + got_down[p].astype(f32)
        keeps.append(full[:own_rows])
        gives.append(swap(full[own_rows:].astype(bf16)).astype(f32))
    grad_head = jnp.where(
        core == 0,
        jnp.concatenate(keeps + gives, axis=1),
        jnp.concatenate(gives + keeps, axis=1),
    )

    late, plane, _ = lax.optimization_barrier((slope, plane, msgs[-1]))
    spot = lax.broadcasted_iota(jnp.int32, (nz, 1, 1), 0)
    every = jnp.where(spot == z, plane[None], 0.0)
    for k in range(1, nz):
        came = hop(plane, [(a, (a + k) % nz) for a in range(nz)])
        every = every + jnp.where(spot == lax.rem(z - k + nz, nz), came[None], 0.0)
    loss = jnp.sum(every[:, 0, 0]) / (rows * n_tok)

    part = 0.0
    for p in range(PARTS):
        ring = [blocks[p]]
        for j in range(1, nz):
            ring.append(jnp.where(z + j < nz, down[p][j], up[p][nz - j]))
        part = part + dot_nt(late[p], jnp.concatenate(ring))
    own_part = flip(part[:rows]) + swap(flip(part[rows:].astype(bf16))).astype(f32)
    twice = jnp.concatenate([own_part, own_part], axis=1)
    width = dh // n_voc

    def wide_slice(w):
        return lax.dynamic_slice_in_dim(twice, lax.rem(w * width - z * deep + dh, dh), width, 1)

    grad_hidden = wide_slice(voc)
    for v in range(1, n_voc):
        give = wide_slice(voc ^ v).astype(bf16)
        grad_hidden = grad_hidden + plane_swap(give, v).astype(f32)
    return loss, grad_hidden, grad_head


def solution(mesh):
    placed = (P("tok", None), P("tok", "voc"), P("tok", "voc"), P("tok"))
    return jax.shard_map(
        functools.partial(body, mesh.shape["tok"], mesh.shape["voc"]),
        mesh=mesh,
        in_specs=placed,
        out_specs=(P(), P("tok", "voc"), P("tok", "voc")),
        check_vma=False,
    )
```

time: 291 us -> 237 us (0.81)
  waiting for transfers between devices: 140 us -> 46.2 us
  blocking collectives: 66.4 us -> 0 us
  starting transfers between devices: 0.12 us -> 62.1 us
  Pallas kernels: 0 us -> 40.3 us
  other arithmetic: 24.6 us -> 50.3 us
  matrix products: 27.2 us -> 11.1 us
  between operations: 15.6 us -> 3.51 us
  local copies, waits for them, and re-layouts: 16.5 us -> 21.1 us
    all_gather x1 -> x0, waiting for transfers between devices: 83.6 us -> none  [body(): whole = lax.all_gather(head_weight, 'tok', axis=0, tiled=True)]
    ppermute x0 -> x38, starting transfers between devices: none -> 62.1 us  [the longest x23 53.8 us: hop(): lax.ppermute(x, 'tok', [(2 * a + k, 2 * b + k) for a, b in pairs for k in...]
    psum x3 -> x0, blocking collectives: 56.6 us -> none  [the longest x1 39.5 us: body(): total = lax.psum(jnp.sum(per_token), ('tok', 'voc'))]
    unnamed x4 -> x0, waiting for transfers between devices: 56.3 us -> none
    ppermute x0 -> x38, waiting for transfers between devices: none -> 46.2 us  [the longest x23 42.8 us: hop(): lax.ppermute(x, 'tok', [(2 * a + k, 2 * b + k) for a, b in pairs for k in...]
    pallas_call x0 -> x7, Pallas kernels: none -> 40.3 us  [the longest x2 12 us: last_call(): pl.pallas_call(functools.partial(last_kernel, earlier), grid_spec=pltpu.P...]
    dot_general x3 -> x10, matrix products: 27.2 us -> 11.1 us  [the longest x8 6.37 us: dot(): lax.dot_general(a, b, (((1,), (0,)), ((), ())), preferred_element_type=f32)]
    select_n x0 -> x7, other arithmetic: none -> 12.4 us  [the longest x2 5.86 us: mine(): return jnp.where((core == 0) != other, left, right)]
  transfers between devices with their start and end apart: 3 -> 38, of which waited for: 2 -> 13; matrix products, arithmetic and copies ran while one was open for 9% -> 29% of each run, Pallas kernels for 0% -> 5%
where the time goes in v2:
time: 237 us; the launch traced here: 235 us
  starting transfers between devices  62.1 us (26%)
  other arithmetic  50.3 us (21%)
  waiting for transfers between devices  46.2 us (19%)
  Pallas kernels  40.3 us (17%)
  local copies, waits for them, and re-layouts  21.1 us (9%)
  matrix products  11.1 us (5%)
  between operations  3.51 us (1%)
    ppermute x23, starting transfers between devices, hop(): lax.ppermute(x, 'tok', [(2 * a + k, 2 * b + k) for a, b in pairs for k in...  53.8 us
    ppermute x23, waiting for transfers between devices, hop(): lax.ppermute(x, 'tok', [(2 * a + k, 2 * b + k) for a, b in pairs for k in...  42.8 us
    unnamed x73, local copies, waits for them, and re-layouts  12.6 us
    unnamed x10, other arithmetic  12.3 us
    pallas_call x2, Pallas kernels, last_call(): pl.pallas_call(functools.partial(last_kernel, earlier), grid_spec=pltpu.P...  12 us
    pallas_call x2, Pallas kernels, partial_call(): pl.pallas_call(functools.partial(partial_kernel, count, deep), grid_spec=...  11.9 us
    pallas_call x2, Pallas kernels, slope_call(): pl.pallas_call(functools.partial(slope_kernel, part, peers), grid_spec=pl...  11.7 us
    ppermute x6, starting transfers between devices, plane_swap(): return lax.ppermute(x, 'voc', [(w, w ^ v) for w in range(n_voc)])  7.1 us
  transfers between devices with their start and end apart: 38, of which 13 were waited for; matrix products, arithmetic and copies ran while one was open for 29% of the time, Pallas kernels for 5%

profile of v2, /device:TPU:0, one launch (start us, length us, event | category | flops | bytes accessed | tf_op | source)
XLA Modules:
  0.0 234.6 jit_solution(4454049334322245749)
XLA Ops:
  4.5 4.6 %broadcast_select_fusion.1 = (bf16[512,2048]{1,0:T(8,128)(2,1)}, bf16[512,2048]{1,0:T(8,128)(2,1)}) fusion(pred[]{:T(512)S(6)} %eq.56, bf16[512,4096]{1,0:T(8,128)(2,1)} %param.6, pred[]{:T(512)S(6)} %ne.4), kind=kLoop, calls=%fused_computation.36 | loop fusion | flops 2097152 | bytes 8388610 | tf_op jit(solution)/shard_map/jit(_where)/select_n | solution.py:295
  11.6 6.3 %collective-permute-start.2 = (bf16[256,1024]{1,0:T(8,128)(2,1)S(1)}, bf16[256,1024]{1,0:T(8,128)(2,1)}, u32[]{:S(2)}, u32[]{:S(2)}) collective-permute-start(bf16[256,1024]{1,0:T(8,128)(2,1)S(1)} %pad_maximum_fusion.2.refs_0_), channel_id=1, source_target_pairs={{0,8},{4,12},{8,16},{12,20},{16,24},{20,28},{1,9},{5,13},{9,17},{1... | collective-permute-start | bytes 1572872 | tf_op jit(solution)/shard_map/ppermute | solution.py:288
  19.3 5.4 %collective-permute-start.10 = (bf16[256,1024]{1,0:T(8,128)(2,1)S(1)}, bf16[256,1024]{1,0:T(8,128)(2,1)}, u32[]{:S(2)}, u32[]{:S(2)}) collective-permute-start(bf16[256,1024]{1,0:T(8,128)(2,1)S(1)} %pad_maximum_fusion.3.refs_0_), channel_id=1, source_target_pairs={{0,8},{4,12},{8,16},{12,20},{16,24},{20,28},{1,9},{5,13},{9,17},{1... | collective-permute-start | bytes 1572872 | tf_op jit(solution)/shard_map/ppermute | solution.py:288
  30.7 8.6 %collective-permute-done.12.refs_2_ = bf16[256,1024]{1,0:T(8,128)(2,1)} collective-permute-done((bf16[256,1024]{1,0:T(8,128)(2,1)S(1)}, bf16[256,1024]{1,0:T(8,128)(2,1)}, u32[]{:S(2)}, u32[]{:S(2)}) %collective-permute-start.12) | collective-permute-done | bytes 524320 | tf_op jit(solution)/shard_map/ppermute | solution.py:288
  54.4 4.1 %fusion.1 = bf16[1024,1024]{0,1:T(8,128)(2,1)} fusion(s32[]{:T(128)S(6)} %select_n.153, bf16[1024,1024]{0,1:T(8,128)(2,1)S(1)} %fusion), kind=kLoop, calls=%fused_computation.31 | loop fusion | flops 4194304 | bytes 4194308 | tf_op jit(solution)/shard_map/concatenate | solution.py:335
  67.2 4.1 %fusion.68.refs_8_.refs_4_ = bf16[1024,1024]{1,0:T(8,128)(2,1)} fusion(s32[]{:T(128)S(6)} %select_n.153, bf16[1024,1024]{0,1:T(8,128)(2,1)S(1)} %copy-done.13), kind=kLoop, calls=%fused_computation.151 | loop fusion | flops 4194304 | bytes 4194308 | tf_op jit(solution)/shard_map/transpose | solution.py:336
  71.3 5.9 %partial_draft.2.acc_ref = f32[1024,1024]{1,0:T(8,128)} custom-call(s32[4]{0:T(128)S(1)} %copy-done.11, bf16[1024,1024]{1,0:T(8,128)(2,1)S(1)} %copy.37.h_ref, bf16[256,1024]{1,0:T(8,128)(2,1)S(1)} %copy-done.8, bf16[256,1024]{1,0:T(8,128)(2,1)} %collective-permute-done.2.refs_1_, bf16[256,1024]{1,0:T(8,128)(2,1)} %collective-permute-done.4.refs_2_, ...), custom_call_target="tpu_custom_call" | custom-call | flops 2147483648 | bytes 6291456 | tf_op jit(solution)/shard_map/partial_draft/pallas_call | solution.py:81
  77.2 6.0 %partial_draft.3.acc_ref = f32[1024,1024]{1,0:T(8,128)} custom-call(s32[4]{0:T(128)S(1)} %copy-done.11, bf16[1024,1024]{1,0:T(8,128)(2,1)S(1)} %copy.37.h_ref, bf16[256,1024]{1,0:T(8,128)(2,1)S(1)} %copy-done.10, bf16[256,1024]{1,0:T(8,128)(2,1)} %collective-permute-done.10.refs_1_, bf16[256,1024]{1,0:T(8,128)(2,1)} %collective-permute-done.12.refs_2_, ...), custom_call_target="tpu_custom_call" | custom-call | flops 2147483648 | bytes 6291456 | tf_op jit(solution)/shard_map/partial_draft/pallas_call | solution.py:81
  85.8 9.0 %collective-permute-done.14.w_ref = bf16[256,1024]{1,0:T(8,128)(2,1)S(1)} collective-permute-done((bf16[256,1024]{1,0:T(8,128)(2,1)S(1)}, bf16[256,1024]{1,0:T(8,128)(2,1)S(1)}, u32[]{:S(2)}, u32[]{:S(2)}) %collective-permute-start.14) | collective-permute-done | bytes 524320 | tf_op jit(solution)/shard_map/ppermute | solution.py:288
  100.6 4.2 %pad_maximum_fusion.1.t_ref = bf16[1024,2048]{1,0:T(8,128)(2,1)} fusion(bf16[512,2048]{1,0:T(8,128)(2,1)} %collective-permute-done.7, bf16[512,2048]{1,0:T(8,128)(2,1)S(1)} %copy-done.16), kind=kLoop, calls=%fused_computation.29 | loop fusion | flops 8388608 | bytes 8388608 | tf_op jit(solution)/shard_map/concatenate | solution.py:337
  104.8 4.6 %target_exps.1 = (bf16[1024,2048]{1,0:T(8,128)(2,1)S(1)}, f32[1024,128]{1,0:T(8,128)S(1)}) custom-call(bf16[1024,2048]{1,0:T(8,128)(2,1)} %pad_maximum_fusion.1.t_ref), custom_call_target="tpu_custom_call" | custom-call | flops 16777216 | bytes 8388608 | tf_op jit(solution)/shard_map/target_exps/pallas_call | solution.py:49
  111.5 5.0 %last_draft.2 = (bf16[1024,1024]{1,0:T(8,128)(2,1)S(1)}, f32[1024,128]{1,0:T(8,128)S(1)}) custom-call(s32[1]{0:T(128)} %bitcast.1.idx_ref, bf16[1024,1024]{1,0:T(8,128)(2,1)S(1)} %copy.37.h_ref, bf16[256,1024]{1,0:T(8,128)(2,1)S(1)} %collective-permute-done.14.w_ref, f32[1024,1024]{1,0:T(8,128)} %partial_draft.3.acc_ref, bf16[1024,2048]{1,0:T(8,128)(2,1)} %copy-done, ...), custom_call_target="tpu_custom_call" | custom-call | flops 536870912 | bytes 8388608 | tf_op jit(solution)/shard_map/last_draft/pallas_call | solution.py:164
  117.9 7.0 %last_draft.3 = (bf16[1024,1024]{1,0:T(8,128)(2,1)S(1)}, f32[8,1024]{1,0:T(8,128)S(1)}, f32[8,1024]{1,0:T(8,128)S(1)}, f32[1024,128]{1,0:T(8,128)S(1)}) custom-call(s32[1]{0:T(128)} %bitcast.1.idx_ref, bf16[1024,1024]{1,0:T(8,128)(2,1)} %copy-done.1, bf16[256,1024]{1,0:T(8,128)(2,1)S(1)} %collective-permute-done.6.w_ref, f32[1024,1024]{1,0:T(8,128)} %partial_draft.2.acc_ref, ...), custom_call_target="tpu_custom_call" | custom-call | flops 536870912 | bytes 8388608 | tf_op jit(solution)/shard_map/last_draft/pallas_call | solution.py:164
  134.7 6.4 %slope.2 = (bf16[1024,1024]{1,0:T(8,128)(2,1)S(1)}, bf16[256,1024]{1,0:T(8,128)(2,1)S(1)}, f32[1024,128]{1,0:T(8,128)S(1)}, f32[8,128]{1,0:T(8,128)S(1)}) custom-call(s32[1]{0:T(128)} %bitcast.idx_ref, f32[8,1024]{1,0:T(8,128)S(1)} %concatenate.71.refs_0_, f32[8,1024]{1,0:T(8,128)S(1)} %collective-permute-done.16.refs_1_, ...), custom_call_target="tpu_custom_call" | custom-call | flops 536870912 | bytes 6291456 | tf_op jit(solution)/shard_map/slope/pallas_call | solution.py:259
  141.1 5.3 %slope.3 = (bf16[1024,1024]{1,0:T(8,128)(2,1)S(1)}, bf16[256,1024]{1,0:T(8,128)(2,1)S(1)}) custom-call(s32[1]{0:T(128)} %bitcast.idx_ref, f32[1024,128]{1,0:T(8,128)S(1)} %get-tuple-element.28.refs_0_, bf16[1024,1024]{1,0:T(8,128)(2,1)S(1)} %copy-done.5, bf16[1024,2048]{1,0:T(8,128)(2,1)} %copy-done, s32[1024,1]{1,0:T(8,128)S(1)} %get-tuple-element.53.id_ref.refs_3_, ...), custom_call_target="tpu_custom_call" | custom-call | flops 536870912 | bytes 6291456 | tf_op jit(solution)/shard_map/slope/pallas_call | solution.py:259
  148.6 3.6 %collective-permute-start.31 = (bf16[256,1024]{1,0:T(8,128)(2,1)S(1)}, bf16[256,1024]{1,0:T(8,128)(2,1)S(1)}, u32[]{:S(2)}, u32[]{:S(2)}) collective-permute-start(bf16[256,1024]{1,0:T(8,128)(2,1)S(1)} %get-tuple-element.32), channel_id=1, source_target_pairs={{0,8},{4,12},{24,16},{28,20},{1,9},{5,13},{25,17},{29,21},{2,10},{... | collective-permute-start | bytes 1572872 | tf_op jit(solution)/shard_map/ppermute | solution.py:288
  159.2 5.3 %collective-permute-done.31 = bf16[256,1024]{1,0:T(8,128)(2,1)S(1)} collective-permute-done((bf16[256,1024]{1,0:T(8,128)(2,1)S(1)}, bf16[256,1024]{1,0:T(8,128)(2,1)S(1)}, u32[]{:S(2)}, u32[]{:S(2)}) %collective-permute-start.31) | collective-permute-done | bytes 524320 | tf_op jit(solution)/shard_map/ppermute | solution.py:288
  168.5 5.1 %collective-permute-start.32 = (bf16[256,1024]{1,0:T(8,128)(2,1)S(1)}, bf16[256,1024]{1,0:T(8,128)(2,1)S(1)}, u32[]{:S(2)}, u32[]{:S(2)}) collective-permute-start(bf16[256,1024]{1,0:T(8,128)(2,1)S(1)} %fusion.9), channel_id=1, source_target_pairs={{0,8},{4,12},{8,16},{12,20},{1,9},{5,13},{9,17},{13,21},{2,10},{6,... | collective-permute-start | bytes 1572872 | tf_op jit(solution)/shard_map/ppermute | solution.py:288
  175.3 5.1 %collective-permute-start.27 = (bf16[256,1024]{1,0:T(8,128)(2,1)S(1)}, bf16[256,1024]{1,0:T(8,128)(2,1)S(1)}, u32[]{:S(2)}, u32[]{:S(2)}) collective-permute-start(bf16[256,1024]{1,0:T(8,128)(2,1)S(1)} %fusion.6), channel_id=1, source_target_pairs={{0,8},{4,12},{8,16},{12,20},{1,9},{5,13},{9,17},{13,21},{2,10},{6,... | collective-permute-start | bytes 1572872 | tf_op jit(solution)/shard_map/ppermute | solution.py:288
  182.5 3.3 %collective-permute-done.32 = bf16[256,1024]{1,0:T(8,128)(2,1)S(1)} collective-permute-done((bf16[256,1024]{1,0:T(8,128)(2,1)S(1)}, bf16[256,1024]{1,0:T(8,128)(2,1)S(1)}, u32[]{:S(2)}, u32[]{:S(2)}) %collective-permute-start.32) | collective-permute-done | bytes 524320 | tf_op jit(solution)/shard_map/ppermute | solution.py:288
  186.6 4.6 %collective-permute-start.33 = (bf16[256,1024]{1,0:T(8,128)(2,1)S(1)}, bf16[256,1024]{1,0:T(8,128)(2,1)S(1)}, u32[]{:S(2)}, u32[]{:S(2)}) collective-permute-start(bf16[256,1024]{1,0:T(8,128)(2,1)S(1)} %fusion.8), channel_id=1, source_target_pairs={{0,8},{4,12},{8,16},{12,20},{16,24},{20,28},{1,9},{5,13},{9,17},{1... | collective-permute-start | bytes 1572872 | tf_op jit(solution)/shard_map/ppermute | solution.py:288
  193.2 3.9 %collective-permute-done.27 = bf16[256,1024]{1,0:T(8,128)(2,1)S(1)} collective-permute-done((bf16[256,1024]{1,0:T(8,128)(2,1)S(1)}, bf16[256,1024]{1,0:T(8,128)(2,1)S(1)}, u32[]{:S(2)}, u32[]{:S(2)}) %collective-permute-start.27) | collective-permute-done | bytes 524320 | tf_op jit(solution)/shard_map/ppermute | solution.py:288
  197.8 4.8 %collective-permute-start.28 = (bf16[256,1024]{1,0:T(8,128)(2,1)S(1)}, bf16[256,1024]{1,0:T(8,128)(2,1)S(1)}, u32[]{:S(2)}, u32[]{:S(2)}) collective-permute-start(bf16[256,1024]{1,0:T(8,128)(2,1)S(1)} %fusion.5), channel_id=1, source_target_pairs={{0,8},{4,12},{8,16},{12,20},{16,24},{20,28},{1,9},{5,13},{9,17},{1... | collective-permute-start | bytes 1572872 | tf_op jit(solution)/shard_map/ppermute | solution.py:288
  211.4 7.7 %collective-permute-done.28 = bf16[256,1024]{1,0:T(8,128)(2,1)S(1)} collective-permute-done((bf16[256,1024]{1,0:T(8,128)(2,1)S(1)}, bf16[256,1024]{1,0:T(8,128)(2,1)S(1)}, u32[]{:S(2)}, u32[]{:S(2)}) %collective-permute-start.28) | collective-permute-done | bytes 524320 | tf_op jit(solution)/shard_map/ppermute | solution.py:288
  (197 shorter events, 101.0 us)
Async XLA Ops:
  0.6 18.6 %collective-permute-start.8 = (s32[512]{0:T(512)}, s32[512]{0:T(512)S(1)}, u32[]{:S(2)}, u32[]{:S(2)}) collective-permute-start(s32[512]{0:T(512)} %param.7), channel_id=1, source_target_pairs={{0,4},{4,0},{8,12},{12,8},{16,20},{20,16},{24,28},{28,24},{1,5},{5... | collective-permute-start | bytes 6152 | tf_op jit(solution)/shard_map/ppermute | solution.py:285
  4.4 37.7 %collective-permute-start = (bf16[512,1024]{0,1:T(8,128)(2,1)S(1)}, bf16[512,1024]{0,1:T(8,128)(2,1)}, u32[]{:S(2)}, u32[]{:S(2)}) collective-permute-start(bf16[512,1024]{0,1:T(8,128)(2,1)S(1)} %copy.32), channel_id=1, source_target_pairs={{0,4},{4,0},{8,12},{12,8},{16,20},{20,16},{24,28},{28,24},{1,5},{5... | collective-permute-start | bytes 3145736 | tf_op jit(solution)/shard_map/ppermute | solution.py:285
  17.9 21.3 %collective-permute-start.12 = (bf16[256,1024]{1,0:T(8,128)(2,1)S(1)}, bf16[256,1024]{1,0:T(8,128)(2,1)}, u32[]{:S(2)}, u32[]{:S(2)}) collective-permute-start(bf16[256,1024]{1,0:T(8,128)(2,1)S(1)} %pad_maximum_fusion.3.refs_0_), channel_id=1, source_target_pairs={{8,0},{12,4},{16,8},{20,12},{24,16},{28,20},{9,1},{13,5},{17,9},{2... | collective-permute-start | bytes 1572872 | tf_op jit(solution)/shard_map/ppermute | solution.py:288
  19.3 21.5 %collective-permute-start.10 = (bf16[256,1024]{1,0:T(8,128)(2,1)S(1)}, bf16[256,1024]{1,0:T(8,128)(2,1)}, u32[]{:S(2)}, u32[]{:S(2)}) collective-permute-start(bf16[256,1024]{1,0:T(8,128)(2,1)S(1)} %pad_maximum_fusion.3.refs_0_), channel_id=1, source_target_pairs={{0,8},{4,12},{8,16},{12,20},{16,24},{20,28},{1,9},{5,13},{9,17},{1... | collective-permute-start | bytes 1572872 | tf_op jit(solution)/shard_map/ppermute | solution.py:288
  28.3 72.2 %collective-permute-start.7 = (bf16[512,2048]{1,0:T(8,128)(2,1)}, bf16[512,2048]{1,0:T(8,128)(2,1)}, u32[]{:S(2)}, u32[]{:S(2)}) collective-permute-start(bf16[512,2048]{1,0:T(8,128)(2,1)} %get-tuple-element.56), channel_id=1, source_target_pairs={{0,4},{4,0},{8,12},{12,8},{16,20},{20,16},{24,28},{28,24},{1,5},{5... | collective-permute-start | bytes 6291464 | tf_op jit(solution)/shard_map/ppermute | solution.py:285
  29.4 32.0 %collective-permute-start.5 = (bf16[256,1024]{1,0:T(8,128)(2,1)}, bf16[256,1024]{1,0:T(8,128)(2,1)}, u32[]{:S(2)}, u32[]{:S(2)}) collective-permute-start(bf16[256,1024]{1,0:T(8,128)(2,1)} %collective-permute-done.4.refs_2_), channel_id=1, source_target_pairs={{8,0},{12,4},{16,8},{20,12},{9,1},{13,5},{17,9},{21,13},{10,2},{14... | collective-permute-start | bytes 1572872 | tf_op jit(solution)/shard_map/ppermute | solution.py:288
  39.3 22.1 %collective-permute-start.3 = (bf16[256,1024]{1,0:T(8,128)(2,1)}, bf16[256,1024]{1,0:T(8,128)(2,1)}, u32[]{:S(2)}, u32[]{:S(2)}) collective-permute-start(bf16[256,1024]{1,0:T(8,128)(2,1)} %collective-permute-done.2.refs_1_), channel_id=1, source_target_pairs={{8,16},{12,20},{16,24},{20,28},{9,17},{13,21},{17,25},{21,29},{10,... | collective-permute-start | bytes 1572872 | tf_op jit(solution)/shard_map/ppermute | solution.py:288
  40.7 23.7 %collective-permute-start.13 = (bf16[256,1024]{1,0:T(8,128)(2,1)}, bf16[256,1024]{1,0:T(8,128)(2,1)}, u32[]{:S(2)}, u32[]{:S(2)}) collective-permute-start(bf16[256,1024]{1,0:T(8,128)(2,1)} %collective-permute-done.12.refs_2_), channel_id=1, source_target_pairs={{8,0},{12,4},{16,8},{20,12},{9,1},{13,5},{17,9},{21,13},{10,2},{14... | collective-permute-start | bytes 1572872 | tf_op jit(solution)/shard_map/ppermute | solution.py:288
  42.0 22.4 %collective-permute-start.11 = (bf16[256,1024]{1,0:T(8,128)(2,1)}, bf16[256,1024]{1,0:T(8,128)(2,1)}, u32[]{:S(2)}, u32[]{:S(2)}) collective-permute-start(bf16[256,1024]{1,0:T(8,128)(2,1)} %collective-permute-done.10.refs_1_), channel_id=1, source_target_pairs={{8,16},{12,20},{16,24},{20,28},{9,17},{13,21},{17,25},{21,29},{10,... | collective-permute-start | bytes 1572872 | tf_op jit(solution)/shard_map/ppermute | solution.py:288
  63.1 22.7 %collective-permute-start.6 = (bf16[256,1024]{1,0:T(8,128)(2,1)S(1)}, bf16[256,1024]{1,0:T(8,128)(2,1)S(1)}, u32[]{:S(2)}, u32[]{:S(2)}) collective-permute-start(bf16[256,1024]{1,0:T(8,128)(2,1)S(1)} %broadcast_select_fusion.5.refs_3_), channel_id=1, source_target_pairs={{16,24},{20,28},{8,0},{12,4},{17,25},{21,29},{9,1},{13,5},{18,26},... | collective-permute-start | bytes 1572872 | tf_op jit(solution)/shard_map/ppermute | solution.py:288
  65.5 29.2 %collective-permute-start.14 = (bf16[256,1024]{1,0:T(8,128)(2,1)S(1)}, bf16[256,1024]{1,0:T(8,128)(2,1)S(1)}, u32[]{:S(2)}, u32[]{:S(2)}) collective-permute-start(bf16[256,1024]{1,0:T(8,128)(2,1)S(1)} %broadcast_select_fusion.4.refs_3_), channel_id=1, source_target_pairs={{16,24},{20,28},{8,0},{12,4},{17,25},{21,29},{9,1},{13,5},{18,26},... | collective-permute-start | bytes 1572872 | tf_op jit(solution)/shard_map/ppermute | solution.py:288
  146.5 20.4 %collective-permute-start.21 = (f32[8,128]{1,0:T(8,128)S(1)}, f32[8,128]{1,0:T(8,128)S(1)}, u32[]{:S(2)}, u32[]{:S(2)}) collective-permute-start(f32[8,128]{1,0:T(8,128)S(1)} %get-tuple-element.33), channel_id=1, source_target_pairs={{0,24},{4,28},{8,0},{12,4},{16,8},{20,12},{24,16},{28,20},{1,25},{... | collective-permute-start | bytes 12296 | tf_op jit(solution)/shard_map/ppermute | solution.py:288
  146.8 20.5 %collective-permute-start.20 = (f32[8,128]{1,0:T(8,128)S(1)}, f32[8,128]{1,0:T(8,128)S(1)}, u32[]{:S(2)}, u32[]{:S(2)}) collective-permute-start(f32[8,128]{1,0:T(8,128)S(1)} %get-tuple-element.33), channel_id=1, source_target_pairs={{0,16},{4,20},{8,24},{12,28},{16,0},{20,4},{24,8},{28,12},{1,17},{... | collective-permute-start | bytes 12296 | tf_op jit(solution)/shard_map/ppermute | solution.py:288
  148.6 19.2 %collective-permute-start.19 = (f32[8,128]{1,0:T(8,128)S(1)}, f32[8,128]{1,0:T(8,128)S(1)}, u32[]{:S(2)}, u32[]{:S(2)}) collective-permute-start(f32[8,128]{1,0:T(8,128)S(1)} %get-tuple-element.33), channel_id=1, source_target_pairs={{0,8},{4,12},{8,16},{12,20},{16,24},{20,28},{24,0},{28,4},{1,9},{5... | collective-permute-start | bytes 12296 | tf_op jit(solution)/shard_map/ppermute | solution.py:288
  152.3 21.3 %collective-permute-start.26 = (bf16[256,1024]{1,0:T(8,128)(2,1)S(1)}, bf16[256,1024]{1,0:T(8,128)(2,1)S(1)}, u32[]{:S(2)}, u32[]{:S(2)}) collective-permute-start(bf16[256,1024]{1,0:T(8,128)(2,1)S(1)} %get-tuple-element.36), channel_id=1, source_target_pairs={{0,8},{4,12},{24,16},{28,20},{1,9},{5,13},{25,17},{29,21},{2,10},{... | collective-permute-start | bytes 1572872 | tf_op jit(solution)/shard_map/ppermute | solution.py:288
  166.9 35.8 %collective-permute-start.22 = (bf16[512,1024]{0,1:T(8,128)(2,1)S(1)}, bf16[512,1024]{0,1:T(8,128)(2,1)S(1)}, u32[]{:S(2)}, u32[]{:S(2)}) collective-permute-start(bf16[512,1024]{0,1:T(8,128)(2,1)S(1)} %slice_select_fusion.1), channel_id=1, source_target_pairs={{0,4},{4,0},{8,12},{12,8},{16,20},{20,16},{24,28},{28,24},{1,5},{5... | collective-permute-start | bytes 3145736 | tf_op jit(solution)/shard_map/ppermute | solution.py:285
  175.3 21.8 %collective-permute-start.27 = (bf16[256,1024]{1,0:T(8,128)(2,1)S(1)}, bf16[256,1024]{1,0:T(8,128)(2,1)S(1)}, u32[]{:S(2)}, u32[]{:S(2)}) collective-permute-start(bf16[256,1024]{1,0:T(8,128)(2,1)S(1)} %fusion.6), channel_id=1, source_target_pairs={{0,8},{4,12},{8,16},{12,20},{1,9},{5,13},{9,17},{13,21},{2,10},{6,... | collective-permute-start | bytes 1572872 | tf_op jit(solution)/shard_map/ppermute | solution.py:288
  181.2 24.2 %collective-permute-start.35 = (bf16[256,1024]{1,0:T(8,128)(2,1)S(1)}, bf16[256,1024]{1,0:T(8,128)(2,1)S(1)}, u32[]{:S(2)}, u32[]{:S(2)}) collective-permute-start(bf16[256,1024]{1,0:T(8,128)(2,1)S(1)} %fusion.10), channel_id=1, source_target_pairs={{8,0},{12,4},{16,8},{20,12},{24,16},{28,20},{9,1},{13,5},{17,9},{2... | collective-permute-start | bytes 1572872 | tf_op jit(solution)/shard_map/ppermute | solution.py:288
  186.6 21.7 %collective-permute-start.33 = (bf16[256,1024]{1,0:T(8,128)(2,1)S(1)}, bf16[256,1024]{1,0:T(8,128)(2,1)S(1)}, u32[]{:S(2)}, u32[]{:S(2)}) collective-permute-start(bf16[256,1024]{1,0:T(8,128)(2,1)S(1)} %fusion.8), channel_id=1, source_target_pairs={{0,8},{4,12},{8,16},{12,20},{16,24},{20,28},{1,9},{5,13},{9,17},{1... | collective-permute-start | bytes 1572872 | tf_op jit(solution)/shard_map/ppermute | solution.py:288
  191.9 19.5 %collective-permute-start.30 = (bf16[256,1024]{1,0:T(8,128)(2,1)S(1)}, bf16[256,1024]{1,0:T(8,128)(2,1)S(1)}, u32[]{:S(2)}, u32[]{:S(2)}) collective-permute-start(bf16[256,1024]{1,0:T(8,128)(2,1)S(1)} %fusion.7), channel_id=1, source_target_pairs={{8,0},{12,4},{16,8},{20,12},{24,16},{28,20},{9,1},{13,5},{17,9},{2... | collective-permute-start | bytes 1572872 | tf_op jit(solution)/shard_map/ppermute | solution.py:288
  197.8 21.3 %collective-permute-start.28 = (bf16[256,1024]{1,0:T(8,128)(2,1)S(1)}, bf16[256,1024]{1,0:T(8,128)(2,1)S(1)}, u32[]{:S(2)}, u32[]{:S(2)}) collective-permute-start(bf16[256,1024]{1,0:T(8,128)(2,1)S(1)} %fusion.5), channel_id=1, source_target_pairs={{0,8},{4,12},{8,16},{12,20},{16,24},{20,28},{1,9},{5,13},{9,17},{1... | collective-permute-start | bytes 1572872 | tf_op jit(solution)/shard_map/ppermute | solution.py:288
  204.9 20.6 %collective-permute-start.23 = (bf16[512,256]{0,1:T(8,128)(2,1)}, bf16[512,256]{0,1:T(8,128)(2,1)}, u32[]{:S(2)}, u32[]{:S(2)}) collective-permute-start(bf16[512,256]{0,1:T(8,128)(2,1)} %get-tuple-element.57), channel_id=1, source_target_pairs={{0,1},{1,0},{2,3},{3,2},{4,5},{5,4},{6,7},{7,6},{8,9},{9,8},{10,11... | collective-permute-start | bytes 786440 | tf_op jit(solution)/shard_map/ppermute | solution.py:291
  205.5 20.1 %collective-permute-start.24 = (bf16[512,256]{0,1:T(8,128)(2,1)}, bf16[512,256]{0,1:T(8,128)(2,1)}, u32[]{:S(2)}, u32[]{:S(2)}) collective-permute-start(bf16[512,256]{0,1:T(8,128)(2,1)} %get-tuple-element.58), channel_id=1, source_target_pairs={{0,2},{1,3},{2,0},{3,1},{4,6},{5,7},{6,4},{7,5},{8,10},{9,11},{10,... | collective-permute-start | bytes 786440 | tf_op jit(solution)/shard_map/ppermute | solution.py:291
  211.4 18.4 %collective-permute-start.37 = (bf16[128,1024]{1,0:T(8,128)(2,1)}, bf16[128,1024]{1,0:T(8,128)(2,1)}, u32[]{:S(2)}, u32[]{:S(2)}) collective-permute-start(bf16[128,1024]{1,0:T(8,128)(2,1)} %slice.429), channel_id=1, source_target_pairs={{0,4},{4,0},{8,12},{12,8},{16,20},{20,16},{24,28},{28,24},{1,5},{5... | collective-permute-start | bytes 786440 | tf_op jit(solution)/shard_map/ppermute | solution.py:285
  (43 other events, 441.7 us)

commit v3 on v2

v3 whole, which is shorter than its diff:
```python
import functools
import jax
import jax.numpy as jnp
from jax import lax
from jax.experimental import pallas as pl
from jax.experimental.pallas import tpu as pltpu
from jax.sharding import PartitionSpec as P


ce_weight = 0.5
PARTS = 2
f32, bf16 = jnp.float32, jnp.bfloat16


def dot(a, b):
    return lax.dot_general(a, b, (((1,), (0,)), ((), ())), preferred_element_type=f32)


def dot_nt(a, b):
    return lax.dot_general(a, b, (((1,), (1,)), ((), ())), preferred_element_type=f32)


def lanes(columns, like):
    lane = lax.broadcasted_iota(jnp.int32, like, 1)
    out = jnp.zeros(like, f32)
    for k, c in enumerate(columns):
        out = jnp.where(lane == k, c, out)
    return out


def cost(flops, size, trans=0):
    return pl.CostEstimate(flops=flops, bytes_accessed=size, transcendentals=trans)


def hbm(x):
    return pltpu.with_memory_space_constraint(x, pltpu.HBM)


def out(shape, dtype):
    return pltpu.HBM(shape, dtype)


def params(size):
    return pltpu.CompilerParams(vmem_limit_bytes=size << 20)


def target_kernel(own_tiles, core_ref, mine_ref, came_ref, id_ref, e_ref, stat_ref):
    t = jnp.where(pl.program_id(0) < own_tiles, mine_ref[...], came_ref[...]).astype(f32)
    top = jnp.max(t, axis=1, keepdims=True)
    e = jnp.exp(t - top)
    e_ref[...] = e.astype(bf16)
    total = jnp.sum(e, axis=1, keepdims=True)
    first = jnp.sum(e * t, axis=1, keepdims=True)
    stat_ref[...] = lanes([top, total, first, id_ref[...].astype(f32)], stat_ref.shape)


def target_call(core, logits, came, ids, tile):
    rows, half = came.shape
    n, own_tiles = 2 * rows, rows // tile
    row = lambda i, s: (i, 0)
    return pl.pallas_call(
        functools.partial(target_kernel, own_tiles),
        grid_spec=pltpu.PrefetchScalarGridSpec(
            num_scalar_prefetch=1,
            grid=(n // tile,),
            in_specs=[
                pl.BlockSpec((tile, half), lambda i, s: (jnp.minimum(i, own_tiles - 1), s[0])),
                pl.BlockSpec((tile, half), lambda i, s: (jnp.maximum(i - own_tiles, 0), 0)),
                pl.BlockSpec((tile, 1), row),
            ],
            out_specs=[pl.BlockSpec((tile, half), row), pl.BlockSpec((tile, 128), row)],
        ),
        out_shape=[
            out((n, half), bf16),
            jax.ShapeDtypeStruct((n, 128), f32),
        ],
        compiler_params=params(20),
        cost_estimate=cost(8 * n * half, 4 * n * half, n * half),
        name="target_exps",
    )(core, hbm(logits), hbm(came), ids)


def turn_kernel(x_ref, out_ref):
    out_ref[...] = x_ref[...].T


def turn_call(x, tile):
    n, dh = x.shape
    return pl.pallas_call(
        turn_kernel,
        grid=(n // tile,),
        in_specs=[pl.BlockSpec((tile, dh), lambda i: (i, 0))],
        out_specs=pl.BlockSpec((dh, tile), lambda i: (0, i)),
        out_shape=out((dh, n), bf16),
        compiler_params=params(16),
        cost_estimate=cost(0, 4 * n * dh),
        name="turn",
    )(x)


def choices(nz):
    unique, table = [("own", 0)], []
    for j in range(1, nz):
        table.append((("down", j), ("up", nz - j)))
        unique += [c for c in table[-1] if c not in unique]
    return unique, table


def gathered(up, down, p, nz):
    unique, _ = choices(nz)
    pick = {"own": up, "up": up, "down": down}
    return [pick[k][p][j] for k, j in unique]


def assemble(z, nz, refs, whole_ref, sem):
    unique, table = choices(nz)
    deep = refs[0].shape[0]

    def copy(k, j):
        at = pl.multiple_of(lax.rem(z + j, nz) * deep, deep)
        return pltpu.make_async_copy(refs[k], whole_ref.at[pl.ds(at, deep), :], sem.at[j])

    copy(0, 0).start()
    for j in range(1, nz):
        near, far = (unique.index(c) for c in table[j - 1])

        @pl.when(z + j < nz)
        def _(near=near, j=j):
            copy(near, j).start()

        @pl.when(z + j >= nz)
        def _(far=far, j=j):
            copy(far, j).start()

    return lambda: [copy(0, j).wait() for j in range(nz)]


def last_kernel(part, nz, count, earlier, z_ref, *refs):
    w_refs, refs = refs[:count], refs[count:]
    h_ref, e_ref, t_ref = refs[:3]
    stat_refs = refs[3:3 + earlier]
    outs = refs[3 + earlier:-2]
    whole_ref, sem = refs[-2:]

    @pl.when(pl.program_id(0) == 0)
    def _():
        assemble(z_ref[0], nz, w_refs, whole_ref, sem)()

    z = dot(h_ref[...], whole_ref[...])
    top = jnp.max(z, axis=1, keepdims=True)
    e = jnp.exp(z - top)
    outs[0][...] = e.astype(bf16)
    total = jnp.sum(e, axis=1, keepdims=True)
    cross = jnp.sum(e_ref[...].astype(f32) * z, axis=1, keepdims=True)
    t_stat = t_ref[...]
    column = lax.broadcasted_iota(jnp.int32, z.shape, 1) + part * z.shape[1]
    id_col = t_stat[:, 3:4].astype(jnp.int32)
    own = jnp.sum(jnp.where(column == id_col, z, 0.0), axis=1, keepdims=True)
    like = t_ref.shape
    if part < PARTS - 1:
        outs[1][...] = lanes([top, total, cross, own], like)
        return
    send_ref, turn_ref, tops_ref = outs[1:]
    tops, all_top = [], top
    for r in stat_refs:
        tops.append(r[:, 0:1])
        all_top = jnp.maximum(all_top, r[:, 0:1])
    tops.append(top)
    total = total * jnp.exp(top - all_top)
    for r in stat_refs:
        total = total + r[:, 1:2] * jnp.exp(r[:, 0:1] - all_top)
        cross = cross + r[:, 2:3]
        own = own + r[:, 3:4]
    t_top, t_total, t_first = t_stat[:, 0:1], t_stat[:, 1:2], t_stat[:, 2:3]
    rows = lanes([t_top, t_total, t_first - cross, all_top, total, own], like).T[:8]
    send_ref[...] = rows
    turn_ref[...] = rows
    tops_ref[...] = lanes([t_top] + tops + [t_stat[:, 3:4]], like)


def last_call(part, nz, z, blocks, hid, e_t, t_stat, stats, tile):
    n, dh = hid.shape
    piece = blocks[0].shape[1]
    grid = n // tile
    row = lambda i, s: (i, 0)
    stat_spec = pl.BlockSpec((tile, 128), row)
    in_specs = [pl.BlockSpec(memory_space=pl.ANY)] * len(blocks) + [
        pl.BlockSpec((tile, dh), row),
        pl.BlockSpec((tile, piece), lambda i, s: (i, part)),
        stat_spec,
    ]
    out_specs = [pl.BlockSpec((tile, piece), row)]
    out_shape = [out((n, piece), bf16)]
    if part < PARTS - 1:
        stats = []
        out_specs += [stat_spec]
        out_shape += [jax.ShapeDtypeStruct((n, 128), f32)]
    else:
        in_specs += [stat_spec] * len(stats)
        out_specs += [
            pl.BlockSpec((8, tile), lambda i, s: (0, i)),
            pl.BlockSpec((8, tile), lambda i, s: (0, lax.rem(i + grid // 2, grid))),
            stat_spec,
        ]
        out_shape += [
            jax.ShapeDtypeStruct((8, n), f32),
            jax.ShapeDtypeStruct((8, n), f32),
            jax.ShapeDtypeStruct((n, 128), f32),
        ]
    return pl.pallas_call(
        functools.partial(last_kernel, part, nz, len(blocks), len(stats)),
        grid_spec=pltpu.PrefetchScalarGridSpec(
            num_scalar_prefetch=1,
            grid=(grid,),
            in_specs=in_specs,
            out_specs=out_specs,
            scratch_shapes=[pltpu.VMEM((dh, piece), bf16), pltpu.SemaphoreType.DMA((nz,))],
        ),
        out_shape=out_shape,
        compiler_params=params(20),
        cost_estimate=cost(2 * n * dh * piece, 6 * n * piece, n * piece),
        name="last_draft",
    )(z, *blocks, hbm(hid), hbm(e_t), t_stat, *stats)


def hidden_kernel(nz, count, z_ref, *refs):
    slope_refs, w_refs = refs[:PARTS], refs[PARTS:PARTS + PARTS * count]
    out_ref, whole_ref, sem = refs[PARTS + PARTS * count:]

    @pl.when(pl.program_id(0) == 0)
    def _():
        waits = [
            assemble(z_ref[0], nz, w_refs[p * count:(p + 1) * count], whole_ref.at[p], sem.at[p])
            for p in range(PARTS)
        ]
        for wait in waits:
            wait()

    acc = dot_nt(slope_refs[0][...], whole_ref[0])
    for p in range(1, PARTS):
        acc = acc + dot_nt(slope_refs[p][...], whole_ref[p])
    out_ref[...] = acc.astype(bf16)


def hidden_call(nz, z, slope, blocks, dh, tile):
    n, piece = slope[0].shape
    count = len(blocks[0])
    row = lambda i, s: (i, 0)
    return pl.pallas_call(
        functools.partial(hidden_kernel, nz, count),
        grid_spec=pltpu.PrefetchScalarGridSpec(
            num_scalar_prefetch=1,
            grid=(n // tile,),
            in_specs=[pl.BlockSpec((tile, piece), row)] * PARTS
            + [pl.BlockSpec(memory_space=pl.ANY)] * (PARTS * count),
            out_specs=pl.BlockSpec((tile, dh), row),
            scratch_shapes=[
                pltpu.VMEM((PARTS, dh, piece), bf16),
                pltpu.SemaphoreType.DMA((PARTS, nz)),
            ],
        ),
        out_shape=out((n, dh), bf16),
        compiler_params=params(20),
        cost_estimate=cost(2 * n * dh * piece * PARTS, 8 * n * piece),
        name="hidden_grad",
    )(z, *map(hbm, slope), *[b for bs in blocks for b in bs])


def fold_rows(a, b):
    t_top = jnp.maximum(a[0:1], b[0:1])
    fa, fb = jnp.exp(a[0:1] - t_top), jnp.exp(b[0:1] - t_top)
    z_top = jnp.maximum(a[3:4], b[3:4])
    ga, gb = jnp.exp(a[3:4] - z_top), jnp.exp(b[3:4] - z_top)
    rows = [
        t_top,
        a[1:2] * fa + b[1:2] * fb,
        a[2:3] * fa + b[2:3] * fb,
        z_top,
        a[4:5] * ga + b[4:5] * gb,
        a[5:6] + b[5:6],
    ]
    return jnp.concatenate(rows + [a[6:8]])


def slope_kernel(part, peers, idx_ref, *refs):
    step = pl.program_id(0)
    if peers:
        tops_ref = refs[peers]
        ez_ref, et_ref, ht_ref = refs[peers + 1:peers + 4]
        slope_ref, msg_ref, coef_ref, loss_ref = refs[peers + 4:]

        @pl.when(step == 0)
        def _():
            got = [r[...] for r in refs[:peers]]
            while len(got) > 1:
                got = [fold_rows(got[j], got[j + 1]) for j in range(0, len(got), 2)]
            s = got[0]
            t_inv = 1.0 / s[1:2]
            lse_t = s[0:1] + jnp.log(s[1:2])
            lse_z = s[3:4] + jnp.log(s[4:5])
            n = s.shape[1]
            per_token = s[2:3] * t_inv - lse_t + (1.0 + ce_weight) * lse_z - ce_weight * s[5:6]
            plane = jnp.sum(per_token[:, :n // 2], axis=1, keepdims=True) + jnp.sum(
                per_token[:, n // 2:], axis=1, keepdims=True
            )
            loss_ref[...] = jnp.broadcast_to(plane, loss_ref.shape)
            z_inv = (1.0 + ce_weight) / s[4:5]
            flat = jnp.concatenate([s[0:1], t_inv, s[3:4], z_inv, jnp.zeros((124, n), f32)]).T
            tops = tops_ref[...]
            lane = lax.broadcasted_iota(jnp.int32, tops.shape, 1)
            base = jnp.where(lane == 0, flat[:, 0:1], flat[:, 2:3])
            gain = jnp.where(lane == 0, flat[:, 1:2], flat[:, 3:4])
            coef_ref[...] = jnp.where(lane <= PARTS, jnp.exp(tops - base) * gain, tops)

    else:
        coef_ref, ez_ref, et_ref, ht_ref, slope_ref, msg_ref = refs
    b = coef_ref[:, 0:1]
    a = coef_ref[:, part + 1:part + 2]
    value = ez_ref[...].astype(f32) * a - et_ref[...].astype(f32) * b
    column = lax.broadcasted_iota(jnp.int32, value.shape, 1)
    tile = value.shape[1]
    start = (part * pl.num_programs(0) + step) * tile
    id_col = coef_ref[:, PARTS + 1:PARTS + 2].astype(jnp.int32) - start
    value = jnp.where(column == id_col, value - ce_weight, value)
    slope = value.astype(bf16)
    slope_ref[...] = slope
    msg_ref[...] = dot(ht_ref[...], slope).astype(bf16)


def slope_call(part, index, head_args, e_z, e_t, hid_t, deep, tile):
    n, piece = e_z.shape
    peers = len(head_args) - 1
    steps = piece // tile
    fixed = lambda i, s: (0, 0)
    in_specs = [pl.BlockSpec(a.shape, fixed) for a in head_args] + [
        pl.BlockSpec((n, tile), lambda i, s: (0, i)),
        pl.BlockSpec((n, tile), lambda i, s: (0, part * steps + i)),
        pl.BlockSpec((deep, n), lambda i, s: (s[0], 0)),
    ]
    out_specs = [
        pl.BlockSpec((n, tile), lambda i, s: (0, i)),
        pl.BlockSpec((deep, tile), lambda i, s: (0, i)),
    ]
    out_shape = [
        out((n, piece), bf16),
        out((deep, piece), bf16),
    ]
    if peers:
        out_specs += [pl.BlockSpec((n, 128), fixed), pl.BlockSpec((8, 128), fixed)]
        out_shape += [
            jax.ShapeDtypeStruct((n, 128), f32),
            jax.ShapeDtypeStruct((8, 128), f32),
        ]
    return pl.pallas_call(
        functools.partial(slope_kernel, part, peers),
        grid_spec=pltpu.PrefetchScalarGridSpec(
            num_scalar_prefetch=1, grid=(steps,), in_specs=in_specs, out_specs=out_specs
        ),
        out_shape=out_shape,
        compiler_params=params(28),
        cost_estimate=cost(2 * n * deep * piece, 6 * n * piece),
        name="slope",
    )(index, *head_args, hbm(e_z), hbm(e_t), hbm(hid_t))


def body(n_tok, n_voc, hidden, head, logits, ids):
    nz = n_tok // 2
    rows, dh = hidden.shape
    own_rows, share = head.shape
    half = share // 2
    piece = half // PARTS
    deep = 2 * own_rows
    tile = min(256, rows)
    wide = min(512, piece)
    me = lax.axis_index("tok")
    core = lax.rem(me, 2)
    z = lax.div(me, 2)
    voc = lax.axis_index("voc")

    def swap(x):
        return lax.ppermute(x, "tok", [(i, i ^ 1) for i in range(n_tok)])

    def hop(x, pairs):
        return lax.ppermute(x, "tok", [(2 * a + k, 2 * b + k) for a, b in pairs for k in range(2)])

    def plane_swap(x, v):
        return lax.ppermute(x, "voc", [(w, w ^ v) for w in range(n_voc)])

    def mine(x, other=False):
        return jnp.where((core == 0) != other, x[:, :half], x[:, half:])

    def scalar(x):
        return jnp.reshape(x, (1,)).astype(jnp.int32)

    keep, send = mine(head), mine(head, True)
    blocks = []
    for p in range(PARTS):
        cut = slice(p * piece, (p + 1) * piece)
        other = swap(send[:, cut])
        blocks.append(
            jnp.where(
                core == 0,
                jnp.concatenate([keep[:, cut], other]),
                jnp.concatenate([other, keep[:, cut]]),
            )
        )

    up = [[b] for b in blocks]
    down = [[b] for b in blocks]
    for s in range(1, nz):
        up_pairs = [(a, a + 1) for a in range(s - 1, nz - 1)]
        down_pairs = [(a, a - 1) for a in range(1, nz - s + 1)]
        for p in range(PARTS):
            u, d = up[p][-1], down[p][-1]
            if 2 * s > nz + 1:
                both = hop(jnp.where(z >= s - 1, u, d), up_pairs + down_pairs)
                up[p].append(both)
                down[p].append(both)
            else:
                up[p].append(hop(u, up_pairs))
                down[p].append(hop(d, down_pairs))

    hid = hbm(jnp.concatenate([hidden, swap(hidden)]))
    hid_t = turn_call(hid, tile)
    tgt = mine(logits, True)
    tgt = swap(tgt)
    local = jnp.concatenate([ids, swap(ids)]) - (voc * share + core * half)
    e_t, t_stat = target_call(scalar(core), logits, tgt, local[:, None], tile)

    stats, e_z = [], []
    whole = [gathered(up, down, p, nz) for p in range(PARTS)]
    for p in range(PARTS):
        outs = last_call(p, nz, scalar(z), whole[p], hid, e_t, t_stat, stats, tile)
        e_z.append(outs[0])
        if p < PARTS - 1:
            stats.append(outs[1])
    mine_rows, turned, tops = outs[1:]

    x = fold_rows(mine_rows, swap(turned))
    bits = n_voc.bit_length() - 1
    done = 0
    while True:
        few = min(2, bits - done)
        got = [x] + [plane_swap(x, v << done) for v in range(1, 1 << few)]
        done += few
        if done >= bits:
            break
        while len(got) > 1:
            got = [fold_rows(got[j], got[j + 1]) for j in range(0, len(got), 2)]
        x = got[0]

    def first_row(s):
        return jnp.where(z < s, jnp.minimum(z + nz - s, nz - 1), jnp.maximum(z - nz + s, 0))

    msgs, slope = [], []
    for p in range(PARTS):
        head_args = got + [tops] if p == 0 else [coef]
        outs = slope_call(
            p, scalar(first_row(1)), head_args, e_z[p], e_t, hid_t, deep, wide
        )
        slope.append(outs[0])
        msgs.append(outs[1])
        if p == 0:
            coef, plane = outs[2:]

    def grad_rows(index, p):
        return dot(lax.dynamic_slice_in_dim(hid_t, index * deep, deep, 0), slope[p])

    got_up, got_down = [None] * PARTS, [None] * PARTS
    for s in range(1, nz):
        up_pairs = [(a, a + 1) for a in range(0, s)]
        down_pairs = [(a, a - 1) for a in range(nz - s, nz)]
        for p in range(PARTS):
            if 2 * s <= nz:
                if s == 1:
                    msg = msgs[p]
                else:
                    msg = grad_rows(first_row(s), p) + got_up[p].astype(f32)
                    if got_down[p] is not got_up[p]:
                        msg = msg + got_down[p].astype(f32)
                    msg = msg.astype(bf16)
                if 2 * s < nz - 1:
                    got_up[p] = got_down[p] = hop(msg, up_pairs + down_pairs)
                else:
                    got_up[p] = hop(msg, up_pairs)
                    got_down[p] = hop(msg, down_pairs)
            else:
                msg_up = grad_rows(jnp.minimum(z + nz - s, nz - 1), p) + got_up[p].astype(f32)
                msg_down = grad_rows(jnp.maximum(z - nz + s, 0), p) + got_down[p].astype(f32)
                got_up[p] = hop(msg_up.astype(bf16), up_pairs)
                got_down[p] = hop(msg_down.astype(bf16), down_pairs)
    keeps, gives = [], []
    for p in range(PARTS):
        full = grad_rows(z, p) + got_up[p].astype(f32) + got_down[p].astype(f32)
        low, high = full[:own_rows], full[own_rows:]
        keeps.append(jnp.where(core == 0, low, high))
        give = jnp.where(core == 0, high, low).astype(bf16)
        gives.append(swap(give).astype(f32))
    grad_head = jnp.where(
        core == 0,
        jnp.concatenate(keeps + gives, axis=1),
        jnp.concatenate(gives + keeps, axis=1),
    )

    late, plane, _ = lax.optimization_barrier((slope, plane, msgs[-1]))
    planes = [hop(plane, [(a, (a + k) % nz) for a in range(nz)]) for k in range(1, nz)]
    planes, _ = lax.optimization_barrier(([plane] + planes, got_up[0]))
    spot = lax.broadcasted_iota(jnp.int32, (nz, 1), 0)
    every = jnp.zeros((nz, 1), f32)
    for k in range(nz):
        every = jnp.where(spot == lax.rem(z - k + nz, nz), planes[k][:1, :1], every)
    loss = jnp.sum(every) / (rows * n_tok)

    part = hidden_call(nz, scalar(z), late, whole, dh, tile)
    part = part[:rows].astype(f32) + swap(part[rows:]).astype(f32)
    width = dh // n_voc

    def wide_slice(w):
        return lax.dynamic_slice_in_dim(part, w * width, width, 1)

    grad_hidden = wide_slice(voc)
    for v in range(1, n_voc):
        came = plane_swap(wide_slice(voc ^ v).astype(bf16), v)
        grad_hidden = grad_hidden + came.astype(f32)
    return loss, grad_hidden, grad_head


def solution(mesh):
    placed = (P("tok", None), P("tok", "voc"), P("tok", "voc"), P("tok"))
    n_tok, n_voc = mesh.shape["tok"], mesh.shape["voc"]
    return jax.shard_map(
        functools.partial(body, n_tok, n_voc),
        mesh=mesh,
        in_specs=placed,
        out_specs=(P(), P("tok", "voc"), P("tok", "voc")),
        check_vma=False,
    )
```

time: 237 us -> 210 us (0.89)
  other arithmetic: 50.3 us -> 11.7 us
  waiting for transfers between devices: 46.2 us -> 63.8 us
  local copies, waits for them, and re-layouts: 21.1 us -> 10.1 us
  Pallas kernels: 40.3 us -> 47.3 us
  matrix products: 11.1 us -> 8.69 us
    ppermute x23, waiting for transfers between devices: 42.8 us -> 60.2 us  [hop(): lax.ppermute(x, 'tok', [(2 * a + k, 2 * b + k) for a, b in pairs for k in...]
    unnamed x10 -> x0, other arithmetic: 12.3 us -> none
    concatenate x7 -> x0, other arithmetic: 10.5 us -> none  [the longest x1 4.24 us: body(): tgt = jnp.concatenate([mine(logits), swap(mine(logits, True))])]
    unnamed x73 -> x45, local copies, waits for them, and re-layouts: 12.6 us -> 3.95 us
    pallas_call x5, Pallas kernels: 28.6 us -> 36.5 us  [the longest x2 17 us: last_call(): pl.pallas_call(functools.partial(last_kernel, part, nz, len(blocks), len(...]
    dot_general x2 -> x0, matrix products: 4.76 us -> none  [dot_nt(): lax.dot_general(a, b, (((1,), (1,)), ((), ())), preferred_element_type=f32)]
    select_n x4 -> x6, other arithmetic: 8.06 us -> 3.36 us  [the longest x2 2.98 us: mine(): return jnp.where((core == 0) != other, x[:, :half], x[:, half:])]
    transpose x1 -> x0, other arithmetic: 4.14 us -> none  [body(): hid_t = hid.T]
  transfers between devices with their start and end apart: 38 -> 38, of which waited for: 13 -> 15; matrix products, arithmetic and copies ran while one was open for 29% -> 12% of each run, Pallas kernels for 5% -> 13%
where the time goes in v3:
time: 210 us; the launch traced here: 209 us
  starting transfers between devices  63.9 us (30%)
  waiting for transfers between devices  63.8 us (30%)
  Pallas kernels  47.3 us (23%)
  other arithmetic  11.7 us (6%)
  local copies, waits for them, and re-layouts  10.1 us (5%)
  matrix products  8.69 us (4%)
  between operations  3.15 us (2%)
    ppermute x23, waiting for transfers between devices, hop(): lax.ppermute(x, 'tok', [(2 * a + k, 2 * b + k) for a, b in pairs for k in...  60.2 us
    ppermute x23, starting transfers between devices, hop(): lax.ppermute(x, 'tok', [(2 * a + k, 2 * b + k) for a, b in pairs for k in...  54.9 us
    pallas_call x2, Pallas kernels, last_call(): pl.pallas_call(functools.partial(last_kernel, part, nz, len(blocks), len(...  17 us
    pallas_call x2, Pallas kernels, slope_call(): pl.pallas_call(functools.partial(slope_kernel, part, peers), grid_spec=pl...  10.8 us
    dot_general x8, matrix products, dot(): lax.dot_general(a, b, (((1,), (0,)), ((), ())), preferred_element_type=f32)  8.69 us
    pallas_call x1, Pallas kernels, hidden_call(): pl.pallas_call(functools.partial(hidden_kernel, nz, count), grid_spec=plt...  8.56 us
    ppermute x6, starting transfers between devices, plane_swap(): return lax.ppermute(x, 'voc', [(w, w ^ v) for w in range(n_voc)])  7.62 us
    pallas_call x1, Pallas kernels, target_call(): pl.pallas_call(functools.partial(target_kernel, own_tiles), grid_spec=plt...  6.71 us
  transfers between devices with their start and end apart: 38, of which 15 were waited for; matrix products, arithmetic and copies ran while one was open for 12% of the time, Pallas kernels for 13%

profile of v3, /device:TPU:0, one launch (start us, length us, event | category | flops | bytes accessed | tf_op | source)
XLA Modules:
  0.0 208.7 jit_solution(1656138514648798669)
XLA Ops:
  4.0 5.0 %collective-permute-start.11 = (bf16[256,1024]{1,0:T(8,128)(2,1)S(1)}, bf16[256,1024]{1,0:T(8,128)(2,1)S(1)}, u32[]{:S(2)}, u32[]{:S(2)}) collective-permute-start(bf16[256,1024]{1,0:T(8,128)(2,1)S(1)} %maximum_select_fusion.2.refs_0_.refs_2_), channel_id=1, source_target_pairs={{0,8},{4,12},{8,16},{12,20},{16,24},{20,28},{1,9},{5,13},{9,17},{1... | collective-permute-start | bytes 1572872 | tf_op jit(solution)/shard_map/ppermute | solution.py:384
  15.1 5.4 %collective-permute-start.2 = (bf16[256,1024]{1,0:T(8,128)(2,1)S(1)}, bf16[256,1024]{1,0:T(8,128)(2,1)}, u32[]{:S(2)}, u32[]{:S(2)}) collective-permute-start(bf16[256,1024]{1,0:T(8,128)(2,1)S(1)} %maximum_select_fusion.1.refs_0_.refs_9_), channel_id=1, source_target_pairs={{0,8},{4,12},{8,16},{12,20},{16,24},{20,28},{1,9},{5,13},{9,17},{1... | collective-permute-start | bytes 1572872 | tf_op jit(solution)/shard_map/ppermute | solution.py:384
  22.4 5.0 %collective-permute-done.10.refs_1_.refs_3_ = bf16[256,1024]{1,0:T(8,128)(2,1)} collective-permute-done((bf16[256,1024]{1,0:T(8,128)(2,1)S(1)}, bf16[256,1024]{1,0:T(8,128)(2,1)}, u32[]{:S(2)}, u32[]{:S(2)}) %collective-permute-start.10) | collective-permute-done | bytes 524320 | tf_op jit(solution)/shard_map/ppermute | solution.py:384
  28.7 9.8 %collective-permute-done.1.refs_1_.refs_10_ = bf16[256,1024]{1,0:T(8,128)(2,1)S(1)} collective-permute-done((bf16[256,1024]{1,0:T(8,128)(2,1)S(1)}, bf16[256,1024]{1,0:T(8,128)(2,1)S(1)}, u32[]{:S(2)}, u32[]{:S(2)}) %collective-permute-start.1) | collective-permute-done | bytes 524320 | tf_op jit(solution)/shard_map/ppermute | solution.py:384
  43.9 5.9 %collective-permute-done.13.refs_3_.refs_5_ = bf16[256,1024]{1,0:T(8,128)(2,1)S(1)} collective-permute-done((bf16[256,1024]{1,0:T(8,128)(2,1)}, bf16[256,1024]{1,0:T(8,128)(2,1)S(1)}, u32[]{:S(2)}, u32[]{:S(2)}) %collective-permute-start.13) | collective-permute-done | bytes 524320 | tf_op jit(solution)/shard_map/ppermute | solution.py:384
  51.1 9.9 %collective-permute-done.4.refs_3_.refs_12_ = bf16[256,1024]{1,0:T(8,128)(2,1)S(1)} collective-permute-done((bf16[256,1024]{1,0:T(8,128)(2,1)S(1)}, bf16[256,1024]{1,0:T(8,128)(2,1)S(1)}, u32[]{:S(2)}, u32[]{:S(2)}) %collective-permute-start.4) | collective-permute-done | bytes 524320 | tf_op jit(solution)/shard_map/ppermute | solution.py:384
  63.7 6.7 %target_exps.1 = (bf16[1024,2048]{1,0:T(8,128)(2,1)}, f32[1024,128]{1,0:T(8,128)S(1)}) custom-call(s32[1]{0:T(128)} %bitcast.2.core_ref, bf16[512,4096]{1,0:T(8,128)(2,1)} %mine_ref.1, bf16[512,2048]{1,0:T(8,128)(2,1)} %collective-permute-done.7.came_ref, s32[1024,1]{1,0:T(8,128)S(1)} %broadcast_subtract_fusion.id_ref), custom_call_target="tpu_custom_call" | custom-call | flops 16777216 | bytes 8388608 | tf_op jit(solution)/shard_map/target_exps/pallas_call | solution.py:61
  72.2 8.0 %last_draft.2 = (bf16[1024,1024]{1,0:T(8,128)(2,1)}, f32[1024,128]{1,0:T(8,128)S(1)}) custom-call(s32[1]{0:T(128)} %bitcast.1.z_ref, bf16[256,1024]{1,0:T(8,128)(2,1)S(1)} %copy-done.1, bf16[256,1024]{1,0:T(8,128)(2,1)} %collective-permute-done.10.refs_1_.refs_3_, bf16[256,1024]{1,0:T(8,128)(2,1)S(1)} %collective-permute-done.14.refs_2_.refs_5_.refs_4_.refs_7_, ...), custom_call_target="tpu_custom_call" | custom-call | flops 2147483648 | bytes 6291456 | tf_op jit(solution)/shard_map/last_draft/pallas_call | solution.py:210
  80.2 2.7 %collective-permute-done.5.refs_2_.refs_5_.refs_11_.refs_14_ = bf16[256,1024]{1,0:T(8,128)(2,1)S(1)} collective-permute-done((bf16[256,1024]{1,0:T(8,128)(2,1)S(1)}, bf16[256,1024]{1,0:T(8,128)(2,1)S(1)}, u32[]{:S(2)}, u32[]{:S(2)}) %collective-permute-start.5) | collective-permute-done | bytes 524320 | tf_op jit(solution)/shard_map/ppermute | solution.py:384
  83.0 9.0 %last_draft.3 = (bf16[1024,1024]{1,0:T(8,128)(2,1)}, f32[8,1024]{1,0:T(8,128)S(1)}, f32[8,1024]{1,0:T(8,128)S(1)}, f32[1024,128]{1,0:T(8,128)S(1)}) custom-call(s32[1]{0:T(128)} %bitcast.1.z_ref, bf16[256,1024]{1,0:T(8,128)(2,1)S(1)} %maximum_select_fusion.1.refs_0_.refs_9_, bf16[256,1024]{1,0:T(8,128)(2,1)S(1)} %copy-done.6, ...), custom_call_target="tpu_custom_call" | custom-call | flops 2147483648 | bytes 6291456 | tf_op jit(solution)/shard_map/last_draft/pallas_call | solution.py:210
  97.6 4.3 %turn.1.refs_7_.refs_3_ = bf16[1024,1024]{1,0:T(8,128)(2,1)} custom-call(bf16[1024,1024]{1,0:T(8,128)(2,1)} %copy-done.15), custom_call_target="tpu_custom_call" | custom-call | bytes 4194304 | tf_op jit(solution)/shard_map/turn/pallas_call | solution.py:89
  102.0 5.7 %slope.2 = (bf16[1024,1024]{1,0:T(8,128)(2,1)}, bf16[256,1024]{1,0:T(8,128)(2,1)}, f32[1024,128]{1,0:T(8,128)S(1)}, f32[8,128]{1,0:T(8,128)S(1)}) custom-call(s32[1]{0:T(128)} %bitcast.idx_ref, f32[8,1024]{1,0:T(8,128)S(1)} %concatenate.46.refs_0_, f32[8,1024]{1,0:T(8,128)S(1)} %collective-permute-done.16.refs_1_, ...), custom_call_target="tpu_custom_call" | custom-call | flops 536870912 | bytes 6291456 | tf_op jit(solution)/shard_map/slope/pallas_call | solution.py:354
  107.7 5.1 %slope.3 = (bf16[1024,1024]{1,0:T(8,128)(2,1)}, bf16[256,1024]{1,0:T(8,128)(2,1)}) custom-call(s32[1]{0:T(128)} %bitcast.idx_ref, f32[1024,128]{1,0:T(8,128)S(1)} %get-tuple-element.32.refs_0_, bf16[1024,1024]{1,0:T(8,128)(2,1)} %get-tuple-element.33.refs_1_, bf16[1024,2048]{1,0:T(8,128)(2,1)} %get-tuple-element.24.refs_8_.refs_6_.refs_2_, ...), custom_call_target="tpu_custom_call" | custom-call | flops 536870912 | bytes 6291456 | tf_op jit(solution)/shard_map/slope/pallas_call | solution.py:354
  112.8 3.3 %collective-permute-start.22 = (bf16[256,1024]{1,0:T(8,128)(2,1)}, bf16[256,1024]{1,0:T(8,128)(2,1)}, u32[]{:S(2)}, u32[]{:S(2)}) collective-permute-start(bf16[256,1024]{1,0:T(8,128)(2,1)} %get-tuple-element.38), channel_id=1, source_target_pairs={{0,8},{4,12},{24,16},{28,20},{1,9},{5,13},{25,17},{29,21},{2,10},{... | collective-permute-start | bytes 1572872 | tf_op jit(solution)/shard_map/ppermute | solution.py:384
  116.1 8.6 %hidden_grad.1 = bf16[1024,1024]{1,0:T(8,128)(2,1)} custom-call(s32[1]{0:T(128)} %bitcast.1.z_ref, bf16[1024,1024]{1,0:T(8,128)(2,1)} %get-tuple-element.43.refs_0_, bf16[1024,1024]{1,0:T(8,128)(2,1)} %get-tuple-element.44.refs_1_, bf16[256,1024]{1,0:T(8,128)(2,1)S(1)} %copy-done.2, bf16[256,1024]{1,0:T(8,128)(2,1)} %collective-permute-done.10.refs_1_.refs_3_, ...), custom_call_target="tpu_custom_call" | custom-call | flops 4294967296 | bytes 8388608 | tf_op jit(solution)/shard_map/hidden_grad/pallas_call | solution.py:249
  133.2 6.9 %collective-permute-done.31 = bf16[256,1024]{1,0:T(8,128)(2,1)} collective-permute-done((bf16[256,1024]{1,0:T(8,128)(2,1)}, bf16[256,1024]{1,0:T(8,128)(2,1)}, u32[]{:S(2)}, u32[]{:S(2)}) %collective-permute-start.31) | collective-permute-done | bytes 524320 | tf_op jit(solution)/shard_map/ppermute | solution.py:384
  142.8 5.0 %collective-permute-start.32 = (bf16[256,1024]{1,0:T(8,128)(2,1)S(1)}, bf16[256,1024]{1,0:T(8,128)(2,1)S(1)}, u32[]{:S(2)}, u32[]{:S(2)}) collective-permute-start(bf16[256,1024]{1,0:T(8,128)(2,1)S(1)} %fusion.6), channel_id=1, source_target_pairs={{0,8},{4,12},{8,16},{12,20},{1,9},{5,13},{9,17},{13,21},{2,10},{6,... | collective-permute-start | bytes 1572872 | tf_op jit(solution)/shard_map/ppermute | solution.py:384
  155.8 6.5 %collective-permute-done.32 = bf16[256,1024]{1,0:T(8,128)(2,1)S(1)} collective-permute-done((bf16[256,1024]{1,0:T(8,128)(2,1)S(1)}, bf16[256,1024]{1,0:T(8,128)(2,1)S(1)}, u32[]{:S(2)}, u32[]{:S(2)}) %collective-permute-start.32) | collective-permute-done | bytes 524320 | tf_op jit(solution)/shard_map/ppermute | solution.py:384
  164.3 10.1 %collective-permute-start.33 = (bf16[256,1024]{1,0:T(8,128)(2,1)S(1)}, bf16[256,1024]{1,0:T(8,128)(2,1)S(1)}, u32[]{:S(2)}, u32[]{:S(2)}) collective-permute-start(bf16[256,1024]{1,0:T(8,128)(2,1)S(1)} %fusion.5), channel_id=1, source_target_pairs={{0,8},{4,12},{8,16},{12,20},{16,24},{20,28},{1,9},{5,13},{9,17},{1... | collective-permute-start | bytes 1572872 | tf_op jit(solution)/shard_map/ppermute | solution.py:384
  175.3 3.8 %collective-permute-start.21 = (f32[8,128]{1,0:T(8,128)S(1)}, f32[8,128]{1,0:T(8,128)S(1)}, u32[]{:S(2)}, u32[]{:S(2)}) collective-permute-start(f32[8,128]{1,0:T(8,128)S(1)} %get-tuple-element.42), channel_id=1, source_target_pairs={{0,24},{4,28},{8,0},{12,4},{16,8},{20,12},{24,16},{28,20},{1,25},{... | collective-permute-start | bytes 12296 | tf_op jit(solution)/shard_map/ppermute | solution.py:384
  180.0 4.6 %collective-permute-start.24 = (bf16[256,1024]{1,0:T(8,128)(2,1)S(1)}, bf16[256,1024]{1,0:T(8,128)(2,1)S(1)}, u32[]{:S(2)}, u32[]{:S(2)}) collective-permute-start(bf16[256,1024]{1,0:T(8,128)(2,1)S(1)} %fusion.2), channel_id=1, source_target_pairs={{0,8},{4,12},{8,16},{12,20},{16,24},{20,28},{1,9},{5,13},{9,17},{1... | collective-permute-start | bytes 1572872 | tf_op jit(solution)/shard_map/ppermute | solution.py:384
  187.5 7.3 %collective-permute-done.24 = bf16[256,1024]{1,0:T(8,128)(2,1)S(1)} collective-permute-done((bf16[256,1024]{1,0:T(8,128)(2,1)S(1)}, bf16[256,1024]{1,0:T(8,128)(2,1)S(1)}, u32[]{:S(2)}, u32[]{:S(2)}) %collective-permute-start.24) | collective-permute-done | bytes 524320 | tf_op jit(solution)/shard_map/ppermute | solution.py:384
  194.8 4.1 %collective-permute-done.30 = bf16[256,1024]{1,0:T(8,128)(2,1)S(1)} collective-permute-done((bf16[256,1024]{1,0:T(8,128)(2,1)S(1)}, bf16[256,1024]{1,0:T(8,128)(2,1)S(1)}, u32[]{:S(2)}, u32[]{:S(2)}) %collective-permute-start.30) | collective-permute-done | bytes 524320 | tf_op jit(solution)/shard_map/ppermute | solution.py:384
  202.0 3.1 %fusion.27 = f32[]{:T(128)} fusion(f32[]{:T(128)} %bitcast.8, s32[]{:T(128)S(6)} %rem.85, f32[]{:T(128)} %bitcast.7, s32[]{:T(128)S(6)} %rem.79, f32[]{:T(128)} %bitcast.6, s32[]{:T(128)S(6)} %rem.73, f32[]{:T(128)} %bitcast.5, s32[]{:T(128)S(6)} %rem.64), kind=kLoop, calls=%fused_computation.68 | loop fusion | flops 35 | bytes 36 | tf_op jit(solution)/shard_map/reduce_sum | solution.py:512
  (144 shorter events, 59.7 us)
Async XLA Ops:
  4.0 16.8 %collective-permute-start.11 = (bf16[256,1024]{1,0:T(8,128)(2,1)S(1)}, bf16[256,1024]{1,0:T(8,128)(2,1)S(1)}, u32[]{:S(2)}, u32[]{:S(2)}) collective-permute-start(bf16[256,1024]{1,0:T(8,128)(2,1)S(1)} %maximum_select_fusion.2.refs_0_.refs_2_), channel_id=1, source_target_pairs={{0,8},{4,12},{8,16},{12,20},{16,24},{20,28},{1,9},{5,13},{9,17},{1... | collective-permute-start | bytes 1572872 | tf_op jit(solution)/shard_map/ppermute | solution.py:384
  10.6 53.1 %collective-permute-start.7 = (bf16[512,2048]{1,0:T(8,128)(2,1)}, bf16[512,2048]{1,0:T(8,128)(2,1)}, u32[]{:S(2)}, u32[]{:S(2)}) collective-permute-start(bf16[512,2048]{1,0:T(8,128)(2,1)} %slice_select_fusion), channel_id=1, source_target_pairs={{0,4},{4,0},{8,12},{12,8},{16,20},{20,16},{24,28},{28,24},{1,5},{5... | collective-permute-start | bytes 6291464 | tf_op jit(solution)/shard_map/ppermute | solution.py:381
  10.6 16.8 %collective-permute-start.10 = (bf16[256,1024]{1,0:T(8,128)(2,1)S(1)}, bf16[256,1024]{1,0:T(8,128)(2,1)}, u32[]{:S(2)}, u32[]{:S(2)}) collective-permute-start(bf16[256,1024]{1,0:T(8,128)(2,1)S(1)} %maximum_select_fusion.2.refs_0_.refs_2_), channel_id=1, source_target_pairs={{8,0},{12,4},{16,8},{20,12},{24,16},{28,20},{9,1},{13,5},{17,9},{2... | collective-permute-start | bytes 1572872 | tf_op jit(solution)/shard_map/ppermute | solution.py:384
  12.0 26.5 %collective-permute-start.1 = (bf16[256,1024]{1,0:T(8,128)(2,1)S(1)}, bf16[256,1024]{1,0:T(8,128)(2,1)S(1)}, u32[]{:S(2)}, u32[]{:S(2)}) collective-permute-start(bf16[256,1024]{1,0:T(8,128)(2,1)S(1)} %maximum_select_fusion.1.refs_0_.refs_9_), channel_id=1, source_target_pairs={{8,0},{12,4},{16,8},{20,12},{24,16},{28,20},{9,1},{13,5},{17,9},{2... | collective-permute-start | bytes 1572872 | tf_op jit(solution)/shard_map/ppermute | solution.py:384
  15.1 23.4 %collective-permute-start.2 = (bf16[256,1024]{1,0:T(8,128)(2,1)S(1)}, bf16[256,1024]{1,0:T(8,128)(2,1)}, u32[]{:S(2)}, u32[]{:S(2)}) collective-permute-start(bf16[256,1024]{1,0:T(8,128)(2,1)S(1)} %maximum_select_fusion.1.refs_0_.refs_9_), channel_id=1, source_target_pairs={{0,8},{4,12},{8,16},{12,20},{16,24},{20,28},{1,9},{5,13},{9,17},{1... | collective-permute-start | bytes 1572872 | tf_op jit(solution)/shard_map/ppermute | solution.py:384
  20.8 18.4 %collective-permute-start.12 = (bf16[256,1024]{1,0:T(8,128)(2,1)S(1)}, bf16[256,1024]{1,0:T(8,128)(2,1)S(1)}, u32[]{:S(2)}, u32[]{:S(2)}) collective-permute-start(bf16[256,1024]{1,0:T(8,128)(2,1)S(1)} %collective-permute-done.11.refs_6_.refs_8_), channel_id=1, source_target_pairs={{8,16},{12,20},{16,24},{20,28},{9,17},{13,21},{17,25},{21,29},{10,... | collective-permute-start | bytes 1572872 | tf_op jit(solution)/shard_map/ppermute | solution.py:384
  27.4 22.4 %collective-permute-start.13 = (bf16[256,1024]{1,0:T(8,128)(2,1)}, bf16[256,1024]{1,0:T(8,128)(2,1)S(1)}, u32[]{:S(2)}, u32[]{:S(2)}) collective-permute-start(bf16[256,1024]{1,0:T(8,128)(2,1)} %collective-permute-done.10.refs_1_.refs_3_), channel_id=1, source_target_pairs={{8,0},{12,4},{16,8},{20,12},{9,1},{13,5},{17,9},{21,13},{10,2},{14... | collective-permute-start | bytes 1572872 | tf_op jit(solution)/shard_map/ppermute | solution.py:384
  38.5 23.9 %collective-permute-start.6 = (bf16[512,1024]{1,0:T(8,128)(2,1)}, bf16[512,1024]{1,0:T(8,128)(2,1)}, u32[]{:S(2)}, u32[]{:S(2)}) collective-permute-start(bf16[512,1024]{1,0:T(8,128)(2,1)} %param.4), channel_id=1, source_target_pairs={{0,4},{4,0},{8,12},{12,8},{16,20},{20,16},{24,28},{28,24},{1,5},{5... | collective-permute-start | bytes 3145736 | tf_op jit(solution)/shard_map/ppermute | solution.py:381
  39.2 21.7 %collective-permute-start.4 = (bf16[256,1024]{1,0:T(8,128)(2,1)S(1)}, bf16[256,1024]{1,0:T(8,128)(2,1)S(1)}, u32[]{:S(2)}, u32[]{:S(2)}) collective-permute-start(bf16[256,1024]{1,0:T(8,128)(2,1)S(1)} %collective-permute-done.1.refs_1_.refs_10_), channel_id=1, source_target_pairs={{8,0},{12,4},{16,8},{20,12},{9,1},{13,5},{17,9},{21,13},{10,2},{14... | collective-permute-start | bytes 1572872 | tf_op jit(solution)/shard_map/ppermute | solution.py:384
  49.8 22.4 %collective-permute-start.14 = (bf16[256,1024]{1,0:T(8,128)(2,1)S(1)}, bf16[256,1024]{1,0:T(8,128)(2,1)S(1)}, u32[]{:S(2)}, u32[]{:S(2)}) collective-permute-start(bf16[256,1024]{1,0:T(8,128)(2,1)S(1)} %broadcast_select_fusion), channel_id=1, source_target_pairs={{16,24},{20,28},{8,0},{12,4},{17,25},{21,29},{9,1},{13,5},{18,26},... | collective-permute-start | bytes 1572872 | tf_op jit(solution)/shard_map/ppermute | solution.py:384
  61.0 21.9 %collective-permute-start.5 = (bf16[256,1024]{1,0:T(8,128)(2,1)S(1)}, bf16[256,1024]{1,0:T(8,128)(2,1)S(1)}, u32[]{:S(2)}, u32[]{:S(2)}) collective-permute-start(bf16[256,1024]{1,0:T(8,128)(2,1)S(1)} %broadcast_select_fusion.1), channel_id=1, source_target_pairs={{16,24},{20,28},{8,0},{12,4},{17,25},{21,29},{9,1},{13,5},{18,26},... | collective-permute-start | bytes 1572872 | tf_op jit(solution)/shard_map/ppermute | solution.py:384
  112.8 15.5 %collective-permute-start.22 = (bf16[256,1024]{1,0:T(8,128)(2,1)}, bf16[256,1024]{1,0:T(8,128)(2,1)}, u32[]{:S(2)}, u32[]{:S(2)}) collective-permute-start(bf16[256,1024]{1,0:T(8,128)(2,1)} %get-tuple-element.38), channel_id=1, source_target_pairs={{0,8},{4,12},{24,16},{28,20},{1,9},{5,13},{25,17},{29,21},{2,10},{... | collective-permute-start | bytes 1572872 | tf_op jit(solution)/shard_map/ppermute | solution.py:384
  126.1 22.3 %collective-permute-start.25 = (bf16[512,1024]{1,0:T(8,128)(2,1)S(1)}, bf16[512,1024]{1,0:T(8,128)(2,1)}, u32[]{:S(2)}, u32[]{:S(2)}) collective-permute-start(bf16[512,1024]{1,0:T(8,128)(2,1)S(1)} %slice.143), channel_id=1, source_target_pairs={{0,4},{4,0},{8,12},{12,8},{16,20},{20,16},{24,28},{28,24},{1,5},{5... | collective-permute-start | bytes 3145736 | tf_op jit(solution)/shard_map/ppermute | solution.py:381
  130.9 21.8 %collective-permute-start.23 = (bf16[256,1024]{1,0:T(8,128)(2,1)S(1)}, bf16[256,1024]{1,0:T(8,128)(2,1)S(1)}, u32[]{:S(2)}, u32[]{:S(2)}) collective-permute-start(bf16[256,1024]{1,0:T(8,128)(2,1)S(1)} %fusion.3), channel_id=1, source_target_pairs={{0,8},{4,12},{8,16},{12,20},{1,9},{5,13},{9,17},{13,21},{2,10},{6,... | collective-permute-start | bytes 1572872 | tf_op jit(solution)/shard_map/ppermute | solution.py:384
  142.8 19.5 %collective-permute-start.32 = (bf16[256,1024]{1,0:T(8,128)(2,1)S(1)}, bf16[256,1024]{1,0:T(8,128)(2,1)S(1)}, u32[]{:S(2)}, u32[]{:S(2)}) collective-permute-start(bf16[256,1024]{1,0:T(8,128)(2,1)S(1)} %fusion.6), channel_id=1, source_target_pairs={{0,8},{4,12},{8,16},{12,20},{1,9},{5,13},{9,17},{13,21},{2,10},{6,... | collective-permute-start | bytes 1572872 | tf_op jit(solution)/shard_map/ppermute | solution.py:384
  147.8 16.5 %collective-permute-start.29 = (bf16[256,1024]{1,0:T(8,128)(2,1)S(1)}, bf16[256,1024]{1,0:T(8,128)(2,1)S(1)}, u32[]{:S(2)}, u32[]{:S(2)}) collective-permute-start(bf16[256,1024]{1,0:T(8,128)(2,1)S(1)} %fusion.3), channel_id=1, source_target_pairs={{16,8},{20,12},{24,16},{28,20},{17,9},{21,13},{25,17},{29,21},{18,... | collective-permute-start | bytes 1572872 | tf_op jit(solution)/shard_map/ppermute | solution.py:384
  150.2 24.9 %collective-permute-start.28 = (bf16[512,256]{1,0:T(8,128)(2,1)S(1)}, bf16[512,256]{1,0:T(8,128)(2,1)S(1)}, u32[]{:S(2)}, u32[]{:S(2)}) collective-permute-start(bf16[512,256]{1,0:T(8,128)(2,1)S(1)} %get-tuple-element.50), channel_id=1, source_target_pairs={{0,3},{1,2},{2,1},{3,0},{4,7},{5,6},{6,5},{7,4},{8,11},{9,10},{10,... | collective-permute-start | bytes 786440 | tf_op jit(solution)/shard_map/ppermute | solution.py:387
  152.7 22.5 %collective-permute-start.27 = (bf16[512,256]{1,0:T(8,128)(2,1)S(1)}, bf16[512,256]{1,0:T(8,128)(2,1)S(1)}, u32[]{:S(2)}, u32[]{:S(2)}) collective-permute-start(bf16[512,256]{1,0:T(8,128)(2,1)S(1)} %get-tuple-element.51), channel_id=1, source_target_pairs={{0,2},{1,3},{2,0},{3,1},{4,6},{5,7},{6,4},{7,5},{8,10},{9,11},{10,... | collective-permute-start | bytes 786440 | tf_op jit(solution)/shard_map/ppermute | solution.py:387
  154.0 21.3 %collective-permute-start.26 = (bf16[512,256]{1,0:T(8,128)(2,1)S(1)}, bf16[512,256]{1,0:T(8,128)(2,1)S(1)}, u32[]{:S(2)}, u32[]{:S(2)}) collective-permute-start(bf16[512,256]{1,0:T(8,128)(2,1)S(1)} %get-tuple-element.49), channel_id=1, source_target_pairs={{0,1},{1,0},{2,3},{3,2},{4,5},{5,4},{6,7},{7,6},{8,9},{9,8},{10,11... | collective-permute-start | bytes 786440 | tf_op jit(solution)/shard_map/ppermute | solution.py:387
  162.3 17.7 %collective-permute-start.35 = (bf16[256,1024]{1,0:T(8,128)(2,1)S(1)}, bf16[256,1024]{1,0:T(8,128)(2,1)S(1)}, u32[]{:S(2)}, u32[]{:S(2)}) collective-permute-start(bf16[256,1024]{1,0:T(8,128)(2,1)S(1)} %fusion.7), channel_id=1, source_target_pairs={{8,0},{12,4},{16,8},{20,12},{24,16},{28,20},{9,1},{13,5},{17,9},{2... | collective-permute-start | bytes 1572872 | tf_op jit(solution)/shard_map/ppermute | solution.py:384
  164.3 20.3 %collective-permute-start.33 = (bf16[256,1024]{1,0:T(8,128)(2,1)S(1)}, bf16[256,1024]{1,0:T(8,128)(2,1)S(1)}, u32[]{:S(2)}, u32[]{:S(2)}) collective-permute-start(bf16[256,1024]{1,0:T(8,128)(2,1)S(1)} %fusion.5), channel_id=1, source_target_pairs={{0,8},{4,12},{8,16},{12,20},{16,24},{20,28},{1,9},{5,13},{9,17},{1... | collective-permute-start | bytes 1572872 | tf_op jit(solution)/shard_map/ppermute | solution.py:384
  175.1 24.7 %collective-permute-start.19 = (f32[8,128]{1,0:T(8,128)S(1)}, f32[8,128]{1,0:T(8,128)S(1)}, u32[]{:S(2)}, u32[]{:S(2)}) collective-permute-start(f32[8,128]{1,0:T(8,128)S(1)} %get-tuple-element.42), channel_id=1, source_target_pairs={{0,8},{4,12},{8,16},{12,20},{16,24},{20,28},{24,0},{28,4},{1,9},{5... | collective-permute-start | bytes 12296 | tf_op jit(solution)/shard_map/ppermute | solution.py:384
  175.2 24.6 %collective-permute-start.20 = (f32[8,128]{1,0:T(8,128)S(1)}, f32[8,128]{1,0:T(8,128)S(1)}, u32[]{:S(2)}, u32[]{:S(2)}) collective-permute-start(f32[8,128]{1,0:T(8,128)S(1)} %get-tuple-element.42), channel_id=1, source_target_pairs={{0,16},{4,20},{8,24},{12,28},{16,0},{20,4},{24,8},{28,12},{1,17},{... | collective-permute-start | bytes 12296 | tf_op jit(solution)/shard_map/ppermute | solution.py:384
  175.3 24.5 %collective-permute-start.21 = (f32[8,128]{1,0:T(8,128)S(1)}, f32[8,128]{1,0:T(8,128)S(1)}, u32[]{:S(2)}, u32[]{:S(2)}) collective-permute-start(f32[8,128]{1,0:T(8,128)S(1)} %get-tuple-element.42), channel_id=1, source_target_pairs={{0,24},{4,28},{8,0},{12,4},{16,8},{20,12},{24,16},{28,20},{1,25},{... | collective-permute-start | bytes 12296 | tf_op jit(solution)/shard_map/ppermute | solution.py:384
  (36 other events, 316.7 us)

commit v4 on v3

v4 whole, which is shorter than its diff:
```python
import functools
import jax
import jax.numpy as jnp
from jax import lax
from jax.experimental import pallas as pl
from jax.experimental.pallas import tpu as pltpu
from jax.sharding import PartitionSpec as P


ce_weight = 0.5
PARTS = 2
f32, bf16 = jnp.float32, jnp.bfloat16


def dot(a, b):
    return lax.dot_general(a, b, (((1,), (0,)), ((), ())), preferred_element_type=f32)


def dot_nt(a, b):
    return lax.dot_general(a, b, (((1,), (1,)), ((), ())), preferred_element_type=f32)


def lanes(columns, like):
    lane = lax.broadcasted_iota(jnp.int32, like, 1)
    out = jnp.zeros(like, f32)
    for k, c in enumerate(columns):
        out = jnp.where(lane == k, c, out)
    return out


def cost(flops, size, trans=0):
    return pl.CostEstimate(flops=flops, bytes_accessed=size, transcendentals=trans)


WHOLE = pl.BlockSpec(memory_space=pltpu.VMEM)


def near(x):
    return pltpu.with_memory_space_constraint(x, pltpu.VMEM)


def out(shape, dtype):
    return pltpu.VMEM(shape, dtype)


def params(size):
    return pltpu.CompilerParams(vmem_limit_bytes=size << 20)


def target_kernel(own_tiles, core_ref, mine_ref, came_ref, id_ref, e_ref, stat_ref):
    step = pl.program_id(0)
    t = jnp.where(step < own_tiles, mine_ref[...], came_ref[...]).astype(f32)
    at = pl.ds(pl.multiple_of(step * t.shape[0], t.shape[0]), t.shape[0])
    top = jnp.max(t, axis=1, keepdims=True)
    e = jnp.exp(t - top)
    e_ref[at, :] = e.astype(bf16)
    total = jnp.sum(e, axis=1, keepdims=True)
    first = jnp.sum(e * t, axis=1, keepdims=True)
    ids = id_ref[...].astype(f32)
    stat_ref[at, :] = lanes([top, total, first, ids], (t.shape[0], 128))


def target_call(core, logits, came, ids, tile):
    rows, half = came.shape
    n, own_tiles = 2 * rows, rows // tile
    return pl.pallas_call(
        functools.partial(target_kernel, own_tiles),
        grid_spec=pltpu.PrefetchScalarGridSpec(
            num_scalar_prefetch=1,
            grid=(n // tile,),
            in_specs=[
                pl.BlockSpec((tile, half), lambda i, s: (jnp.minimum(i, own_tiles - 1), s[0])),
                pl.BlockSpec((tile, half), lambda i, s: (jnp.maximum(i - own_tiles, 0), 0)),
                pl.BlockSpec((tile, 1), lambda i, s: (i, 0)),
            ],
            out_specs=[WHOLE, WHOLE],
        ),
        out_shape=[out((n, half), bf16), out((n, 128), f32)],
        compiler_params=params(16),
        cost_estimate=cost(8 * n * half, 4 * n * half, n * half),
        name="target_exps",
    )(core, logits, came, ids)


def turn_kernel(tile, x_ref, out_ref):
    for k in range(x_ref.shape[0] // tile):
        at = slice(k * tile, (k + 1) * tile)
        out_ref[:, at] = x_ref[at, :].T


def turn_call(x, tile):
    n, dh = x.shape
    return pl.pallas_call(
        functools.partial(turn_kernel, tile),
        in_specs=[WHOLE],
        out_specs=WHOLE,
        out_shape=out((dh, n), bf16),
        compiler_params=params(8),
        cost_estimate=cost(0, 4 * n * dh),
        name="turn",
    )(near(x))


def choices(nz):
    unique, table = [("own", 0)], []
    for j in range(1, nz):
        table.append((("down", j), ("up", nz - j)))
        unique += [c for c in table[-1] if c not in unique]
    return unique, table


def gathered(up, down, p, nz, all_steps):
    unique, _ = choices(nz)
    pick = {"own": up, "up": up, "down": down}
    return [pick[k][p][j] for k, j in unique if all_steps or j < nz - 1]


def assemble(z, nz, refs, whole_ref, sem):
    unique, table = choices(nz)
    if len(refs) < len(unique):
        unique = [c for c in unique if c[1] < nz - 1]
    deep = refs[0].shape[0]

    def place(j):
        return pl.ds(pl.multiple_of(lax.rem(z + j, nz) * deep, deep), deep)

    def copy(k, j):
        return pltpu.make_async_copy(refs[k], whole_ref.at[place(j), :], sem.at[j])

    def each(do):
        do(0, 0)
        for j in range(1, nz):
            for choice, here in zip(table[j - 1], (z + j < nz, z + j >= nz)):

                @pl.when(here)
                def _(choice=choice, j=j):
                    if choice in unique:
                        do(unique.index(choice), j)
                    else:
                        do(None, j)

    def start(k, j):
        if k is None:
            whole_ref[place(j), :] = jnp.zeros((deep, whole_ref.shape[1]), bf16)
        else:
            copy(k, j).start()

    def wait(k, j):
        if k is not None:
            copy(k, j).wait()

    each(start)
    return lambda: each(wait)


def early_kernel(nz, count, z_ref, *refs):
    w_refs = refs[:count]
    h_ref, acc_ref, whole_ref, sem = refs[count:]

    @pl.when(pl.program_id(0) == 0)
    def _():
        assemble(z_ref[0], nz, w_refs, whole_ref, sem)()

    tile = h_ref.shape[0] // pl.num_programs(0)
    at = pl.ds(pl.multiple_of(pl.program_id(0) * tile, tile), tile)
    acc_ref[at, :] = dot(h_ref[at, :], whole_ref[...])


def early_call(nz, z, blocks, hid, tile):
    n, dh = hid.shape
    piece = blocks[0].shape[1]
    return pl.pallas_call(
        functools.partial(early_kernel, nz, len(blocks)),
        grid_spec=pltpu.PrefetchScalarGridSpec(
            num_scalar_prefetch=1,
            grid=(n // tile,),
            in_specs=[pl.BlockSpec(memory_space=pl.ANY)] * len(blocks) + [WHOLE],
            out_specs=WHOLE,
            scratch_shapes=[pltpu.VMEM((dh, piece), bf16), pltpu.SemaphoreType.DMA((nz,))],
        ),
        out_shape=out((n, piece), f32),
        compiler_params=params(10),
        cost_estimate=cost(2 * n * dh * piece, 6 * n * piece),
        name="early_draft",
    )(z, *blocks, near(hid))


def last_kernel(part, earlier, tile, at_ref, *refs):
    w_ref, acc_ref, h_ref, e_ref, t_ref = refs[:5]
    stat_refs = refs[5:5 + earlier]
    outs = refs[5 + earlier:]
    n, piece = acc_ref.shape
    deep = w_ref.shape[0]
    block = pl.ds(pl.multiple_of(at_ref[0] * deep, deep), deep)
    like = (tile, 128)
    for k in range(n // tile):
        at = slice(k * tile, (k + 1) * tile)
        z = acc_ref[at, :] + dot(h_ref[at, block], w_ref[...])
        top = jnp.max(z, axis=1, keepdims=True)
        e = jnp.exp(z - top)
        outs[0][at, :] = e.astype(bf16)
        total = jnp.sum(e, axis=1, keepdims=True)
        e_t = e_ref[at, part * piece:(part + 1) * piece].astype(f32)
        cross = jnp.sum(e_t * z, axis=1, keepdims=True)
        t_stat = t_ref[at, :]
        column = lax.broadcasted_iota(jnp.int32, z.shape, 1) + part * piece
        id_col = t_stat[:, 3:4].astype(jnp.int32)
        own = jnp.sum(jnp.where(column == id_col, z, 0.0), axis=1, keepdims=True)
        if part < PARTS - 1:
            outs[1][at, :] = lanes([top, total, cross, own], like)
            continue
        send_ref, turn_ref, tops_ref = outs[1:]
        stats = [r[at, :] for r in stat_refs]
        all_top = top
        for r in stats:
            all_top = jnp.maximum(all_top, r[:, 0:1])
        total = total * jnp.exp(top - all_top)
        for r in stats:
            total = total + r[:, 1:2] * jnp.exp(r[:, 0:1] - all_top)
            cross = cross + r[:, 2:3]
            own = own + r[:, 3:4]
        t_top, t_total, t_first = t_stat[:, 0:1], t_stat[:, 1:2], t_stat[:, 2:3]
        rows = lanes([t_top, t_total, t_first - cross, all_top, total, own], like).T[:8]
        send_ref[:, at] = rows
        turned = (k * tile + n // 2) % n
        turn_ref[:, turned:turned + tile] = rows
        tops = [r[:, 0:1] for r in stats] + [top]
        tops_ref[at, :] = lanes([t_top] + tops + [t_stat[:, 3:4]], like)


def last_call(part, at, w, acc, hid, e_t, t_stat, stats, tile):
    n, piece = acc.shape
    out_shape = [out((n, piece), bf16)]
    if part < PARTS - 1:
        stats = []
        out_shape += [out((n, 128), f32)]
    else:
        out_shape += [out((8, n), f32), out((8, n), f32), out((n, 128), f32)]
    return pl.pallas_call(
        functools.partial(last_kernel, part, len(stats), tile),
        grid_spec=pltpu.PrefetchScalarGridSpec(
            num_scalar_prefetch=1,
            grid=(1,),
            in_specs=[WHOLE] * (5 + len(stats)),
            out_specs=[WHOLE] * len(out_shape),
        ),
        out_shape=out_shape,
        compiler_params=params(10),
        cost_estimate=cost(2 * n * w.shape[0] * piece, 8 * n * piece, n * piece),
        name="last_draft",
    )(at, near(w), near(acc), near(hid), near(e_t), near(t_stat), *map(near, stats))


def hidden_kernel(nz, count, z_ref, *refs):
    slope_refs, w_refs = refs[:PARTS], refs[PARTS:PARTS + PARTS * count]
    out_ref, whole_ref, sem = refs[PARTS + PARTS * count:]

    @pl.when(pl.program_id(0) == 0)
    def _():
        waits = [
            assemble(z_ref[0], nz, w_refs[p * count:(p + 1) * count], whole_ref.at[p], sem.at[p])
            for p in range(PARTS)
        ]
        for wait in waits:
            wait()

    tile = out_ref.shape[0]
    at = pl.ds(pl.multiple_of(pl.program_id(0) * tile, tile), tile)
    acc = dot_nt(slope_refs[0][at, :], whole_ref[0])
    for p in range(1, PARTS):
        acc = acc + dot_nt(slope_refs[p][at, :], whole_ref[p])
    out_ref[...] = acc.astype(bf16)


def hidden_call(nz, z, slope, blocks, dh, tile):
    n, piece = slope[0].shape
    count = len(blocks[0])
    row = lambda i, s: (i, 0)
    return pl.pallas_call(
        functools.partial(hidden_kernel, nz, count),
        grid_spec=pltpu.PrefetchScalarGridSpec(
            num_scalar_prefetch=1,
            grid=(n // tile,),
            in_specs=[WHOLE] * PARTS
            + [pl.BlockSpec(memory_space=pl.ANY)] * (PARTS * count),
            out_specs=pl.BlockSpec((tile, dh), row),
            scratch_shapes=[
                pltpu.VMEM((PARTS, dh, piece), bf16),
                pltpu.SemaphoreType.DMA((PARTS, nz)),
            ],
        ),
        out_shape=jax.ShapeDtypeStruct((n, dh), bf16),
        compiler_params=params(16),
        cost_estimate=cost(2 * n * dh * piece * PARTS, 8 * n * piece),
        name="hidden_grad",
    )(z, *map(near, slope), *[b for bs in blocks for b in bs])


def fold_rows(a, b):
    t_top = jnp.maximum(a[0:1], b[0:1])
    fa, fb = jnp.exp(a[0:1] - t_top), jnp.exp(b[0:1] - t_top)
    z_top = jnp.maximum(a[3:4], b[3:4])
    ga, gb = jnp.exp(a[3:4] - z_top), jnp.exp(b[3:4] - z_top)
    rows = [
        t_top,
        a[1:2] * fa + b[1:2] * fb,
        a[2:3] * fa + b[2:3] * fb,
        z_top,
        a[4:5] * ga + b[4:5] * gb,
        a[5:6] + b[5:6],
    ]
    return jnp.concatenate(rows + [a[6:8]])


def fold_kernel(*refs):
    got = [r[...] for r in refs[:-1]]
    while len(got) > 1:
        got = [fold_rows(got[j], got[j + 1]) for j in range(0, len(got), 2)]
    refs[-1][...] = got[0]


def fold_call(rows):
    return pl.pallas_call(
        fold_kernel,
        in_specs=[WHOLE] * len(rows),
        out_specs=WHOLE,
        out_shape=out(rows[0].shape, f32),
        compiler_params=params(4),
        name="fold",
    )(*map(near, rows))


def slope_kernel(part, peers, idx_ref, *refs):
    step = pl.program_id(0)
    if peers:
        tops_ref = refs[peers]
        ez_ref, et_ref, ht_ref = refs[peers + 1:peers + 4]
        slope_ref, msg_ref, coef_ref, loss_ref = refs[peers + 4:]

        @pl.when(step == 0)
        def _():
            got = [r[...] for r in refs[:peers]]
            while len(got) > 1:
                got = [fold_rows(got[j], got[j + 1]) for j in range(0, len(got), 2)]
            s = got[0]
            t_inv = 1.0 / s[1:2]
            lse_t = s[0:1] + jnp.log(s[1:2])
            lse_z = s[3:4] + jnp.log(s[4:5])
            n = s.shape[1]
            per_token = s[2:3] * t_inv - lse_t + (1.0 + ce_weight) * lse_z - ce_weight * s[5:6]
            plane = jnp.sum(per_token[:, :n // 2], axis=1, keepdims=True) + jnp.sum(
                per_token[:, n // 2:], axis=1, keepdims=True
            )
            loss_ref[...] = jnp.broadcast_to(plane, loss_ref.shape)
            z_inv = (1.0 + ce_weight) / s[4:5]
            flat = jnp.concatenate([s[0:1], t_inv, s[3:4], z_inv, jnp.zeros((124, n), f32)]).T
            tops = tops_ref[...]
            lane = lax.broadcasted_iota(jnp.int32, tops.shape, 1)
            base = jnp.where(lane == 0, flat[:, 0:1], flat[:, 2:3])
            gain = jnp.where(lane == 0, flat[:, 1:2], flat[:, 3:4])
            coef_ref[...] = jnp.where(lane <= PARTS, jnp.exp(tops - base) * gain, tops)

    else:
        coef_ref, ez_ref, et_ref, ht_ref, slope_ref, msg_ref = refs
    b = coef_ref[:, 0:1]
    a = coef_ref[:, part + 1:part + 2]
    piece = ez_ref.shape[1]
    tile = piece // pl.num_programs(0)
    first = pl.multiple_of(step * tile, tile)
    at = pl.ds(first, tile)
    e_t = et_ref[:, pl.ds(pl.multiple_of(part * piece + first, tile), tile)]
    value = ez_ref[:, at].astype(f32) * a - e_t.astype(f32) * b
    column = lax.broadcasted_iota(jnp.int32, value.shape, 1)
    id_col = coef_ref[:, PARTS + 1:PARTS + 2].astype(jnp.int32) - (part * piece + first)
    value = jnp.where(column == id_col, value - ce_weight, value)
    slope = value.astype(bf16)
    slope_ref[:, at] = slope
    deep = msg_ref.shape[0]
    rows = pl.ds(pl.multiple_of(idx_ref[0] * deep, deep), deep)
    msg_ref[...] = dot(ht_ref[rows, :], slope).astype(bf16)


def slope_call(part, index, head_args, e_z, e_t, hid_t, deep, tile):
    n, piece = e_z.shape
    peers = len(head_args) - 1
    out_specs = [WHOLE, pl.BlockSpec((deep, tile), lambda i, s: (0, i))]
    out_shape = [out((n, piece), bf16), jax.ShapeDtypeStruct((deep, piece), bf16)]
    if peers:
        out_specs += [WHOLE, WHOLE]
        out_shape += [out((n, 128), f32), out((8, 128), f32)]
    args = [*head_args, e_z, e_t, hid_t]
    return pl.pallas_call(
        functools.partial(slope_kernel, part, peers),
        grid_spec=pltpu.PrefetchScalarGridSpec(
            num_scalar_prefetch=1,
            grid=(piece // tile,),
            in_specs=[WHOLE] * len(args),
            out_specs=out_specs,
        ),
        out_shape=out_shape,
        compiler_params=params(16),
        cost_estimate=cost(2 * n * deep * piece, 6 * n * piece),
        name="slope",
    )(index, *map(near, args))


def loss_kernel(scale, z_ref, *refs):
    planes, out_ref = [r[...] for r in refs[:-1]], refs[-1]
    nz = len(planes)
    total = jnp.zeros(out_ref.shape, f32)
    for chip in range(nz):
        k = lax.rem(z_ref[0] - chip + nz, nz)
        term = planes[0]
        for j in range(1, nz):
            term = jnp.where(k == j, planes[j], term)
        total = total + term
    out_ref[...] = total * scale


def loss_call(z, planes, scale):
    return pl.pallas_call(
        functools.partial(loss_kernel, scale),
        grid_spec=pltpu.PrefetchScalarGridSpec(
            num_scalar_prefetch=1,
            grid=(1,),
            in_specs=[WHOLE] * len(planes),
            out_specs=WHOLE,
        ),
        out_shape=jax.ShapeDtypeStruct(planes[0].shape, f32),
        compiler_params=params(4),
        name="loss_sum",
    )(z, *planes)


def body(n_tok, n_voc, hidden, head, logits, ids):
    nz = n_tok // 2
    rows, dh = hidden.shape
    own_rows, share = head.shape
    half = share // 2
    piece = half // PARTS
    deep = 2 * own_rows
    tile = min(256, rows)
    wide = min(512, piece)
    me = lax.axis_index("tok")
    core = lax.rem(me, 2)
    z = lax.div(me, 2)
    voc = lax.axis_index("voc")
    width = dh // n_voc

    def first_row(s):
        return jnp.where(z < s, jnp.minimum(z + nz - s, nz - 1), jnp.maximum(z - nz + s, 0))

    def scalar(x):
        return jnp.reshape(x, (1,)).astype(jnp.int32)

    even = core == 0
    above = [z >= s for s in range(nz)]
    ahead = {
        "core": scalar(core),
        "z": scalar(z),
        "last": scalar(jnp.where(z == 0, nz - 1, 0)),
        "first": scalar(first_row(1)),
    }
    row_of = {("own", 0): z * deep}
    for s in range(1, nz):
        if 2 * s <= nz:
            row_of["first", s] = first_row(s) * deep
        row_of["up", s] = jnp.minimum(z + nz - s, nz - 1) * deep
        row_of["down", s] = jnp.maximum(z - nz + s, 0) * deep
    col_of = [(voc ^ v) * width for v in range(n_voc)]
    vocab_start = voc * share + core * half
    (even, above, ahead, row_of, col_of, vocab_start), head, hidden, logits, ids = (
        lax.optimization_barrier(
            ((even, above, ahead, row_of, col_of, vocab_start), head, hidden, logits, ids)
        )
    )

    def swap(x):
        return lax.ppermute(x, "tok", [(i, i ^ 1) for i in range(n_tok)])

    def hop(x, pairs):
        return lax.ppermute(x, "tok", [(2 * a + k, 2 * b + k) for a, b in pairs for k in range(2)])

    def plane_swap(x, v):
        return lax.ppermute(x, "voc", [(w, w ^ v) for w in range(n_voc)])

    def mine(x, other=False):
        left, right = x[:, :half], x[:, half:]
        return jnp.where(even, right, left) if other else jnp.where(even, left, right)

    keep, send = mine(head), mine(head, True)
    blocks = []
    for p in range(PARTS):
        cut = slice(p * piece, (p + 1) * piece)
        other = swap(send[:, cut])
        blocks.append(
            jnp.where(
                even,
                jnp.concatenate([keep[:, cut], other]),
                jnp.concatenate([other, keep[:, cut]]),
            )
        )

    up = [[b] for b in blocks]
    down = [[b] for b in blocks]
    for s in range(1, nz):
        up_pairs = [(a, a + 1) for a in range(s - 1, nz - 1)]
        down_pairs = [(a, a - 1) for a in range(1, nz - s + 1)]
        for p in range(PARTS):
            u, d = up[p][-1], down[p][-1]
            if 2 * s > nz + 1:
                both = hop(jnp.where(above[s - 1], u, d), up_pairs + down_pairs)
                up[p].append(both)
                down[p].append(both)
            else:
                up[p].append(hop(u, up_pairs))
                down[p].append(hop(d, down_pairs))

    hid = jnp.concatenate([hidden, swap(hidden)])
    hid_t = turn_call(hid, tile)
    tgt = mine(logits, True)
    tgt = swap(tgt)
    local = jnp.concatenate([ids, swap(ids)]) - vocab_start
    e_t, t_stat = target_call(ahead["core"], logits, tgt, local[:, None], tile)

    stats, e_z = [], []
    whole = [gathered(up, down, p, nz, True) for p in range(PARTS)]
    for p in range(PARTS):
        acc = early_call(nz, ahead["z"], gathered(up, down, p, nz, False), hid, tile)
        final_u, final_d = up[p][-1], down[p][-1]
        w = final_u if final_u is final_d else jnp.where(above[nz - 1], final_u, final_d)
        outs = last_call(p, ahead["last"], w, acc, hid, e_t, t_stat, stats, tile)
        e_z.append(outs[0])
        if p < PARTS - 1:
            stats.append(outs[1])
    mine_rows, turned, tops = outs[1:]

    x = fold_call([mine_rows, swap(turned)])
    bits = n_voc.bit_length() - 1
    done = 0
    while True:
        few = min(2, bits - done)
        got = [x] + [plane_swap(x, v << done) for v in range(1, 1 << few)]
        done += few
        if done >= bits:
            break
        x = fold_call(got)

    msgs, slope = [], []
    for p in range(PARTS):
        head_args = got + [tops] if p == 0 else [coef]
        outs = slope_call(
            p, ahead["first"], head_args, e_z[p], e_t, hid_t, deep, wide
        )
        slope.append(outs[0])
        msgs.append(outs[1])
        if p == 0:
            coef, plane = outs[2:]

    def cut(x, row, col, shape):
        row, col = (jnp.asarray(i, jnp.int32) for i in (row, col))
        return lax.dynamic_slice(x, (row, col), shape, allow_negative_indices=False)

    def grad_rows(way, s, p):
        return dot(cut(hid_t, row_of[way, s], 0, (deep, 2 * rows)), slope[p])

    got_up, got_down = [None] * PARTS, [None] * PARTS
    for s in range(1, nz):
        up_pairs = [(a, a + 1) for a in range(0, s)]
        down_pairs = [(a, a - 1) for a in range(nz - s, nz)]
        for p in range(PARTS):
            if 2 * s <= nz:
                if s == 1:
                    msg = msgs[p]
                else:
                    msg = grad_rows("first", s, p) + got_up[p].astype(f32)
                    if got_down[p] is not got_up[p]:
                        msg = msg + got_down[p].astype(f32)
                    msg = msg.astype(bf16)
                if 2 * s < nz - 1:
                    got_up[p] = got_down[p] = hop(msg, up_pairs + down_pairs)
                else:
                    got_up[p] = hop(msg, up_pairs)
                    got_down[p] = hop(msg, down_pairs)
            else:
                msg_up = grad_rows("up", s, p) + got_up[p].astype(f32)
                msg_down = grad_rows("down", s, p) + got_down[p].astype(f32)
                got_up[p] = hop(msg_up.astype(bf16), up_pairs)
                got_down[p] = hop(msg_down.astype(bf16), down_pairs)
    keeps, gives = [], []
    for p in range(PARTS):
        full = grad_rows("own", 0, p) + got_up[p].astype(f32) + got_down[p].astype(f32)
        low, high = full[:own_rows], full[own_rows:]
        keeps.append(jnp.where(even, low, high))
        give = jnp.where(even, high, low).astype(bf16)
        gives.append(swap(give).astype(f32))
    grad_head = jnp.where(
        even,
        jnp.concatenate(keeps + gives, axis=1),
        jnp.concatenate(gives + keeps, axis=1),
    )

    late, plane, _ = lax.optimization_barrier((slope, plane, msgs[-1]))
    planes = [hop(plane, [(a, (a + k) % nz) for a in range(nz)]) for k in range(1, nz)]
    loss = loss_call(ahead["z"], [plane] + planes, 1.0 / (rows * n_tok))[0, 0]

    part = hidden_call(nz, ahead["z"], late, whole, dh, tile)
    part = part[:rows].astype(f32) + swap(part[rows:]).astype(f32)

    def wide_slice(v):
        return cut(part, 0, col_of[v], (rows, width))

    grad_hidden = wide_slice(0)
    for v in range(1, n_voc):
        came = plane_swap(wide_slice(v).astype(bf16), v)
        grad_hidden = grad_hidden + came.astype(f32)
    return loss, grad_hidden, grad_head


def solution(mesh):
    placed = (P("tok", None), P("tok", "voc"), P("tok", "voc"), P("tok"))
    n_tok, n_voc = mesh.shape["tok"], mesh.shape["voc"]
    return jax.shard_map(
        functools.partial(body, n_tok, n_voc),
        mesh=mesh,
        in_specs=placed,
        out_specs=(P(), P("tok", "voc"), P("tok", "voc")),
        check_vma=False,
    )
```

time: 210 us -> 192 us (0.914)
  waiting for transfers between devices: 63.8 us -> 85.4 us
  Pallas kernels: 47.3 us -> 34.3 us
  starting transfers between devices: 63.9 us -> 51.5 us
  local copies, waits for them, and re-layouts: 10.1 us -> 4.61 us
  other arithmetic: 11.7 us -> 8.56 us
  matrix products: 8.69 us -> 5.8 us
    ppermute x23, waiting for transfers between devices: 60.2 us -> 74.1 us  [hop(): lax.ppermute(x, 'tok', [(2 * a + k, 2 * b + k) for a, b in pairs for k in...]
    ppermute x23, starting transfers between devices: 54.9 us -> 44.9 us  [hop(): lax.ppermute(x, 'tok', [(2 * a + k, 2 * b + k) for a, b in pairs for k in...]
    pallas_call x2, Pallas kernels: 10.8 us -> 5.68 us  [slope_call(): pl.pallas_call(functools.partial(slope_kernel, part, peers), grid_spec=pl...]
    pallas_call x3 -> x7, Pallas kernels: 21.3 us -> 16.8 us  [the longest x2 8.35 us: early_call(): pl.pallas_call(functools.partial(early_kernel, nz, len(blocks)), grid_spe...]
    ppermute x9, waiting for transfers between devices: 3.43 us -> 7.57 us  [swap(): return lax.ppermute(x, 'tok', [(i, i ^ 1) for i in range(n_tok)])]
    ppermute x6, waiting for transfers between devices: 0.07 us -> 3.69 us  [plane_swap(): return lax.ppermute(x, 'voc', [(w, w ^ v) for w in range(n_voc)])]
    reduce_sum x1 -> x0, other arithmetic: 3.13 us -> none  [body(): loss = jnp.sum(every) / (rows * n_tok)]
    dot_general x8, matrix products: 8.69 us -> 5.8 us  [dot(): lax.dot_general(a, b, (((1,), (0,)), ((), ())), preferred_element_type=f32)]
  transfers between devices with their start and end apart: 38 -> 38, of which waited for: 15 -> 20; matrix products, arithmetic and copies ran while one was open for 12% -> 8% of each run, Pallas kernels for 13% -> 13%
where the time goes in v4:
time: 192 us; the launch traced here: 191 us
  waiting for transfers between devices  85.4 us (44%)
  starting transfers between devices  51.5 us (27%)
  Pallas kernels  34.3 us (18%)
  other arithmetic  8.56 us (4%)
  matrix products  5.8 us (3%)
  local copies, waits for them, and re-layouts  4.61 us (2%)
    ppermute x23, waiting for transfers between devices, hop(): lax.ppermute(x, 'tok', [(2 * a + k, 2 * b + k) for a, b in pairs for k in...  74.1 us
    ppermute x23, starting transfers between devices, hop(): lax.ppermute(x, 'tok', [(2 * a + k, 2 * b + k) for a, b in pairs for k in...  44.9 us
    pallas_call x2, Pallas kernels, early_call(): pl.pallas_call(functools.partial(early_kernel, nz, len(blocks)), grid_spe...  8.35 us
    pallas_call x2, Pallas kernels, last_call(): pl.pallas_call(functools.partial(last_kernel, part, len(stats), tile), gr...  7.78 us
    ppermute x9, waiting for transfers between devices, swap(): return lax.ppermute(x, 'tok', [(i, i ^ 1) for i in range(n_tok)])  7.57 us
    pallas_call x1, Pallas kernels, hidden_call(): pl.pallas_call(functools.partial(hidden_kernel, nz, count), grid_spec=plt...  6.72 us
    dot_general x8, matrix products, dot(): lax.dot_general(a, b, (((1,), (0,)), ((), ())), preferred_element_type=f32)  5.8 us
    pallas_call x2, Pallas kernels, slope_call(): pl.pallas_call(functools.partial(slope_kernel, part, peers), grid_spec=pl...  5.68 us
  transfers between devices with their start and end apart: 38, of which 20 were waited for; matrix products, arithmetic and copies ran while one was open for 8% of the time, Pallas kernels for 13%

profile of v4, /device:TPU:0, one launch (start us, length us, event | category | flops | bytes accessed | tf_op | source)
XLA Modules:
  0.0 191.4 jit_solution(4649699536826160365)
XLA Ops:
  3.9 4.9 %collective-permute-start.10 = (bf16[256,1024]{1,0:T(8,128)(2,1)S(1)}, bf16[256,1024]{1,0:T(8,128)(2,1)S(1)}, u32[]{:S(2)}, u32[]{:S(2)}) collective-permute-start(bf16[256,1024]{1,0:T(8,128)(2,1)S(1)} %maximum_select_fusion.2.refs_0_.refs_2_), channel_id=1, source_target_pairs={{0,8},{4,12},{8,16},{12,20},{16,24},{20,28},{1,9},{5,13},{9,17},{1... | collective-permute-start | bytes 1572872 | tf_op jit(solution)/shard_map/ppermute | solution.py:482
  10.2 5.5 %collective-permute-start.1 = (bf16[256,1024]{1,0:T(8,128)(2,1)S(1)}, bf16[256,1024]{1,0:T(8,128)(2,1)}, u32[]{:S(2)}, u32[]{:S(2)}) collective-permute-start(bf16[256,1024]{1,0:T(8,128)(2,1)S(1)} %maximum_select_fusion.1.refs_0_.refs_9_), channel_id=1, source_target_pairs={{0,8},{4,12},{8,16},{12,20},{16,24},{20,28},{1,9},{5,13},{9,17},{1... | collective-permute-start | bytes 1572872 | tf_op jit(solution)/shard_map/ppermute | solution.py:482
  17.8 4.0 %collective-permute-done.8 = s32[512]{0:T(512)S(1)} collective-permute-done((s32[512]{0:T(512)S(1)}, s32[512]{0:T(512)S(1)}, u32[]{:S(2)}, u32[]{:S(2)}) %collective-permute-start.8) | collective-permute-done | bytes 2080 | tf_op jit(solution)/shard_map/ppermute | solution.py:479
  25.7 5.7 %collective-permute-done.1.refs_4_.refs_15_ = bf16[256,1024]{1,0:T(8,128)(2,1)} collective-permute-done((bf16[256,1024]{1,0:T(8,128)(2,1)S(1)}, bf16[256,1024]{1,0:T(8,128)(2,1)}, u32[]{:S(2)}, u32[]{:S(2)}) %collective-permute-start.1) | collective-permute-done | bytes 524320 | tf_op jit(solution)/shard_map/ppermute | solution.py:482
  32.7 5.8 %collective-permute-done.3.refs_1_.refs_10_ = bf16[256,1024]{1,0:T(8,128)(2,1)} collective-permute-done((bf16[256,1024]{1,0:T(8,128)(2,1)S(1)}, bf16[256,1024]{1,0:T(8,128)(2,1)}, u32[]{:S(2)}, u32[]{:S(2)}) %collective-permute-start.3) | collective-permute-done | bytes 524320 | tf_op jit(solution)/shard_map/ppermute | solution.py:482
  43.4 6.3 %collective-permute-done.13.refs_2_.refs_5_ = bf16[256,1024]{1,0:T(8,128)(2,1)S(1)} collective-permute-done((bf16[256,1024]{1,0:T(8,128)(2,1)}, bf16[256,1024]{1,0:T(8,128)(2,1)S(1)}, u32[]{:S(2)}, u32[]{:S(2)}) %collective-permute-start.13) | collective-permute-done | bytes 524320 | tf_op jit(solution)/shard_map/ppermute | solution.py:482
  51.2 9.8 %collective-permute-done.4.refs_2_.refs_12_ = bf16[256,1024]{1,0:T(8,128)(2,1)} collective-permute-done((bf16[256,1024]{1,0:T(8,128)(2,1)}, bf16[256,1024]{1,0:T(8,128)(2,1)}, u32[]{:S(2)}, u32[]{:S(2)}) %collective-permute-start.4) | collective-permute-done | bytes 524320 | tf_op jit(solution)/shard_map/ppermute | solution.py:482
  64.9 4.0 %early_draft.3.refs_1_ = f32[1024,1024]{1,0:T(8,128)S(1)} custom-call(s32[1]{0:T(128)} %bitcast.3.z_ref, bf16[256,1024]{1,0:T(8,128)(2,1)S(1)} %copy-done.3, bf16[256,1024]{1,0:T(8,128)(2,1)} %collective-permute-done.12.refs_1_.refs_3_, bf16[256,1024]{1,0:T(8,128)(2,1)S(1)} %collective-permute-done.13.refs_2_.refs_5_, ...), custom_call_target="tpu_custom_call" | custom-call | flops 2147483648 | bytes 6291456 | tf_op jit(solution)/shard_map/early_draft/pallas_call | solution.py:172
  69.0 4.3 %early_draft.2.refs_1_ = f32[1024,1024]{1,0:T(8,128)S(1)} custom-call(s32[1]{0:T(128)} %bitcast.3.z_ref, bf16[256,1024]{1,0:T(8,128)(2,1)S(1)} %copy-done.5, bf16[256,1024]{1,0:T(8,128)(2,1)} %collective-permute-done.3.refs_1_.refs_10_, bf16[256,1024]{1,0:T(8,128)(2,1)} %collective-permute-done.4.refs_2_.refs_12_, ...), custom_call_target="tpu_custom_call" | custom-call | flops 2147483648 | bytes 6291456 | tf_op jit(solution)/shard_map/early_draft/pallas_call | solution.py:172
  73.3 5.0 %target_exps.1 = (bf16[1024,2048]{1,0:T(8,128)(2,1)S(1)}, f32[1024,128]{1,0:T(8,128)S(1)}) custom-call(s32[1]{0:T(128)} %bitcast.core_ref, bf16[512,4096]{1,0:T(8,128)(2,1)S(1)} %copy-done.1, bf16[512,2048]{1,0:T(8,128)(2,1)} %collective-permute-done.7.came_ref, s32[1024,1]{1,0:T(8,128)S(1)} %broadcast_subtract_fusion.id_ref), custom_call_target="tpu_custom_call" | custom-call | flops 16777216 | bytes 8388608 | tf_op jit(solution)/shard_map/target_exps/pallas_call | solution.py:66
  82.5 5.3 %last_draft.3 = (bf16[1024,1024]{1,0:T(8,128)(2,1)S(1)}, f32[8,1024]{1,0:T(8,128)S(1)}, f32[8,1024]{1,0:T(8,128)S(1)}, f32[1024,128]{1,0:T(8,128)S(1)}) custom-call(s32[1]{0:T(128)} %bitcast.2.at_ref, bf16[256,1024]{1,0:T(8,128)(2,1)S(1)} %collective-permute-done.5.refs_0_.refs_11_.refs_14_, f32[1024,1024]{1,0:T(8,128)S(1)} %early_draft.2.refs_1_, ...), custom_call_target="tpu_custom_call" | custom-call | flops 536870912 | bytes 8388608 | tf_op jit(solution)/shard_map/last_draft/pallas_call | solution.py:239
  97.1 3.3 %slope.2 = (bf16[1024,1024]{1,0:T(8,128)(2,1)S(1)}, bf16[256,1024]{1,0:T(8,128)(2,1)S(1)}, f32[1024,128]{1,0:T(8,128)S(1)}, f32[8,128]{1,0:T(8,128)S(1)}) custom-call(s32[1]{0:T(128)} %bitcast.1.idx_ref, f32[8,1024]{1,0:T(8,128)S(1)} %fold.1.refs_0_, f32[8,1024]{1,0:T(8,128)S(1)} %collective-permute-done.16.refs_1_, ...), custom_call_target="tpu_custom_call" | custom-call | flops 536870912 | bytes 6291456 | tf_op jit(solution)/shard_map/slope/pallas_call | solution.py:392
  100.3 3.3 %collective-permute-start.26 = (bf16[256,1024]{1,0:T(8,128)(2,1)S(1)}, bf16[256,1024]{1,0:T(8,128)(2,1)S(1)}, u32[]{:S(2)}, u32[]{:S(2)}) collective-permute-start(bf16[256,1024]{1,0:T(8,128)(2,1)S(1)} %get-tuple-element.73), channel_id=1, source_target_pairs={{0,8},{4,12},{24,16},{28,20},{1,9},{5,13},{25,17},{29,21},{2,10},{... | collective-permute-start | bytes 1572872 | tf_op jit(solution)/shard_map/ppermute | solution.py:482
  106.1 6.7 %hidden_grad.1 = bf16[1024,1024]{1,0:T(8,128)(2,1)S(1)} custom-call(s32[1]{0:T(128)} %bitcast.3.z_ref, bf16[1024,1024]{1,0:T(8,128)(2,1)S(1)} %get-tuple-element.64.refs_0_, bf16[1024,1024]{1,0:T(8,128)(2,1)S(1)} %get-tuple-element.65.refs_1_, bf16[256,1024]{1,0:T(8,128)(2,1)S(1)} %copy-done.3, bf16[256,1024]{1,0:T(8,128)(2,1)} %collective-permute-done.12.refs_1_.refs_3_, ...), custom_call_target="tpu_custom_call" | custom-call | flops 4294967296 | bytes 8388608 | tf_op jit(solution)/shard_map/hidden_grad/pallas_call | solution.py:279
  114.5 11.9 %collective-permute-done.19.refs_1_ = f32[8,128]{1,0:T(8,128)S(1)} collective-permute-done((f32[8,128]{1,0:T(8,128)S(1)}, f32[8,128]{1,0:T(8,128)S(1)}, u32[]{:S(2)}, u32[]{:S(2)}) %collective-permute-start.19) | collective-permute-done | bytes 4128 | tf_op jit(solution)/shard_map/ppermute | solution.py:482
  126.5 4.0 %collective-permute-done.21.refs_3_ = f32[8,128]{1,0:T(8,128)S(1)} collective-permute-done((f32[8,128]{1,0:T(8,128)S(1)}, f32[8,128]{1,0:T(8,128)S(1)}, u32[]{:S(2)}, u32[]{:S(2)}) %collective-permute-start.21) | collective-permute-done | bytes 4128 | tf_op jit(solution)/shard_map/ppermute | solution.py:482
  131.8 4.0 %collective-permute-start.27 = (bf16[256,1024]{1,0:T(8,128)(2,1)S(1)}, bf16[256,1024]{1,0:T(8,128)(2,1)S(1)}, u32[]{:S(2)}, u32[]{:S(2)}) collective-permute-start(bf16[256,1024]{1,0:T(8,128)(2,1)S(1)} %fusion.3), channel_id=1, source_target_pairs={{0,8},{4,12},{8,16},{12,20},{1,9},{5,13},{9,17},{13,21},{2,10},{6,... | collective-permute-start | bytes 1572872 | tf_op jit(solution)/shard_map/ppermute | solution.py:482
  141.8 6.3 %collective-permute-done.27 = bf16[256,1024]{1,0:T(8,128)(2,1)S(1)} collective-permute-done((bf16[256,1024]{1,0:T(8,128)(2,1)S(1)}, bf16[256,1024]{1,0:T(8,128)(2,1)S(1)}, u32[]{:S(2)}, u32[]{:S(2)}) %collective-permute-start.27) | collective-permute-done | bytes 524320 | tf_op jit(solution)/shard_map/ppermute | solution.py:482
  149.3 7.6 %collective-permute-done.32 = bf16[256,1024]{1,0:T(8,128)(2,1)S(1)} collective-permute-done((bf16[256,1024]{1,0:T(8,128)(2,1)S(1)}, bf16[256,1024]{1,0:T(8,128)(2,1)S(1)}, u32[]{:S(2)}, u32[]{:S(2)}) %collective-permute-start.32) | collective-permute-done | bytes 524320 | tf_op jit(solution)/shard_map/ppermute | solution.py:482
  158.1 4.4 %collective-permute-start.28 = (bf16[256,1024]{1,0:T(8,128)(2,1)S(1)}, bf16[256,1024]{1,0:T(8,128)(2,1)S(1)}, u32[]{:S(2)}, u32[]{:S(2)}) collective-permute-start(bf16[256,1024]{1,0:T(8,128)(2,1)S(1)} %fusion.2), channel_id=1, source_target_pairs={{0,8},{4,12},{8,16},{12,20},{16,24},{20,28},{1,9},{5,13},{9,17},{1... | collective-permute-start | bytes 1572872 | tf_op jit(solution)/shard_map/ppermute | solution.py:482
  165.3 4.6 %collective-permute-start.33 = (bf16[256,1024]{1,0:T(8,128)(2,1)S(1)}, bf16[256,1024]{1,0:T(8,128)(2,1)S(1)}, u32[]{:S(2)}, u32[]{:S(2)}) collective-permute-start(bf16[256,1024]{1,0:T(8,128)(2,1)S(1)} %fusion.5), channel_id=1, source_target_pairs={{0,8},{4,12},{8,16},{12,20},{16,24},{20,28},{1,9},{5,13},{9,17},{1... | collective-permute-start | bytes 1572872 | tf_op jit(solution)/shard_map/ppermute | solution.py:482
  172.3 2.5 %collective-permute-done.28 = bf16[256,1024]{1,0:T(8,128)(2,1)S(1)} collective-permute-done((bf16[256,1024]{1,0:T(8,128)(2,1)S(1)}, bf16[256,1024]{1,0:T(8,128)(2,1)S(1)}, u32[]{:S(2)}, u32[]{:S(2)}) %collective-permute-start.28) | collective-permute-done | bytes 524320 | tf_op jit(solution)/shard_map/ppermute | solution.py:482
  174.8 5.2 %collective-permute-done.30 = bf16[256,1024]{1,0:T(8,128)(2,1)S(1)} collective-permute-done((bf16[256,1024]{1,0:T(8,128)(2,1)S(1)}, bf16[256,1024]{1,0:T(8,128)(2,1)S(1)}, u32[]{:S(2)}, u32[]{:S(2)}) %collective-permute-start.30) | collective-permute-done | bytes 524320 | tf_op jit(solution)/shard_map/ppermute | solution.py:482
  182.5 4.9 %collective-permute-done.35 = bf16[256,1024]{1,0:T(8,128)(2,1)S(1)} collective-permute-done((bf16[256,1024]{1,0:T(8,128)(2,1)S(1)}, bf16[256,1024]{1,0:T(8,128)(2,1)S(1)}, u32[]{:S(2)}, u32[]{:S(2)}) %collective-permute-start.35) | collective-permute-done | bytes 524320 | tf_op jit(solution)/shard_map/ppermute | solution.py:482
  (114 shorter events, 60.8 us)
Async XLA Ops:
  3.9 19.2 %collective-permute-start.10 = (bf16[256,1024]{1,0:T(8,128)(2,1)S(1)}, bf16[256,1024]{1,0:T(8,128)(2,1)S(1)}, u32[]{:S(2)}, u32[]{:S(2)}) collective-permute-start(bf16[256,1024]{1,0:T(8,128)(2,1)S(1)} %maximum_select_fusion.2.refs_0_.refs_2_), channel_id=1, source_target_pairs={{0,8},{4,12},{8,16},{12,20},{16,24},{20,28},{1,9},{5,13},{9,17},{1... | collective-permute-start | bytes 1572872 | tf_op jit(solution)/shard_map/ppermute | solution.py:482
  8.8 15.7 %collective-permute-start.12 = (bf16[256,1024]{1,0:T(8,128)(2,1)S(1)}, bf16[256,1024]{1,0:T(8,128)(2,1)}, u32[]{:S(2)}, u32[]{:S(2)}) collective-permute-start(bf16[256,1024]{1,0:T(8,128)(2,1)S(1)} %maximum_select_fusion.2.refs_0_.refs_2_), channel_id=1, source_target_pairs={{8,0},{12,4},{16,8},{20,12},{24,16},{28,20},{9,1},{13,5},{17,9},{2... | collective-permute-start | bytes 1572872 | tf_op jit(solution)/shard_map/ppermute | solution.py:482
  10.2 21.2 %collective-permute-start.1 = (bf16[256,1024]{1,0:T(8,128)(2,1)S(1)}, bf16[256,1024]{1,0:T(8,128)(2,1)}, u32[]{:S(2)}, u32[]{:S(2)}) collective-permute-start(bf16[256,1024]{1,0:T(8,128)(2,1)S(1)} %maximum_select_fusion.1.refs_0_.refs_9_), channel_id=1, source_target_pairs={{0,8},{4,12},{8,16},{12,20},{16,24},{20,28},{1,9},{5,13},{9,17},{1... | collective-permute-start | bytes 1572872 | tf_op jit(solution)/shard_map/ppermute | solution.py:482
  17.2 56.1 %collective-permute-start.7 = (bf16[512,2048]{1,0:T(8,128)(2,1)}, bf16[512,2048]{1,0:T(8,128)(2,1)}, u32[]{:S(2)}, u32[]{:S(2)}) collective-permute-start(bf16[512,2048]{1,0:T(8,128)(2,1)} %slice_select_fusion), channel_id=1, source_target_pairs={{0,4},{4,0},{8,12},{12,8},{16,20},{20,16},{24,28},{28,24},{1,5},{5... | collective-permute-start | bytes 6291464 | tf_op jit(solution)/shard_map/ppermute | solution.py:479
  21.8 16.8 %collective-permute-start.3 = (bf16[256,1024]{1,0:T(8,128)(2,1)S(1)}, bf16[256,1024]{1,0:T(8,128)(2,1)}, u32[]{:S(2)}, u32[]{:S(2)}) collective-permute-start(bf16[256,1024]{1,0:T(8,128)(2,1)S(1)} %maximum_select_fusion.1.refs_0_.refs_9_), channel_id=1, source_target_pairs={{8,0},{12,4},{16,8},{20,12},{24,16},{28,20},{9,1},{13,5},{17,9},{2... | collective-permute-start | bytes 1572872 | tf_op jit(solution)/shard_map/ppermute | solution.py:482
  23.1 16.9 %collective-permute-start.11 = (bf16[256,1024]{1,0:T(8,128)(2,1)S(1)}, bf16[256,1024]{1,0:T(8,128)(2,1)S(1)}, u32[]{:S(2)}, u32[]{:S(2)}) collective-permute-start(bf16[256,1024]{1,0:T(8,128)(2,1)S(1)} %collective-permute-done.10.refs_4_.refs_8_), channel_id=1, source_target_pairs={{8,16},{12,20},{16,24},{20,28},{9,17},{13,21},{17,25},{21,29},{10,... | collective-permute-start | bytes 1572872 | tf_op jit(solution)/shard_map/ppermute | solution.py:482
  24.4 25.2 %collective-permute-start.13 = (bf16[256,1024]{1,0:T(8,128)(2,1)}, bf16[256,1024]{1,0:T(8,128)(2,1)S(1)}, u32[]{:S(2)}, u32[]{:S(2)}) collective-permute-start(bf16[256,1024]{1,0:T(8,128)(2,1)} %collective-permute-done.12.refs_1_.refs_3_), channel_id=1, source_target_pairs={{8,0},{12,4},{16,8},{20,12},{9,1},{13,5},{17,9},{21,13},{10,2},{14... | collective-permute-start | bytes 1572872 | tf_op jit(solution)/shard_map/ppermute | solution.py:482
  31.4 32.2 %collective-permute-start.6 = (bf16[512,1024]{1,0:T(8,128)(2,1)}, bf16[512,1024]{1,0:T(8,128)(2,1)}, u32[]{:S(2)}, u32[]{:S(2)}) collective-permute-start(bf16[512,1024]{1,0:T(8,128)(2,1)} %param.4), channel_id=1, source_target_pairs={{0,4},{4,0},{8,12},{12,8},{16,20},{20,16},{24,28},{28,24},{1,5},{5... | collective-permute-start | bytes 3145736 | tf_op jit(solution)/shard_map/ppermute | solution.py:479
  40.0 21.0 %collective-permute-start.4 = (bf16[256,1024]{1,0:T(8,128)(2,1)}, bf16[256,1024]{1,0:T(8,128)(2,1)}, u32[]{:S(2)}, u32[]{:S(2)}) collective-permute-start(bf16[256,1024]{1,0:T(8,128)(2,1)} %collective-permute-done.3.refs_1_.refs_10_), channel_id=1, source_target_pairs={{8,0},{12,4},{16,8},{20,12},{9,1},{13,5},{17,9},{21,13},{10,2},{14... | collective-permute-start | bytes 1572872 | tf_op jit(solution)/shard_map/ppermute | solution.py:482
  49.7 28.6 %collective-permute-start.14 = (bf16[256,1024]{1,0:T(8,128)(2,1)S(1)}, bf16[256,1024]{1,0:T(8,128)(2,1)S(1)}, u32[]{:S(2)}, u32[]{:S(2)}) collective-permute-start(bf16[256,1024]{1,0:T(8,128)(2,1)S(1)} %broadcast_select_fusion.2), channel_id=1, source_target_pairs={{16,24},{20,28},{8,0},{12,4},{17,25},{21,29},{9,1},{13,5},{18,26},... | collective-permute-start | bytes 1572872 | tf_op jit(solution)/shard_map/ppermute | solution.py:482
  62.1 20.4 %collective-permute-start.5 = (bf16[256,1024]{1,0:T(8,128)(2,1)S(1)}, bf16[256,1024]{1,0:T(8,128)(2,1)S(1)}, u32[]{:S(2)}, u32[]{:S(2)}) collective-permute-start(bf16[256,1024]{1,0:T(8,128)(2,1)S(1)} %broadcast_select_fusion.3), channel_id=1, source_target_pairs={{16,24},{20,28},{8,0},{12,4},{17,25},{21,29},{9,1},{13,5},{18,26},... | collective-permute-start | bytes 1572872 | tf_op jit(solution)/shard_map/ppermute | solution.py:482
  100.3 30.7 %collective-permute-start.26 = (bf16[256,1024]{1,0:T(8,128)(2,1)S(1)}, bf16[256,1024]{1,0:T(8,128)(2,1)S(1)}, u32[]{:S(2)}, u32[]{:S(2)}) collective-permute-start(bf16[256,1024]{1,0:T(8,128)(2,1)S(1)} %get-tuple-element.73), channel_id=1, source_target_pairs={{0,8},{4,12},{24,16},{28,20},{1,9},{5,13},{25,17},{29,21},{2,10},{... | collective-permute-start | bytes 1572872 | tf_op jit(solution)/shard_map/ppermute | solution.py:482
  112.9 27.6 %collective-permute-start.22 = (bf16[512,1024]{1,0:T(8,128)(2,1)S(1)}, bf16[512,1024]{1,0:T(8,128)(2,1)S(1)}, u32[]{:S(2)}, u32[]{:S(2)}) collective-permute-start(bf16[512,1024]{1,0:T(8,128)(2,1)S(1)} %slice.69), channel_id=1, source_target_pairs={{0,4},{4,0},{8,12},{12,8},{16,20},{20,16},{24,28},{28,24},{1,5},{5... | collective-permute-start | bytes 3145736 | tf_op jit(solution)/shard_map/ppermute | solution.py:479
  113.0 23.5 %collective-permute-start.31 = (bf16[256,1024]{1,0:T(8,128)(2,1)S(1)}, bf16[256,1024]{1,0:T(8,128)(2,1)S(1)}, u32[]{:S(2)}, u32[]{:S(2)}) collective-permute-start(bf16[256,1024]{1,0:T(8,128)(2,1)S(1)} %get-tuple-element.62), channel_id=1, source_target_pairs={{0,8},{4,12},{24,16},{28,20},{1,9},{5,13},{25,17},{29,21},{2,10},{... | collective-permute-start | bytes 1572872 | tf_op jit(solution)/shard_map/ppermute | solution.py:482
  131.8 16.2 %collective-permute-start.27 = (bf16[256,1024]{1,0:T(8,128)(2,1)S(1)}, bf16[256,1024]{1,0:T(8,128)(2,1)S(1)}, u32[]{:S(2)}, u32[]{:S(2)}) collective-permute-start(bf16[256,1024]{1,0:T(8,128)(2,1)S(1)} %fusion.3), channel_id=1, source_target_pairs={{0,8},{4,12},{8,16},{12,20},{1,9},{5,13},{9,17},{13,21},{2,10},{6,... | collective-permute-start | bytes 1572872 | tf_op jit(solution)/shard_map/ppermute | solution.py:482
  135.8 22.4 %collective-permute-start.29 = (bf16[256,1024]{1,0:T(8,128)(2,1)S(1)}, bf16[256,1024]{1,0:T(8,128)(2,1)S(1)}, u32[]{:S(2)}, u32[]{:S(2)}) collective-permute-start(bf16[256,1024]{1,0:T(8,128)(2,1)S(1)} %fusion.3), channel_id=1, source_target_pairs={{16,8},{20,12},{24,16},{28,20},{17,9},{21,13},{25,17},{29,21},{18,... | collective-permute-start | bytes 1572872 | tf_op jit(solution)/shard_map/ppermute | solution.py:482
  137.2 19.7 %collective-permute-start.32 = (bf16[256,1024]{1,0:T(8,128)(2,1)S(1)}, bf16[256,1024]{1,0:T(8,128)(2,1)S(1)}, u32[]{:S(2)}, u32[]{:S(2)}) collective-permute-start(bf16[256,1024]{1,0:T(8,128)(2,1)S(1)} %fusion.6), channel_id=1, source_target_pairs={{0,8},{4,12},{8,16},{12,20},{1,9},{5,13},{9,17},{13,21},{2,10},{6,... | collective-permute-start | bytes 1572872 | tf_op jit(solution)/shard_map/ppermute | solution.py:482
  139.7 23.6 %collective-permute-start.34 = (bf16[256,1024]{1,0:T(8,128)(2,1)S(1)}, bf16[256,1024]{1,0:T(8,128)(2,1)S(1)}, u32[]{:S(2)}, u32[]{:S(2)}) collective-permute-start(bf16[256,1024]{1,0:T(8,128)(2,1)S(1)} %fusion.6), channel_id=1, source_target_pairs={{16,8},{20,12},{24,16},{28,20},{17,9},{21,13},{25,17},{29,21},{18,... | collective-permute-start | bytes 1572872 | tf_op jit(solution)/shard_map/ppermute | solution.py:482
  141.2 24.2 %collective-permute-start.23 = (bf16[512,256]{1,0:T(8,128)(2,1)S(1)}, bf16[512,256]{1,0:T(8,128)(2,1)S(1)}, u32[]{:S(2)}, u32[]{:S(2)}) collective-permute-start(bf16[512,256]{1,0:T(8,128)(2,1)S(1)} %get-tuple-element.75), channel_id=1, source_target_pairs={{0,1},{1,0},{2,3},{3,2},{4,5},{5,4},{6,7},{7,6},{8,9},{9,8},{10,11... | collective-permute-start | bytes 786440 | tf_op jit(solution)/shard_map/ppermute | solution.py:485
  148.0 21.9 %collective-permute-start.24 = (bf16[512,256]{1,0:T(8,128)(2,1)S(1)}, bf16[512,256]{1,0:T(8,128)(2,1)S(1)}, u32[]{:S(2)}, u32[]{:S(2)}) collective-permute-start(bf16[512,256]{1,0:T(8,128)(2,1)S(1)} %get-tuple-element.77), channel_id=1, source_target_pairs={{0,2},{1,3},{2,0},{3,1},{4,6},{5,7},{6,4},{7,5},{8,10},{9,11},{10,... | collective-permute-start | bytes 786440 | tf_op jit(solution)/shard_map/ppermute | solution.py:485
  158.1 16.7 %collective-permute-start.28 = (bf16[256,1024]{1,0:T(8,128)(2,1)S(1)}, bf16[256,1024]{1,0:T(8,128)(2,1)S(1)}, u32[]{:S(2)}, u32[]{:S(2)}) collective-permute-start(bf16[256,1024]{1,0:T(8,128)(2,1)S(1)} %fusion.2), channel_id=1, source_target_pairs={{0,8},{4,12},{8,16},{12,20},{16,24},{20,28},{1,9},{5,13},{9,17},{1... | collective-permute-start | bytes 1572872 | tf_op jit(solution)/shard_map/ppermute | solution.py:482
  163.3 16.7 %collective-permute-start.30 = (bf16[256,1024]{1,0:T(8,128)(2,1)S(1)}, bf16[256,1024]{1,0:T(8,128)(2,1)S(1)}, u32[]{:S(2)}, u32[]{:S(2)}) collective-permute-start(bf16[256,1024]{1,0:T(8,128)(2,1)S(1)} %fusion.4), channel_id=1, source_target_pairs={{8,0},{12,4},{16,8},{20,12},{24,16},{28,20},{9,1},{13,5},{17,9},{2... | collective-permute-start | bytes 1572872 | tf_op jit(solution)/shard_map/ppermute | solution.py:482
  165.3 17.2 %collective-permute-start.33 = (bf16[256,1024]{1,0:T(8,128)(2,1)S(1)}, bf16[256,1024]{1,0:T(8,128)(2,1)S(1)}, u32[]{:S(2)}, u32[]{:S(2)}) collective-permute-start(bf16[256,1024]{1,0:T(8,128)(2,1)S(1)} %fusion.5), channel_id=1, source_target_pairs={{0,8},{4,12},{8,16},{12,20},{16,24},{20,28},{1,9},{5,13},{9,17},{1... | collective-permute-start | bytes 1572872 | tf_op jit(solution)/shard_map/ppermute | solution.py:482
  169.9 17.5 %collective-permute-start.35 = (bf16[256,1024]{1,0:T(8,128)(2,1)S(1)}, bf16[256,1024]{1,0:T(8,128)(2,1)S(1)}, u32[]{:S(2)}, u32[]{:S(2)}) collective-permute-start(bf16[256,1024]{1,0:T(8,128)(2,1)S(1)} %fusion.7), channel_id=1, source_target_pairs={{8,0},{12,4},{16,8},{20,12},{24,16},{28,20},{9,1},{13,5},{17,9},{2... | collective-permute-start | bytes 1572872 | tf_op jit(solution)/shard_map/ppermute | solution.py:482
  (23 other events, 193.8 us)

commit v5 on v4

--- a/solution.py
+++ b/solution.py
@@ -20,12 +20,31 @@
     return lax.dot_general(a, b, (((1,), (1,)), ((), ())), preferred_element_type=f32)
 
 
-def lanes(columns, like):
+def lanes(columns, like, first=0):
     lane = lax.broadcasted_iota(jnp.int32, like, 1)
     out = jnp.zeros(like, f32)
     for k, c in enumerate(columns):
-        out = jnp.where(lane == k, c, out)
+        out = jnp.where(lane == first + k, c, out)
     return out
+
+
+def block_of(kind, z, s):
+    ahead = (z % 2 == 0) == (kind == "even")
+    return z + s if ahead else z - s
+
+
+def edge(kind, z):
+    return z ^ 1 if kind == "even" else ((z + 1) ^ 1) - 1
+
+
+def holders(kind, nz, s):
+    return [z for z in range(nz) if 0 <= block_of(kind, z, s) < nz]
+
+
+def arrivals(nz):
+    return [("own", 0)] + [
+        (kind, s) for s in range(1, nz) for kind in ("even", "odd") if holders(kind, nz, s)
+    ]
 
 
 def cost(flops, size, trans=0):
@@ -101,56 +120,37 @@
     )(near(x))
 
 
-def choices(nz):
-    unique, table = [("own", 0)], []
-    for j in range(1, nz):
-        table.append((("down", j), ("up", nz - j)))
-        unique += [c for c in table[-1] if c not in unique]
-    return unique, table
-
-
-def gathered(up, down, p, nz, all_steps):
-    unique, _ = choices(nz)
-    pick = {"own": up, "up": up, "down": down}
-    return [pick[k][p][j] for k, j in unique if all_steps or j < nz - 1]
-
-
-def assemble(z, nz, refs, whole_ref, sem):
-    unique, table = choices(nz)
-    if len(refs) < len(unique):
-        unique = [c for c in unique if c[1] < nz - 1]
+def assemble(z, nz, count, refs, whole_ref, sem):
     deep = refs[0].shape[0]
-
-    def place(j):
-        return pl.ds(pl.multiple_of(lax.rem(z + j, nz) * deep, deep), deep)
-
-    def copy(k, j):
-        return pltpu.make_async_copy(refs[k], whole_ref.at[place(j), :], sem.at[j])
-
-    def each(do):
-        do(0, 0)
-        for j in range(1, nz):
-            for choice, here in zip(table[j - 1], (z + j < nz, z + j >= nz)):
-
-                @pl.when(here)
-                def _(choice=choice, j=j):
-                    if choice in unique:
-                        do(unique.index(choice), j)
-                    else:
-                        do(None, j)
-
-    def start(k, j):
-        if k is None:
-            whole_ref[place(j), :] = jnp.zeros((deep, whole_ref.shape[1]), bf16)
-        else:
-            copy(k, j).start()
-
-    def wait(k, j):
-        if k is not None:
-            copy(k, j).wait()
-
-    each(start)
-    return lambda: each(wait)
+    given = arrivals(nz)[:count]
+
+    def place(block):
+        return pl.ds(pl.multiple_of(block * deep, deep), deep)
+
+    def each(act):
+        for k, (kind, s) in enumerate(given):
+            if kind == "own":
+                act(k, z)
+                continue
+            sign = jnp.where((lax.rem(z, 2) == 0) == (kind == "even"), 1, -1)
+            block = z + sign * s
+
+            @pl.when(jnp.logical_and(block >= 0, block < nz))
+            def _(k=k, block=block):
+                act(k, block)
+
+    def copy(k, block):
+        return pltpu.make_async_copy(refs[k], whole_ref.at[place(block), :], sem.at[k])
+
+    each(lambda k, block: copy(k, block).start())
+    if count < len(arrivals(nz)):
+
+        @pl.when(jnp.logical_or(z == 0, z == nz - 1))
+        def _():
+            hole = jnp.where(z == 0, nz - 1, 0)
+            whole_ref[place(hole), :] = jnp.zeros((deep, whole_ref.shape[1]), bf16)
+
+    return lambda: each(lambda k, block: copy(k, block).wait())
 
 
 def early_kernel(nz, count, z_ref, *refs):
@@ -159,7 +159,7 @@
 
     @pl.when(pl.program_id(0) == 0)
     def _():
-        assemble(z_ref[0], nz, w_refs, whole_ref, sem)()
+        assemble(z_ref[0], nz, count, w_refs, whole_ref, sem)()
 
     tile = h_ref.shape[0] // pl.num_programs(0)
     at = pl.ds(pl.multiple_of(pl.program_id(0) * tile, tile), tile)
@@ -176,7 +176,10 @@
             grid=(n // tile,),
             in_specs=[pl.BlockSpec(memory_space=pl.ANY)] * len(blocks) + [WHOLE],
             out_specs=WHOLE,
-            scratch_shapes=[pltpu.VMEM((dh, piece), bf16), pltpu.SemaphoreType.DMA((nz,))],
+            scratch_shapes=[
+                pltpu.VMEM((dh, piece), bf16),
+                pltpu.SemaphoreType.DMA((len(blocks),)),
+            ],
         ),
         out_shape=out((n, piece), f32),
         compiler_params=params(10),
@@ -206,26 +209,28 @@
         column = lax.broadcasted_iota(jnp.int32, z.shape, 1) + part * piece
         id_col = t_stat[:, 3:4].astype(jnp.int32)
         own = jnp.sum(jnp.where(column == id_col, z, 0.0), axis=1, keepdims=True)
+        stat = lanes([top, total, cross, own], like, 4 + 4 * part)
         if part < PARTS - 1:
-            outs[1][at, :] = lanes([top, total, cross, own], like)
+            outs[1][at, :] = stat
             continue
         send_ref, turn_ref, tops_ref = outs[1:]
-        stats = [r[at, :] for r in stat_refs]
-        all_top = top
-        for r in stats:
-            all_top = jnp.maximum(all_top, r[:, 0:1])
-        total = total * jnp.exp(top - all_top)
-        for r in stats:
-            total = total + r[:, 1:2] * jnp.exp(r[:, 0:1] - all_top)
-            cross = cross + r[:, 2:3]
-            own = own + r[:, 3:4]
-        t_top, t_total, t_first = t_stat[:, 0:1], t_stat[:, 1:2], t_stat[:, 2:3]
-        rows = lanes([t_top, t_total, t_first - cross, all_top, total, own], like).T[:8]
+        stat = stat + t_stat
+        for r in stat_refs:
+            stat = stat + r[at, :]
+        row = stat.T
+        row = [row[k:k + 1] for k in range(4 + 4 * PARTS)]
+        tops = row[4::4]
+        all_top = functools.reduce(jnp.maximum, tops)
+        total = sum(row[5 + 4 * p] * jnp.exp(tops[p] - all_top) for p in range(PARTS))
+        cross, own = sum(row[6::4]), sum(row[7::4])
+        blank = jnp.zeros((1, tile), f32)
+        rows = [row[0], row[1], row[2] - cross, all_top, total, own, blank, blank]
+        rows = jnp.concatenate(rows)
         send_ref[:, at] = rows
         turned = (k * tile + n // 2) % n
         turn_ref[:, turned:turned + tile] = rows
-        tops = [r[:, 0:1] for r in stats] + [top]
-        tops_ref[at, :] = lanes([t_top] + tops + [t_stat[:, 3:4]], like)
+        tops = [row[0]] + tops + [row[3]]
+        tops_ref[:, at] = jnp.concatenate(tops + [blank] * (8 - len(tops)))
 
 
 def last_call(part, at, w, acc, hid, e_t, t_stat, stats, tile):
@@ -235,7 +240,7 @@
         stats = []
         out_shape += [out((n, 128), f32)]
     else:
-        out_shape += [out((8, n), f32), out((8, n), f32), out((n, 128), f32)]
+        out_shape += [out((8, n), f32)] * 3
     return pl.pallas_call(
         functools.partial(last_kernel, part, len(stats), tile),
         grid_spec=pltpu.PrefetchScalarGridSpec(
@@ -258,7 +263,9 @@
     @pl.when(pl.program_id(0) == 0)
     def _():
         waits = [
-            assemble(z_ref[0], nz, w_refs[p * count:(p + 1) * count], whole_ref.at[p], sem.at[p])
+            assemble(
+                z_ref[0], nz, count, w_refs[p * count:(p + 1) * count], whole_ref.at[p], sem.at[p]
+            )
             for p in range(PARTS)
         ]
         for wait in waits:
@@ -286,7 +293,7 @@
             out_specs=pl.BlockSpec((tile, dh), row),
             scratch_shapes=[
                 pltpu.VMEM((PARTS, dh, piece), bf16),
-                pltpu.SemaphoreType.DMA((PARTS, nz)),
+                pltpu.SemaphoreType.DMA((PARTS, count)),
             ],
         ),
         out_shape=jax.ShapeDtypeStruct((n, dh), bf16),
@@ -353,12 +360,12 @@
             )
             loss_ref[...] = jnp.broadcast_to(plane, loss_ref.shape)
             z_inv = (1.0 + ce_weight) / s[4:5]
-            flat = jnp.concatenate([s[0:1], t_inv, s[3:4], z_inv, jnp.zeros((124, n), f32)]).T
             tops = tops_ref[...]
-            lane = lax.broadcasted_iota(jnp.int32, tops.shape, 1)
-            base = jnp.where(lane == 0, flat[:, 0:1], flat[:, 2:3])
-            gain = jnp.where(lane == 0, flat[:, 1:2], flat[:, 3:4])
-            coef_ref[...] = jnp.where(lane <= PARTS, jnp.exp(tops - base) * gain, tops)
+            rows = [jnp.exp(tops[0:1] - s[0:1]) * t_inv]
+            rows += [jnp.exp(tops[p + 1:p + 2] - s[3:4]) * z_inv for p in range(PARTS)]
+            rows += [tops[PARTS + 1:PARTS + 2]]
+            rows += [jnp.zeros((128 - len(rows), n), f32)]
+            coef_ref[...] = jnp.concatenate(rows).T
 
     else:
         coef_ref, ez_ref, et_ref, ht_ref, slope_ref, msg_ref = refs
@@ -447,31 +454,40 @@
     voc = lax.axis_index("voc")
     width = dh // n_voc
 
-    def first_row(s):
-        return jnp.where(z < s, jnp.minimum(z + nz - s, nz - 1), jnp.maximum(z - nz + s, 0))
+    def here(kind, s):
+        return z + jnp.where((lax.rem(z, 2) == 0) == (kind == "even"), s, -s)
+
+    def inside(block):
+        return jnp.logical_and(block >= 0, block < nz)
+
+    def single(s):
+        return not set(holders("even", nz, s)) & set(holders("odd", nz, s))
 
     def scalar(x):
         return jnp.reshape(x, (1,)).astype(jnp.int32)
 
     even = core == 0
-    above = [z >= s for s in range(nz)]
+    first_chip = z == 0
+    row_of = {("own", 0): z}
+    for s in range(1, nz):
+        even_block, odd_block = here("even", s), here("odd", s)
+        row_of["even", s] = jnp.clip(even_block, 0, nz - 1)
+        row_of["odd", s] = jnp.clip(odd_block, 0, nz - 1)
+        if single(s):
+            either = jnp.where(inside(even_block), even_block, odd_block)
+            row_of["even", s] = row_of["odd", s] = jnp.clip(either, 0, nz - 1)
     ahead = {
         "core": scalar(core),
         "z": scalar(z),
         "last": scalar(jnp.where(z == 0, nz - 1, 0)),
-        "first": scalar(first_row(1)),
+        "first": scalar(row_of["even", nz - 1]),
     }
-    row_of = {("own", 0): z * deep}
-    for s in range(1, nz):
-        if 2 * s <= nz:
-            row_of["first", s] = first_row(s) * deep
-        row_of["up", s] = jnp.minimum(z + nz - s, nz - 1) * deep
-        row_of["down", s] = jnp.maximum(z - nz + s, 0) * deep
+    row_of = {k: v * deep for k, v in row_of.items()}
     col_of = [(voc ^ v) * width for v in range(n_voc)]
     vocab_start = voc * share + core * half
-    (even, above, ahead, row_of, col_of, vocab_start), head, hidden, logits, ids = (
+    (even, first_chip, ahead, row_of, col_of, vocab_start), head, hidden, logits, ids = (
         lax.optimization_barrier(
-            ((even, above, ahead, row_of, col_of, vocab_start), head, hidden, logits, ids)
+            ((even, first_chip, ahead, row_of, col_of, vocab_start), head, hidden, logits, ids)
         )
     )
 
@@ -479,7 +495,9 @@
         return lax.ppermute(x, "tok", [(i, i ^ 1) for i in range(n_tok)])
 
     def hop(x, pairs):
-        return lax.ppermute(x, "tok", [(2 * a + k, 2 * b + k) for a, b in pairs for k in range(2)])
+        return lax.ppermute(
+            x, "tok", [(2 * a + k, 2 * b + k) for a, b in pairs for k in range(2)]
+        )
 
     def plane_swap(x, v):
         return lax.ppermute(x, "voc", [(w, w ^ v) for w in range(n_voc)])
@@ -501,20 +519,14 @@
             )
         )
 
-    up = [[b] for b in blocks]
-    down = [[b] for b in blocks]
+    came = [{("own", 0): b, ("even", 0): b, ("odd", 0): b} for b in blocks]
+    other_kind = {"even": "odd", "odd": "even"}
     for s in range(1, nz):
-        up_pairs = [(a, a + 1) for a in range(s - 1, nz - 1)]
-        down_pairs = [(a, a - 1) for a in range(1, nz - s + 1)]
         for p in range(PARTS):
-            u, d = up[p][-1], down[p][-1]
-            if 2 * s > nz + 1:
-                both = hop(jnp.where(above[s - 1], u, d), up_pairs + down_pairs)
-                up[p].append(both)
-                down[p].append(both)
-            else:
-                up[p].append(hop(u, up_pairs))
-                down[p].append(hop(d, down_pairs))
+            for kind in ("even", "odd"):
+                pairs = [(edge(kind, a), a) for a in holders(kind, nz, s)]
+                if pairs:
+                    came[p][kind, s] = hop(came[p][other_kind[kind], s - 1], pairs)
 
     hid = jnp.concatenate([hidden, swap(hidden)])
     hid_t = turn_call(hid, tile)
@@ -524,11 +536,13 @@
     e_t, t_stat = target_call(ahead["core"], logits, tgt, local[:, None], tile)
 
     stats, e_z = [], []
-    whole = [gathered(up, down, p, nz, True) for p in range(PARTS)]
+    order = arrivals(nz)
+    whole = [[came[p][k] for k in order] for p in range(PARTS)]
+    early = [k for k in order if k[1] < nz - 1]
     for p in range(PARTS):
-        acc = early_call(nz, ahead["z"], gathered(up, down, p, nz, False), hid, tile)
-        final_u, final_d = up[p][-1], down[p][-1]
-        w = final_u if final_u is final_d else jnp.where(above[nz - 1], final_u, final_d)
+        acc = early_call(nz, ahead["z"], whole[p][:len(early)], hid, tile)
+        w = whole[p][len(early):]
+        w = w[0] if len(w) == 1 else jnp.where(first_chip, w[0], w[1])
         outs = last_call(p, ahead["last"], w, acc, hid, e_t, t_stat, stats, tile)
         e_z.append(outs[0])
         if p < PARTS - 1:
@@ -539,7 +553,7 @@
     bits = n_voc.bit_length() - 1
     done = 0
     while True:
-        few = min(2, bits - done)
+        few = min(1, bits - done)
         got = [x] + [plane_swap(x, v << done) for v in range(1, 1 << few)]
         done += few
         if done >= bits:
@@ -549,9 +563,7 @@
     msgs, slope = [], []
     for p in range(PARTS):
         head_args = got + [tops] if p == 0 else [coef]
-        outs = slope_call(
-            p, ahead["first"], head_args, e_z[p], e_t, hid_t, deep, wide
-        )
+        outs = slope_call(p, ahead["first"], head_args, e_z[p], e_t, hid_t, deep, wide)
         slope.append(outs[0])
         msgs.append(outs[1])
         if p == 0:
@@ -564,32 +576,30 @@
     def grad_rows(way, s, p):
         return dot(cut(hid_t, row_of[way, s], 0, (deep, 2 * rows)), slope[p])
 
-    got_up, got_down = [None] * PARTS, [None] * PARTS
-    for s in range(1, nz):
-        up_pairs = [(a, a + 1) for a in range(0, s)]
-        down_pairs = [(a, a - 1) for a in range(nz - s, nz)]
+    def add(x, *terms):
+        for t in terms:
+            if t is not None:
+                x = x + t.astype(f32)
+        return x
+
+    got = [{} for _ in range(PARTS)]
+    for s in range(nz - 1, 0, -1):
         for p in range(PARTS):
-            if 2 * s <= nz:
-                if s == 1:
+            for kind in ("even", "odd"):
+                pairs = [(a, edge(kind, a)) for a in holders(kind, nz, s)]
+                if not pairs:
+                    continue
+                back = {k: got[p].get((k, s + 1)) for k in other_kind}
+                if s == nz - 1 and kind == "even":
                     msg = msgs[p]
-                else:
-                    msg = grad_rows("first", s, p) + got_up[p].astype(f32)
-                    if got_down[p] is not got_up[p]:
-                        msg = msg + got_down[p].astype(f32)
-                    msg = msg.astype(bf16)
-                if 2 * s < nz - 1:
-                    got_up[p] = got_down[p] = hop(msg, up_pairs + down_pairs)
-                else:
-                    got_up[p] = hop(msg, up_pairs)
-                    got_down[p] = hop(msg, down_pairs)
-            else:
-                msg_up = grad_rows("up", s, p) + got_up[p].astype(f32)
-                msg_down = grad_rows("down", s, p) + got_down[p].astype(f32)
-                got_up[p] = hop(msg_up.astype(bf16), up_pairs)
-                got_down[p] = hop(msg_down.astype(bf16), down_pairs)
+                elif not single(s):
+                    msg = add(grad_rows(kind, s, p), back[other_kind[kind]]).astype(bf16)
+                elif kind == "even" or s == nz - 1:
+                    msg = add(grad_rows(kind, s, p), *back.values()).astype(bf16)
+                got[p][kind, s] = hop(msg, pairs)
     keeps, gives = [], []
     for p in range(PARTS):
-        full = grad_rows("own", 0, p) + got_up[p].astype(f32) + got_down[p].astype(f32)
+        full = add(grad_rows("own", 0, p), got[p].get(("even", 1)), got[p].get(("odd", 1)))
         low, high = full[:own_rows], full[own_rows:]
         keeps.append(jnp.where(even, low, high))
         give = jnp.where(even, high, low).astype(bf16)

time: 192 us -> 189 us (0.984)
  Pallas kernels: 34.3 us -> 31.1 us
    ppermute x23, starting transfers between devices: 44.9 us -> 40.6 us  [hop(): lax.ppermute(x, 'tok', [(2 * a + k, 2 * b + k) for a, b in pairs for k in...]
    ppermute x9, waiting for transfers between devices: 7.57 us -> 3.58 us  [swap(): return lax.ppermute(x, 'tok', [(i, i ^ 1) for i in range(n_tok)])]
    ppermute x6 -> x5, starting transfers between devices: 5.18 us -> 8.64 us  [plane_swap(): return lax.ppermute(x, 'voc', [(w, w ^ v) for w in range(n_voc)])]
    pallas_call x2, Pallas kernels: 7.78 us -> 5.24 us  [last_call(): pl.pallas_call(functools.partial(last_kernel, part, len(stats), tile), gr...]
    select_n x1, other arithmetic: 1.54 us -> 3.76 us  [mine(): jnp.where(even, right, left)]
    ppermute x6 -> x5, waiting for transfers between devices: 3.69 us -> 5.05 us  [plane_swap(): return lax.ppermute(x, 'voc', [(w, w ^ v) for w in range(n_voc)])]
  transfers between devices with their start and end apart: 38 -> 37, of which waited for: 20 -> 20; matrix products, arithmetic and copies ran while one was open for 8% -> 9% of each run, Pallas kernels for 13% -> 14%
where the time goes in v5:
time: 189 us; the launch traced here: 188 us
  waiting for transfers between devices  84.4 us (45%)
  starting transfers between devices  50.7 us (27%)
  Pallas kernels  31.1 us (16%)
  other arithmetic  9.61 us (5%)
  matrix products  5.79 us (3%)
  local copies, waits for them, and re-layouts  5.37 us (3%)
    ppermute x23, waiting for transfers between devices, hop(): lax.ppermute(x, 'tok', [(2 * a + k, 2 * b + k) for a, b in pairs for k in...  75.8 us
    ppermute x23, starting transfers between devices, hop(): lax.ppermute(x, 'tok', [(2 * a + k, 2 * b + k) for a, b in pairs for k in...  40.6 us
    ppermute x5, starting transfers between devices, plane_swap(): return lax.ppermute(x, 'voc', [(w, w ^ v) for w in range(n_voc)])  8.64 us
    pallas_call x2, Pallas kernels, early_call(): pl.pallas_call(functools.partial(early_kernel, nz, len(blocks)), grid_spe...  8.26 us
    pallas_call x1, Pallas kernels, hidden_call(): pl.pallas_call(functools.partial(hidden_kernel, nz, count), grid_spec=plt...  6.74 us
    dot_general x8, matrix products, dot(): lax.dot_general(a, b, (((1,), (0,)), ((), ())), preferred_element_type=f32)  5.79 us
    pallas_call x2, Pallas kernels, last_call(): pl.pallas_call(functools.partial(last_kernel, part, len(stats), tile), gr...  5.24 us
    pallas_call x2, Pallas kernels, slope_call(): pl.pallas_call(functools.partial(slope_kernel, part, peers), grid_spec=pl...  5.08 us
  transfers between devices with their start and end apart: 37, of which 20 were waited for; matrix products, arithmetic and copies ran while one was open for 9% of the time, Pallas kernels for 14%

profile of v5, /device:TPU:0, one launch (start us, length us, event | category | flops | bytes accessed | tf_op | source)
XLA Modules:
  0.0 188.1 jit_solution(13845197940192395405)
XLA Ops:
  2.6 3.8 %slice_select_fusion = bf16[512,2048]{1,0:T(8,128)(2,1)} fusion(bf16[512,4096]{1,0:T(8,128)(2,1)} %mine_ref, pred[]{:T(512)S(6)} %eq.8), kind=kLoop, calls=%fused_computation.2 | loop fusion | flops 1048576 | bytes 6291457 | tf_op jit(solution)/shard_map/jit(_where)/select_n | solution.py:507
  6.6 3.1 %collective-permute-start.10 = (bf16[256,1024]{1,0:T(8,128)(2,1)S(1)}, bf16[256,1024]{1,0:T(8,128)(2,1)}, u32[]{:S(2)}, u32[]{:S(2)}) collective-permute-start(bf16[256,1024]{1,0:T(8,128)(2,1)S(1)} %maximum_select_fusion.2.refs_0_.refs_2_), channel_id=1, source_target_pairs={{8,0},{12,4},{0,8},{4,12},{24,16},{28,20},{16,24},{20,28},{9,1},{1... | collective-permute-start | bytes 1572872 | tf_op jit(solution)/shard_map/ppermute | solution.py:498
  12.8 4.6 %collective-permute-start.1 = (bf16[256,1024]{1,0:T(8,128)(2,1)S(1)}, bf16[256,1024]{1,0:T(8,128)(2,1)}, u32[]{:S(2)}, u32[]{:S(2)}) collective-permute-start(bf16[256,1024]{1,0:T(8,128)(2,1)S(1)} %maximum_select_fusion.1.refs_0_.refs_8_), channel_id=1, source_target_pairs={{8,0},{12,4},{0,8},{4,12},{24,16},{28,20},{16,24},{20,28},{9,1},{1... | collective-permute-start | bytes 1572872 | tf_op jit(solution)/shard_map/ppermute | solution.py:498
  17.5 5.1 %collective-permute-done.10.refs_1_.refs_3_ = bf16[256,1024]{1,0:T(8,128)(2,1)} collective-permute-done((bf16[256,1024]{1,0:T(8,128)(2,1)S(1)}, bf16[256,1024]{1,0:T(8,128)(2,1)}, u32[]{:S(2)}, u32[]{:S(2)}) %collective-permute-start.10) | collective-permute-done | bytes 524320 | tf_op jit(solution)/shard_map/ppermute | solution.py:498
  24.8 8.4 %collective-permute-done.1.refs_1_.refs_9_ = bf16[256,1024]{1,0:T(8,128)(2,1)} collective-permute-done((bf16[256,1024]{1,0:T(8,128)(2,1)S(1)}, bf16[256,1024]{1,0:T(8,128)(2,1)}, u32[]{:S(2)}, u32[]{:S(2)}) %collective-permute-start.1) | collective-permute-done | bytes 524320 | tf_op jit(solution)/shard_map/ppermute | solution.py:498
  45.3 11.5 %collective-permute-done.14.refs_3_.refs_5_ = bf16[256,1024]{1,0:T(8,128)(2,1)} collective-permute-done((bf16[256,1024]{1,0:T(8,128)(2,1)}, bf16[256,1024]{1,0:T(8,128)(2,1)}, u32[]{:S(2)}, u32[]{:S(2)}) %collective-permute-start.14) | collective-permute-done | bytes 524320 | tf_op jit(solution)/shard_map/ppermute | solution.py:498
  56.9 4.1 %early_draft.3.refs_1_ = f32[1024,1024]{1,0:T(8,128)S(1)} custom-call(s32[1]{0:T(128)} %bitcast.3.z_ref, bf16[256,1024]{1,0:T(8,128)(2,1)S(1)} %maximum_select_fusion.2.refs_0_.refs_2_, bf16[256,1024]{1,0:T(8,128)(2,1)} %collective-permute-done.10.refs_1_.refs_3_, bf16[256,1024]{1,0:T(8,128)(2,1)} %collective-permute-done.13.refs_2_.refs_4_, ...), custom_call_target="tpu_custom_call" | custom-call | flops 2147483648 | bytes 6291456 | tf_op jit(solution)/shard_map/early_draft/pallas_call | solution.py:172
  61.0 7.0 %collective-permute-done.5.refs_3_.refs_11_ = bf16[256,1024]{1,0:T(8,128)(2,1)S(1)} collective-permute-done((bf16[256,1024]{1,0:T(8,128)(2,1)}, bf16[256,1024]{1,0:T(8,128)(2,1)S(1)}, u32[]{:S(2)}, u32[]{:S(2)}) %collective-permute-start.5) | collective-permute-done | bytes 524320 | tf_op jit(solution)/shard_map/ppermute | solution.py:498
  68.0 4.1 %early_draft.2.refs_1_ = f32[1024,1024]{1,0:T(8,128)S(1)} custom-call(s32[1]{0:T(128)} %bitcast.3.z_ref, bf16[256,1024]{1,0:T(8,128)(2,1)S(1)} %maximum_select_fusion.1.refs_0_.refs_8_, bf16[256,1024]{1,0:T(8,128)(2,1)} %collective-permute-done.1.refs_1_.refs_9_, bf16[256,1024]{1,0:T(8,128)(2,1)S(1)} %copy-done.2, ...), custom_call_target="tpu_custom_call" | custom-call | flops 2147483648 | bytes 6291456 | tf_op jit(solution)/shard_map/early_draft/pallas_call | solution.py:172
  72.1 5.0 %target_exps.1 = (bf16[1024,2048]{1,0:T(8,128)(2,1)S(1)}, f32[1024,128]{1,0:T(8,128)S(1)}) custom-call(s32[1]{0:T(128)} %bitcast.core_ref, bf16[512,4096]{1,0:T(8,128)(2,1)S(1)} %copy-done, bf16[512,2048]{1,0:T(8,128)(2,1)} %collective-permute-done.7.came_ref, s32[1024,1]{1,0:T(8,128)S(1)} %broadcast_subtract_fusion.id_ref), custom_call_target="tpu_custom_call" | custom-call | flops 16777216 | bytes 8388608 | tf_op jit(solution)/shard_map/target_exps/pallas_call | solution.py:85
  79.2 2.5 %last_draft.2 = (bf16[1024,1024]{1,0:T(8,128)(2,1)S(1)}, f32[1024,128]{1,0:T(8,128)S(1)}) custom-call(s32[1]{0:T(128)} %bitcast.2.at_ref, bf16[256,1024]{1,0:T(8,128)(2,1)S(1)} %collective-permute-done.12.refs_0_.refs_7_, f32[1024,1024]{1,0:T(8,128)S(1)} %early_draft.3.refs_1_, ...), custom_call_target="tpu_custom_call" | custom-call | flops 536870912 | bytes 8388608 | tf_op jit(solution)/shard_map/last_draft/pallas_call | solution.py:244
  81.7 7.0 %collective-permute-done.3.refs_0_.refs_13_ = bf16[256,1024]{1,0:T(8,128)(2,1)S(1)} collective-permute-done((bf16[256,1024]{1,0:T(8,128)(2,1)}, bf16[256,1024]{1,0:T(8,128)(2,1)S(1)}, u32[]{:S(2)}, u32[]{:S(2)}) %collective-permute-start.3) | collective-permute-done | bytes 524320 | tf_op jit(solution)/shard_map/ppermute | solution.py:498
  88.7 2.8 %last_draft.3 = (bf16[1024,1024]{1,0:T(8,128)(2,1)S(1)}, f32[8,1024]{1,0:T(8,128)S(1)}, f32[8,1024]{1,0:T(8,128)S(1)}, f32[8,1024]{1,0:T(8,128)S(1)}) custom-call(s32[1]{0:T(128)} %bitcast.2.at_ref, bf16[256,1024]{1,0:T(8,128)(2,1)S(1)} %collective-permute-done.3.refs_0_.refs_13_, f32[1024,1024]{1,0:T(8,128)S(1)} %early_draft.2.refs_1_, ...), custom_call_target="tpu_custom_call" | custom-call | flops 536870912 | bytes 8388608 | tf_op jit(solution)/shard_map/last_draft/pallas_call | solution.py:244
  100.8 2.7 %slope.2 = (bf16[1024,1024]{1,0:T(8,128)(2,1)S(1)}, bf16[256,1024]{1,0:T(8,128)(2,1)S(1)}, f32[1024,128]{1,0:T(8,128)S(1)}, f32[8,128]{1,0:T(8,128)S(1)}) custom-call(s32[1]{0:T(128)} %bitcast.1.idx_ref, f32[8,1024]{1,0:T(8,128)S(1)} %fold.3.refs_0_, f32[8,1024]{1,0:T(8,128)S(1)} %collective-permute-done.17.refs_1_, ...), custom_call_target="tpu_custom_call" | custom-call | flops 536870912 | bytes 6291456 | tf_op jit(solution)/shard_map/slope/pallas_call | solution.py:399
  109.0 8.3 %collective-permute-done.25 = bf16[256,1024]{1,0:T(8,128)(2,1)S(1)} collective-permute-done((bf16[256,1024]{1,0:T(8,128)(2,1)S(1)}, bf16[256,1024]{1,0:T(8,128)(2,1)S(1)}, u32[]{:S(2)}, u32[]{:S(2)}) %collective-permute-start.25) | collective-permute-done | bytes 524320 | tf_op jit(solution)/shard_map/ppermute | solution.py:498
  118.7 6.7 %hidden_grad.1 = bf16[1024,1024]{1,0:T(8,128)(2,1)S(1)} custom-call(s32[1]{0:T(128)} %bitcast.3.z_ref, bf16[1024,1024]{1,0:T(8,128)(2,1)S(1)} %get-tuple-element.62.refs_0_, bf16[1024,1024]{1,0:T(8,128)(2,1)S(1)} %get-tuple-element.63.refs_1_, bf16[256,1024]{1,0:T(8,128)(2,1)S(1)} %maximum_select_fusion.2.refs_0_.refs_2_, ...), custom_call_target="tpu_custom_call" | custom-call | flops 4294967296 | bytes 8388608 | tf_op jit(solution)/shard_map/hidden_grad/pallas_call | solution.py:286
  125.6 5.6 %collective-permute-start.18 = (f32[8,128]{1,0:T(8,128)S(1)}, f32[8,128]{1,0:T(8,128)S(1)}, u32[]{:S(2)}, u32[]{:S(2)}) collective-permute-start(f32[8,128]{1,0:T(8,128)S(1)} %get-tuple-element.61.refs_0_), channel_id=1, source_target_pairs={{0,8},{4,12},{8,16},{12,20},{16,24},{20,28},{24,0},{28,4},{1,9},{5... | collective-permute-start | bytes 12296 | tf_op jit(solution)/shard_map/ppermute | solution.py:498
  137.0 3.9 %collective-permute-start.28 = (bf16[256,1024]{1,0:T(8,128)(2,1)S(1)}, bf16[256,1024]{1,0:T(8,128)(2,1)S(1)}, u32[]{:S(2)}, u32[]{:S(2)}) collective-permute-start(bf16[256,1024]{1,0:T(8,128)(2,1)S(1)} %fusion.3), channel_id=1, source_target_pairs={{0,8},{4,12},{24,16},{28,20},{1,9},{5,13},{25,17},{29,21},{2,10},{... | collective-permute-start | bytes 1572872 | tf_op jit(solution)/shard_map/ppermute | solution.py:498
  142.4 3.0 %collective-permute-start.33 = (bf16[256,1024]{1,0:T(8,128)(2,1)S(1)}, bf16[256,1024]{1,0:T(8,128)(2,1)S(1)}, u32[]{:S(2)}, u32[]{:S(2)}) collective-permute-start(bf16[256,1024]{1,0:T(8,128)(2,1)S(1)} %fusion.6), channel_id=1, source_target_pairs={{0,8},{4,12},{24,16},{28,20},{1,9},{5,13},{25,17},{29,21},{2,10},{... | collective-permute-start | bytes 1572872 | tf_op jit(solution)/shard_map/ppermute | solution.py:498
  146.2 7.0 %collective-permute-done.28 = bf16[256,1024]{1,0:T(8,128)(2,1)S(1)} collective-permute-done((bf16[256,1024]{1,0:T(8,128)(2,1)S(1)}, bf16[256,1024]{1,0:T(8,128)(2,1)S(1)}, u32[]{:S(2)}, u32[]{:S(2)}) %collective-permute-start.28) | collective-permute-done | bytes 524320 | tf_op jit(solution)/shard_map/ppermute | solution.py:498
  159.2 5.3 %collective-permute-done.33 = bf16[256,1024]{1,0:T(8,128)(2,1)S(1)} collective-permute-done((bf16[256,1024]{1,0:T(8,128)(2,1)S(1)}, bf16[256,1024]{1,0:T(8,128)(2,1)S(1)}, u32[]{:S(2)}, u32[]{:S(2)}) %collective-permute-start.33) | collective-permute-done | bytes 524320 | tf_op jit(solution)/shard_map/ppermute | solution.py:498
  167.6 2.5 %collective-permute-start.32 = (bf16[256,1024]{1,0:T(8,128)(2,1)S(1)}, bf16[256,1024]{1,0:T(8,128)(2,1)S(1)}, u32[]{:S(2)}, u32[]{:S(2)}) collective-permute-start(bf16[256,1024]{1,0:T(8,128)(2,1)S(1)} %fusion.5), channel_id=1, source_target_pairs={{0,8},{4,12},{8,0},{12,4},{16,24},{20,28},{24,16},{28,20},{1,9},{5... | collective-permute-start | bytes 1572872 | tf_op jit(solution)/shard_map/ppermute | solution.py:498
  172.7 3.0 %collective-permute-done.27 = bf16[256,1024]{1,0:T(8,128)(2,1)S(1)} collective-permute-done((bf16[256,1024]{1,0:T(8,128)(2,1)S(1)}, bf16[256,1024]{1,0:T(8,128)(2,1)S(1)}, u32[]{:S(2)}, u32[]{:S(2)}) %collective-permute-start.27) | collective-permute-done | bytes 524320 | tf_op jit(solution)/shard_map/ppermute | solution.py:498
  176.6 7.5 %collective-permute-done.32 = bf16[256,1024]{1,0:T(8,128)(2,1)S(1)} collective-permute-done((bf16[256,1024]{1,0:T(8,128)(2,1)S(1)}, bf16[256,1024]{1,0:T(8,128)(2,1)S(1)}, u32[]{:S(2)}, u32[]{:S(2)}) %collective-permute-start.32) | collective-permute-done | bytes 524320 | tf_op jit(solution)/shard_map/ppermute | solution.py:498
  (101 shorter events, 62.2 us)
Async XLA Ops:
  6.3 65.8 %collective-permute-start.7 = (bf16[512,2048]{1,0:T(8,128)(2,1)}, bf16[512,2048]{1,0:T(8,128)(2,1)}, u32[]{:S(2)}, u32[]{:S(2)}) collective-permute-start(bf16[512,2048]{1,0:T(8,128)(2,1)} %slice_select_fusion), channel_id=1, source_target_pairs={{0,4},{4,0},{8,12},{12,8},{16,20},{20,16},{24,28},{28,24},{1,5},{5... | collective-permute-start | bytes 6291464 | tf_op jit(solution)/shard_map/ppermute | solution.py:495
  6.6 16.0 %collective-permute-start.10 = (bf16[256,1024]{1,0:T(8,128)(2,1)S(1)}, bf16[256,1024]{1,0:T(8,128)(2,1)}, u32[]{:S(2)}, u32[]{:S(2)}) collective-permute-start(bf16[256,1024]{1,0:T(8,128)(2,1)S(1)} %maximum_select_fusion.2.refs_0_.refs_2_), channel_id=1, source_target_pairs={{8,0},{12,4},{0,8},{4,12},{24,16},{28,20},{16,24},{20,28},{9,1},{1... | collective-permute-start | bytes 1572872 | tf_op jit(solution)/shard_map/ppermute | solution.py:498
  9.7 29.3 %collective-permute-start.6 = (bf16[512,1024]{1,0:T(8,128)(2,1)}, bf16[512,1024]{1,0:T(8,128)(2,1)}, u32[]{:S(2)}, u32[]{:S(2)}) collective-permute-start(bf16[512,1024]{1,0:T(8,128)(2,1)} %param.4), channel_id=1, source_target_pairs={{0,4},{4,0},{8,12},{12,8},{16,20},{20,16},{24,28},{28,24},{1,5},{5... | collective-permute-start | bytes 3145736 | tf_op jit(solution)/shard_map/ppermute | solution.py:495
  11.2 12.0 %collective-permute-start.13 = (bf16[256,1024]{1,0:T(8,128)(2,1)S(1)}, bf16[256,1024]{1,0:T(8,128)(2,1)}, u32[]{:S(2)}, u32[]{:S(2)}) collective-permute-start(bf16[256,1024]{1,0:T(8,128)(2,1)S(1)} %maximum_select_fusion.2.refs_0_.refs_2_), channel_id=1, source_target_pairs={{16,8},{20,12},{8,16},{12,20},{17,9},{21,13},{9,17},{13,21},{18,10... | collective-permute-start | bytes 1572872 | tf_op jit(solution)/shard_map/ppermute | solution.py:498
  12.8 20.3 %collective-permute-start.1 = (bf16[256,1024]{1,0:T(8,128)(2,1)S(1)}, bf16[256,1024]{1,0:T(8,128)(2,1)}, u32[]{:S(2)}, u32[]{:S(2)}) collective-permute-start(bf16[256,1024]{1,0:T(8,128)(2,1)S(1)} %maximum_select_fusion.1.refs_0_.refs_8_), channel_id=1, source_target_pairs={{8,0},{12,4},{0,8},{4,12},{24,16},{28,20},{16,24},{20,28},{9,1},{1... | collective-permute-start | bytes 1572872 | tf_op jit(solution)/shard_map/ppermute | solution.py:498
  22.6 12.0 %collective-permute-start.4 = (bf16[256,1024]{1,0:T(8,128)(2,1)S(1)}, bf16[256,1024]{1,0:T(8,128)(2,1)S(1)}, u32[]{:S(2)}, u32[]{:S(2)}) collective-permute-start(bf16[256,1024]{1,0:T(8,128)(2,1)S(1)} %maximum_select_fusion.1.refs_0_.refs_8_), channel_id=1, source_target_pairs={{16,8},{20,12},{8,16},{12,20},{17,9},{21,13},{9,17},{13,21},{18,10... | collective-permute-start | bytes 1572872 | tf_op jit(solution)/shard_map/ppermute | solution.py:498
  23.3 18.1 %collective-permute-start.11 = (bf16[256,1024]{1,0:T(8,128)(2,1)}, bf16[256,1024]{1,0:T(8,128)(2,1)}, u32[]{:S(2)}, u32[]{:S(2)}) collective-permute-start(bf16[256,1024]{1,0:T(8,128)(2,1)} %collective-permute-done.10.refs_1_.refs_3_), channel_id=1, source_target_pairs={{16,8},{20,12},{8,16},{12,20},{17,9},{21,13},{9,17},{13,21},{18,10... | collective-permute-start | bytes 1572872 | tf_op jit(solution)/shard_map/ppermute | solution.py:498
  35.4 21.5 %collective-permute-start.14 = (bf16[256,1024]{1,0:T(8,128)(2,1)}, bf16[256,1024]{1,0:T(8,128)(2,1)}, u32[]{:S(2)}, u32[]{:S(2)}) collective-permute-start(bf16[256,1024]{1,0:T(8,128)(2,1)} %collective-permute-done.13.refs_2_.refs_4_), channel_id=1, source_target_pairs={{8,0},{12,4},{16,24},{20,28},{9,1},{13,5},{17,25},{21,29},{10,2},{... | collective-permute-start | bytes 1572872 | tf_op jit(solution)/shard_map/ppermute | solution.py:498
  39.0 29.0 %collective-permute-start.5 = (bf16[256,1024]{1,0:T(8,128)(2,1)}, bf16[256,1024]{1,0:T(8,128)(2,1)S(1)}, u32[]{:S(2)}, u32[]{:S(2)}) collective-permute-start(bf16[256,1024]{1,0:T(8,128)(2,1)} %copy-done.1), channel_id=1, source_target_pairs={{8,0},{12,4},{16,24},{20,28},{9,1},{13,5},{17,25},{21,29},{10,2},{... | collective-permute-start | bytes 1572872 | tf_op jit(solution)/shard_map/ppermute | solution.py:498
  41.4 37.8 %collective-permute-start.12 = (bf16[256,1024]{1,0:T(8,128)(2,1)}, bf16[256,1024]{1,0:T(8,128)(2,1)S(1)}, u32[]{:S(2)}, u32[]{:S(2)}) collective-permute-start(bf16[256,1024]{1,0:T(8,128)(2,1)} %collective-permute-done.11.refs_4_.refs_6_), channel_id=1, source_target_pairs={{8,0},{12,4},{16,24},{20,28},{9,1},{13,5},{17,25},{21,29},{10,2},{... | collective-permute-start | bytes 1572872 | tf_op jit(solution)/shard_map/ppermute | solution.py:498
  42.7 46.0 %collective-permute-start.3 = (bf16[256,1024]{1,0:T(8,128)(2,1)}, bf16[256,1024]{1,0:T(8,128)(2,1)S(1)}, u32[]{:S(2)}, u32[]{:S(2)}) collective-permute-start(bf16[256,1024]{1,0:T(8,128)(2,1)} %collective-permute-done.2.refs_4_.refs_12_), channel_id=1, source_target_pairs={{8,0},{12,4},{16,24},{20,28},{9,1},{13,5},{17,25},{21,29},{10,2},{... | collective-permute-start | bytes 1572872 | tf_op jit(solution)/shard_map/ppermute | solution.py:498
  103.5 13.8 %collective-permute-start.25 = (bf16[256,1024]{1,0:T(8,128)(2,1)S(1)}, bf16[256,1024]{1,0:T(8,128)(2,1)S(1)}, u32[]{:S(2)}, u32[]{:S(2)}) collective-permute-start(bf16[256,1024]{1,0:T(8,128)(2,1)S(1)} %get-tuple-element.71), channel_id=1, source_target_pairs={{0,8},{4,12},{24,16},{28,20},{1,9},{5,13},{25,17},{29,21},{2,10},{... | collective-permute-start | bytes 1572872 | tf_op jit(solution)/shard_map/ppermute | solution.py:498
  107.6 33.3 %collective-permute-start.30 = (bf16[256,1024]{1,0:T(8,128)(2,1)S(1)}, bf16[256,1024]{1,0:T(8,128)(2,1)S(1)}, u32[]{:S(2)}, u32[]{:S(2)}) collective-permute-start(bf16[256,1024]{1,0:T(8,128)(2,1)S(1)} %get-tuple-element.60), channel_id=1, source_target_pairs={{0,8},{4,12},{24,16},{28,20},{1,9},{5,13},{25,17},{29,21},{2,10},{... | collective-permute-start | bytes 1572872 | tf_op jit(solution)/shard_map/ppermute | solution.py:498
  118.0 27.3 %collective-permute-start.26 = (bf16[256,1024]{1,0:T(8,128)(2,1)S(1)}, bf16[256,1024]{1,0:T(8,128)(2,1)S(1)}, u32[]{:S(2)}, u32[]{:S(2)}) collective-permute-start(bf16[256,1024]{1,0:T(8,128)(2,1)S(1)} %fusion.3), channel_id=1, source_target_pairs={{8,16},{12,20},{16,8},{20,12},{9,17},{13,21},{17,9},{21,13},{10,18... | collective-permute-start | bytes 1572872 | tf_op jit(solution)/shard_map/ppermute | solution.py:498
  125.6 29.1 %collective-permute-start.21 = (bf16[512,1024]{1,0:T(8,128)(2,1)S(1)}, bf16[512,1024]{1,0:T(8,128)(2,1)S(1)}, u32[]{:S(2)}, u32[]{:S(2)}) collective-permute-start(bf16[512,1024]{1,0:T(8,128)(2,1)S(1)} %slice.69), channel_id=1, source_target_pairs={{0,4},{4,0},{8,12},{12,8},{16,20},{20,16},{24,28},{28,24},{1,5},{5... | collective-permute-start | bytes 3145736 | tf_op jit(solution)/shard_map/ppermute | solution.py:495
  137.0 16.2 %collective-permute-start.28 = (bf16[256,1024]{1,0:T(8,128)(2,1)S(1)}, bf16[256,1024]{1,0:T(8,128)(2,1)S(1)}, u32[]{:S(2)}, u32[]{:S(2)}) collective-permute-start(bf16[256,1024]{1,0:T(8,128)(2,1)S(1)} %fusion.3), channel_id=1, source_target_pairs={{0,8},{4,12},{24,16},{28,20},{1,9},{5,13},{25,17},{29,21},{2,10},{... | collective-permute-start | bytes 1572872 | tf_op jit(solution)/shard_map/ppermute | solution.py:498
  141.7 15.2 %collective-permute-start.31 = (bf16[256,1024]{1,0:T(8,128)(2,1)S(1)}, bf16[256,1024]{1,0:T(8,128)(2,1)S(1)}, u32[]{:S(2)}, u32[]{:S(2)}) collective-permute-start(bf16[256,1024]{1,0:T(8,128)(2,1)S(1)} %fusion.6), channel_id=1, source_target_pairs={{8,16},{12,20},{16,8},{20,12},{9,17},{13,21},{17,9},{21,13},{10,18... | collective-permute-start | bytes 1572872 | tf_op jit(solution)/shard_map/ppermute | solution.py:498
  142.4 22.1 %collective-permute-start.33 = (bf16[256,1024]{1,0:T(8,128)(2,1)S(1)}, bf16[256,1024]{1,0:T(8,128)(2,1)S(1)}, u32[]{:S(2)}, u32[]{:S(2)}) collective-permute-start(bf16[256,1024]{1,0:T(8,128)(2,1)S(1)} %fusion.6), channel_id=1, source_target_pairs={{0,8},{4,12},{24,16},{28,20},{1,9},{5,13},{25,17},{29,21},{2,10},{... | collective-permute-start | bytes 1572872 | tf_op jit(solution)/shard_map/ppermute | solution.py:498
  146.1 29.6 %collective-permute-start.27 = (bf16[256,1024]{1,0:T(8,128)(2,1)S(1)}, bf16[256,1024]{1,0:T(8,128)(2,1)S(1)}, u32[]{:S(2)}, u32[]{:S(2)}) collective-permute-start(bf16[256,1024]{1,0:T(8,128)(2,1)S(1)} %fusion.2), channel_id=1, source_target_pairs={{0,8},{4,12},{8,0},{12,4},{16,24},{20,28},{24,16},{28,20},{1,9},{5... | collective-permute-start | bytes 1572872 | tf_op jit(solution)/shard_map/ppermute | solution.py:498
  154.0 21.7 %collective-permute-start.29 = (bf16[256,1024]{1,0:T(8,128)(2,1)S(1)}, bf16[256,1024]{1,0:T(8,128)(2,1)S(1)}, u32[]{:S(2)}, u32[]{:S(2)}) collective-permute-start(bf16[256,1024]{1,0:T(8,128)(2,1)S(1)} %fusion.4), channel_id=1, source_target_pairs={{8,16},{12,20},{16,8},{20,12},{9,17},{13,21},{17,9},{21,13},{10,18... | collective-permute-start | bytes 1572872 | tf_op jit(solution)/shard_map/ppermute | solution.py:498
  155.4 12.3 %collective-permute-start.22 = (bf16[512,256]{1,0:T(8,128)(2,1)S(1)}, bf16[512,256]{1,0:T(8,128)(2,1)S(1)}, u32[]{:S(2)}, u32[]{:S(2)}) collective-permute-start(bf16[512,256]{1,0:T(8,128)(2,1)S(1)} %get-tuple-element.73), channel_id=1, source_target_pairs={{0,1},{1,0},{2,3},{3,2},{4,5},{5,4},{6,7},{7,6},{8,9},{9,8},{10,11... | collective-permute-start | bytes 786440 | tf_op jit(solution)/shard_map/ppermute | solution.py:503
  156.9 13.3 %collective-permute-start.23 = (bf16[512,256]{1,0:T(8,128)(2,1)S(1)}, bf16[512,256]{1,0:T(8,128)(2,1)S(1)}, u32[]{:S(2)}, u32[]{:S(2)}) collective-permute-start(bf16[512,256]{1,0:T(8,128)(2,1)S(1)} %get-tuple-element.75), channel_id=1, source_target_pairs={{0,2},{1,3},{2,0},{3,1},{4,6},{5,7},{6,4},{7,5},{8,10},{9,11},{10,... | collective-permute-start | bytes 786440 | tf_op jit(solution)/shard_map/ppermute | solution.py:503
  167.6 16.5 %collective-permute-start.32 = (bf16[256,1024]{1,0:T(8,128)(2,1)S(1)}, bf16[256,1024]{1,0:T(8,128)(2,1)S(1)}, u32[]{:S(2)}, u32[]{:S(2)}) collective-permute-start(bf16[256,1024]{1,0:T(8,128)(2,1)S(1)} %fusion.5), channel_id=1, source_target_pairs={{0,8},{4,12},{8,0},{12,4},{16,24},{20,28},{24,16},{28,20},{1,9},{5... | collective-permute-start | bytes 1572872 | tf_op jit(solution)/shard_map/ppermute | solution.py:498
  170.2 13.9 %collective-permute-start.34 = (bf16[256,1024]{1,0:T(8,128)(2,1)S(1)}, bf16[256,1024]{1,0:T(8,128)(2,1)S(1)}, u32[]{:S(2)}, u32[]{:S(2)}) collective-permute-start(bf16[256,1024]{1,0:T(8,128)(2,1)S(1)} %fusion.7), channel_id=1, source_target_pairs={{8,16},{12,20},{16,8},{20,12},{9,17},{13,21},{17,9},{21,13},{10,18... | collective-permute-start | bytes 1572872 | tf_op jit(solution)/shard_map/ppermute | solution.py:498
  (17 other events, 91.7 us)

commit v6 on v5

--- a/solution.py
+++ b/solution.py
@@ -337,70 +337,65 @@
     )(*map(near, rows))
 
 
-def slope_kernel(part, peers, idx_ref, *refs):
-    step = pl.program_id(0)
+def slope_kernel(part, peers, tile, idx_ref, *refs):
     if peers:
         tops_ref = refs[peers]
         ez_ref, et_ref, ht_ref = refs[peers + 1:peers + 4]
         slope_ref, msg_ref, coef_ref, loss_ref = refs[peers + 4:]
 
-        @pl.when(step == 0)
-        def _():
-            got = [r[...] for r in refs[:peers]]
-            while len(got) > 1:
-                got = [fold_rows(got[j], got[j + 1]) for j in range(0, len(got), 2)]
-            s = got[0]
-            t_inv = 1.0 / s[1:2]
-            lse_t = s[0:1] + jnp.log(s[1:2])
-            lse_z = s[3:4] + jnp.log(s[4:5])
-            n = s.shape[1]
-            per_token = s[2:3] * t_inv - lse_t + (1.0 + ce_weight) * lse_z - ce_weight * s[5:6]
-            plane = jnp.sum(per_token[:, :n // 2], axis=1, keepdims=True) + jnp.sum(
-                per_token[:, n // 2:], axis=1, keepdims=True
-            )
-            loss_ref[...] = jnp.broadcast_to(plane, loss_ref.shape)
-            z_inv = (1.0 + ce_weight) / s[4:5]
-            tops = tops_ref[...]
-            rows = [jnp.exp(tops[0:1] - s[0:1]) * t_inv]
-            rows += [jnp.exp(tops[p + 1:p + 2] - s[3:4]) * z_inv for p in range(PARTS)]
-            rows += [tops[PARTS + 1:PARTS + 2]]
-            rows += [jnp.zeros((128 - len(rows), n), f32)]
-            coef_ref[...] = jnp.concatenate(rows).T
+        got = [r[...] for r in refs[:peers]]
+        while len(got) > 1:
+            got = [fold_rows(got[j], got[j + 1]) for j in range(0, len(got), 2)]
+        s = got[0]
+        t_inv = 1.0 / s[1:2]
+        lse_t = s[0:1] + jnp.log(s[1:2])
+        lse_z = s[3:4] + jnp.log(s[4:5])
+        n = s.shape[1]
+        per_token = s[2:3] * t_inv - lse_t + (1.0 + ce_weight) * lse_z - ce_weight * s[5:6]
+        plane = jnp.sum(per_token[:, :n // 2], axis=1, keepdims=True) + jnp.sum(
+            per_token[:, n // 2:], axis=1, keepdims=True
+        )
+        loss_ref[...] = jnp.broadcast_to(plane, loss_ref.shape)
+        z_inv = (1.0 + ce_weight) / s[4:5]
+        tops = tops_ref[...]
+        rows = [jnp.exp(tops[0:1] - s[0:1]) * t_inv]
+        rows += [jnp.exp(tops[p + 1:p + 2] - s[3:4]) * z_inv for p in range(PARTS)]
+        rows += [tops[PARTS + 1:PARTS + 2]]
+        rows += [jnp.zeros((128 - len(rows), n), f32)]
+        coef_ref[...] = jnp.concatenate(rows).T
 
     else:
         coef_ref, ez_ref, et_ref, ht_ref, slope_ref, msg_ref = refs
     b = coef_ref[:, 0:1]
     a = coef_ref[:, part + 1:part + 2]
-    piece = ez_ref.shape[1]
-    tile = piece // pl.num_programs(0)
-    first = pl.multiple_of(step * tile, tile)
-    at = pl.ds(first, tile)
-    e_t = et_ref[:, pl.ds(pl.multiple_of(part * piece + first, tile), tile)]
-    value = ez_ref[:, at].astype(f32) * a - e_t.astype(f32) * b
-    column = lax.broadcasted_iota(jnp.int32, value.shape, 1)
-    id_col = coef_ref[:, PARTS + 1:PARTS + 2].astype(jnp.int32) - (part * piece + first)
-    value = jnp.where(column == id_col, value - ce_weight, value)
-    slope = value.astype(bf16)
-    slope_ref[:, at] = slope
-    deep = msg_ref.shape[0]
+    id_col = coef_ref[:, PARTS + 1:PARTS + 2].astype(jnp.int32)
+    deep, piece = msg_ref.shape
     rows = pl.ds(pl.multiple_of(idx_ref[0] * deep, deep), deep)
-    msg_ref[...] = dot(ht_ref[rows, :], slope).astype(bf16)
+    for first in range(0, piece, tile):
+        at = slice(first, first + tile)
+        e_t = et_ref[:, part * piece + first:part * piece + first + tile]
+        value = ez_ref[:, at].astype(f32) * a - e_t.astype(f32) * b
+        column = lax.broadcasted_iota(jnp.int32, value.shape, 1) + (part * piece + first)
+        value = jnp.where(column == id_col, value - ce_weight, value)
+        slope = value.astype(bf16)
+        slope_ref[:, at] = slope
+        msg_ref[:, at] = dot(ht_ref[rows, :], slope).astype(bf16)
 
 
 def slope_call(part, index, head_args, e_z, e_t, hid_t, deep, tile):
     n, piece = e_z.shape
     peers = len(head_args) - 1
-    out_specs = [WHOLE, pl.BlockSpec((deep, tile), lambda i, s: (0, i))]
-    out_shape = [out((n, piece), bf16), jax.ShapeDtypeStruct((deep, piece), bf16)]
+    out_specs = [WHOLE, WHOLE]
+    out_shape = [out((n, piece), bf16), out((deep, piece), bf16)]
     if peers:
         out_specs += [WHOLE, WHOLE]
         out_shape += [out((n, 128), f32), out((8, 128), f32)]
     args = [*head_args, e_z, e_t, hid_t]
     return pl.pallas_call(
-        functools.partial(slope_kernel, part, peers),
+        functools.partial(slope_kernel, part, peers, tile),
         grid_spec=pltpu.PrefetchScalarGridSpec(
             num_scalar_prefetch=1,
-            grid=(piece // tile,),
+            grid=(1,),
             in_specs=[WHOLE] * len(args),
             out_specs=out_specs,
         ),
@@ -447,7 +442,7 @@
     piece = half // PARTS
     deep = 2 * own_rows
     tile = min(256, rows)
-    wide = min(512, piece)
+    wide = min(256, piece)
     me = lax.axis_index("tok")
     core = lax.rem(me, 2)
     z = lax.div(me, 2)
@@ -485,9 +480,11 @@
     row_of = {k: v * deep for k, v in row_of.items()}
     col_of = [(voc ^ v) * width for v in range(n_voc)]
     vocab_start = voc * share + core * half
-    (even, first_chip, ahead, row_of, col_of, vocab_start), head, hidden, logits, ids = (
+    keep_cols = [core * half + p * piece for p in range(PARTS)]
+    send_cols = [(1 - core) * half + p * piece for p in range(PARTS)]
+    (even, first_chip, ahead, row_of, col_of, vocab_start, keep_cols, send_cols), head, hidden, logits, ids = (
         lax.optimization_barrier(
-            ((even, first_chip, ahead, row_of, col_of, vocab_start), head, hidden, logits, ids)
+            ((even, first_chip, ahead, row_of, col_of, vocab_start, keep_cols, send_cols), head, hidden, logits, ids)
         )
     )
 
@@ -495,28 +492,25 @@
         return lax.ppermute(x, "tok", [(i, i ^ 1) for i in range(n_tok)])
 
     def hop(x, pairs):
-        return lax.ppermute(
-            x, "tok", [(2 * a + k, 2 * b + k) for a, b in pairs for k in range(2)]
-        )
+        return lax.ppermute(x, "tok", [(2 * a + k, 2 * b + k) for a, b in pairs for k in range(2)])
 
     def plane_swap(x, v):
         return lax.ppermute(x, "voc", [(w, w ^ v) for w in range(n_voc)])
+
+    def cut(x, row, col, shape):
+        row, col = (jnp.asarray(i, jnp.int32) for i in (row, col))
+        return lax.dynamic_slice(x, (row, col), shape, allow_negative_indices=False)
 
     def mine(x, other=False):
         left, right = x[:, :half], x[:, half:]
         return jnp.where(even, right, left) if other else jnp.where(even, left, right)
 
-    keep, send = mine(head), mine(head, True)
     blocks = []
     for p in range(PARTS):
-        cut = slice(p * piece, (p + 1) * piece)
-        other = swap(send[:, cut])
+        keep, send = (cut(head, 0, c[p], (own_rows, piece)) for c in (keep_cols, send_cols))
+        other = swap(send)
         blocks.append(
-            jnp.where(
-                even,
-                jnp.concatenate([keep[:, cut], other]),
-                jnp.concatenate([other, keep[:, cut]]),
-            )
+            jnp.where(even, jnp.concatenate([keep, other]), jnp.concatenate([other, keep]))
         )
 
     came = [{("own", 0): b, ("even", 0): b, ("odd", 0): b} for b in blocks]
@@ -563,15 +557,13 @@
     msgs, slope = [], []
     for p in range(PARTS):
         head_args = got + [tops] if p == 0 else [coef]
-        outs = slope_call(p, ahead["first"], head_args, e_z[p], e_t, hid_t, deep, wide)
+        outs = slope_call(
+            p, ahead["first"], head_args, e_z[p], e_t, hid_t, deep, wide
+        )
         slope.append(outs[0])
         msgs.append(outs[1])
         if p == 0:
             coef, plane = outs[2:]
-
-    def cut(x, row, col, shape):
-        row, col = (jnp.asarray(i, jnp.int32) for i in (row, col))
-        return lax.dynamic_slice(x, (row, col), shape, allow_negative_indices=False)
 
     def grad_rows(way, s, p):
         return dot(cut(hid_t, row_of[way, s], 0, (deep, 2 * rows)), slope[p])

time: 189 us -> 189 us (level)
  transfers between devices with their start and end apart: 37 -> 37, of which waited for: 20 -> 20; matrix products, arithmetic and copies ran while one was open for 9% -> 9% of each run, Pallas kernels for 14% -> 13%
where the time goes in v6:
time: 189 us; the launch traced here: 188 us
  waiting for transfers between devices  84.9 us (45%)
  starting transfers between devices  51 us (27%)
  Pallas kernels  29.9 us (16%)
  other arithmetic  8.33 us (4%)
  local copies, waits for them, and re-layouts  7.17 us (4%)
  matrix products  5.79 us (3%)
    ppermute x23, waiting for transfers between devices, hop(): lax.ppermute(x, 'tok', [(2 * a + k, 2 * b + k) for a, b in pairs for k in...  76.3 us
    ppermute x23, starting transfers between devices, hop(): lax.ppermute(x, 'tok', [(2 * a + k, 2 * b + k) for a, b in pairs for k in...  40.9 us
    ppermute x5, starting transfers between devices, plane_swap(): return lax.ppermute(x, 'voc', [(w, w ^ v) for w in range(n_voc)])  8.68 us
    pallas_call x2, Pallas kernels, early_call(): pl.pallas_call(functools.partial(early_kernel, nz, len(blocks)), grid_spe...  8.26 us
    pallas_call x1, Pallas kernels, hidden_call(): pl.pallas_call(functools.partial(hidden_kernel, nz, count), grid_spec=plt...  6.74 us
    dot_general x8, matrix products, dot(): lax.dot_general(a, b, (((1,), (0,)), ((), ())), preferred_element_type=f32)  5.79 us
    pallas_call x2, Pallas kernels, last_call(): pl.pallas_call(functools.partial(last_kernel, part, len(stats), tile), gr...  5.25 us
    ppermute x5, waiting for transfers between devices, plane_swap(): return lax.ppermute(x, 'voc', [(w, w ^ v) for w in range(n_voc)])  5.03 us
  transfers between devices with their start and end apart: 37, of which 20 were waited for; matrix products, arithmetic and copies ran while one was open for 9% of the time, Pallas kernels for 13%

profile of v6, /device:TPU:0, one launch (start us, length us, event | category | flops | bytes accessed | tf_op | source)
XLA Modules:
  0.0 188.3 jit_solution(12756090765878308328)
XLA Ops:
  3.1 3.8 %slice_select_fusion = bf16[512,2048]{1,0:T(8,128)(2,1)} fusion(bf16[512,4096]{1,0:T(8,128)(2,1)} %mine_ref, pred[]{:T(512)S(6)} %eq.8), kind=kLoop, calls=%fused_computation.2 | loop fusion | flops 1048576 | bytes 6291457 | tf_op jit(solution)/shard_map/jit(_where)/select_n | solution.py:506
  7.1 3.1 %collective-permute-start.10 = (bf16[256,1024]{1,0:T(8,128)(2,1)S(1)}, bf16[256,1024]{1,0:T(8,128)(2,1)}, u32[]{:S(2)}, u32[]{:S(2)}) collective-permute-start(bf16[256,1024]{1,0:T(8,128)(2,1)S(1)} %maximum_select_fusion.2.refs_0_.refs_2_), channel_id=1, source_target_pairs={{8,0},{12,4},{0,8},{4,12},{24,16},{28,20},{16,24},{20,28},{9,1},{1... | collective-permute-start | bytes 1572872 | tf_op jit(solution)/shard_map/ppermute | solution.py:495
  13.4 4.7 %collective-permute-start.1 = (bf16[256,1024]{1,0:T(8,128)(2,1)S(1)}, bf16[256,1024]{1,0:T(8,128)(2,1)}, u32[]{:S(2)}, u32[]{:S(2)}) collective-permute-start(bf16[256,1024]{1,0:T(8,128)(2,1)S(1)} %maximum_select_fusion.1.refs_0_.refs_8_), channel_id=1, source_target_pairs={{8,0},{12,4},{0,8},{4,12},{24,16},{28,20},{16,24},{20,28},{9,1},{1... | collective-permute-start | bytes 1572872 | tf_op jit(solution)/shard_map/ppermute | solution.py:495
  18.0 5.0 %collective-permute-done.10.refs_1_.refs_3_ = bf16[256,1024]{1,0:T(8,128)(2,1)} collective-permute-done((bf16[256,1024]{1,0:T(8,128)(2,1)S(1)}, bf16[256,1024]{1,0:T(8,128)(2,1)}, u32[]{:S(2)}, u32[]{:S(2)}) %collective-permute-start.10) | collective-permute-done | bytes 524320 | tf_op jit(solution)/shard_map/ppermute | solution.py:495
  25.3 8.4 %collective-permute-done.1.refs_1_.refs_9_ = bf16[256,1024]{1,0:T(8,128)(2,1)} collective-permute-done((bf16[256,1024]{1,0:T(8,128)(2,1)S(1)}, bf16[256,1024]{1,0:T(8,128)(2,1)}, u32[]{:S(2)}, u32[]{:S(2)}) %collective-permute-start.1) | collective-permute-done | bytes 524320 | tf_op jit(solution)/shard_map/ppermute | solution.py:495
  46.0 11.4 %collective-permute-done.14.refs_3_.refs_5_ = bf16[256,1024]{1,0:T(8,128)(2,1)} collective-permute-done((bf16[256,1024]{1,0:T(8,128)(2,1)}, bf16[256,1024]{1,0:T(8,128)(2,1)}, u32[]{:S(2)}, u32[]{:S(2)}) %collective-permute-start.14) | collective-permute-done | bytes 524320 | tf_op jit(solution)/shard_map/ppermute | solution.py:495
  57.4 4.1 %early_draft.3.refs_1_ = f32[1024,1024]{1,0:T(8,128)S(1)} custom-call(s32[1]{0:T(128)} %bitcast.3.z_ref, bf16[256,1024]{1,0:T(8,128)(2,1)S(1)} %maximum_select_fusion.2.refs_0_.refs_2_, bf16[256,1024]{1,0:T(8,128)(2,1)} %collective-permute-done.10.refs_1_.refs_3_, bf16[256,1024]{1,0:T(8,128)(2,1)} %collective-permute-done.13.refs_2_.refs_4_, ...), custom_call_target="tpu_custom_call" | custom-call | flops 2147483648 | bytes 6291456 | tf_op jit(solution)/shard_map/early_draft/pallas_call | solution.py:172
  61.6 7.0 %collective-permute-done.5.refs_3_.refs_11_ = bf16[256,1024]{1,0:T(8,128)(2,1)S(1)} collective-permute-done((bf16[256,1024]{1,0:T(8,128)(2,1)}, bf16[256,1024]{1,0:T(8,128)(2,1)S(1)}, u32[]{:S(2)}, u32[]{:S(2)}) %collective-permute-start.5) | collective-permute-done | bytes 524320 | tf_op jit(solution)/shard_map/ppermute | solution.py:495
  68.5 4.1 %early_draft.2.refs_1_ = f32[1024,1024]{1,0:T(8,128)S(1)} custom-call(s32[1]{0:T(128)} %bitcast.3.z_ref, bf16[256,1024]{1,0:T(8,128)(2,1)S(1)} %maximum_select_fusion.1.refs_0_.refs_8_, bf16[256,1024]{1,0:T(8,128)(2,1)} %collective-permute-done.1.refs_1_.refs_9_, bf16[256,1024]{1,0:T(8,128)(2,1)S(1)} %copy-done.2, ...), custom_call_target="tpu_custom_call" | custom-call | flops 2147483648 | bytes 6291456 | tf_op jit(solution)/shard_map/early_draft/pallas_call | solution.py:172
  72.7 5.0 %target_exps.1 = (bf16[1024,2048]{1,0:T(8,128)(2,1)S(1)}, f32[1024,128]{1,0:T(8,128)S(1)}) custom-call(s32[1]{0:T(128)} %bitcast.core_ref, bf16[512,4096]{1,0:T(8,128)(2,1)S(1)} %copy-done, bf16[512,2048]{1,0:T(8,128)(2,1)} %collective-permute-done.7.came_ref, s32[1024,1]{1,0:T(8,128)S(1)} %broadcast_subtract_fusion.id_ref), custom_call_target="tpu_custom_call" | custom-call | flops 16777216 | bytes 8388608 | tf_op jit(solution)/shard_map/target_exps/pallas_call | solution.py:85
  79.8 2.5 %last_draft.2 = (bf16[1024,1024]{1,0:T(8,128)(2,1)S(1)}, f32[1024,128]{1,0:T(8,128)S(1)}) custom-call(s32[1]{0:T(128)} %bitcast.2.at_ref, bf16[256,1024]{1,0:T(8,128)(2,1)S(1)} %collective-permute-done.12.refs_0_.refs_7_, f32[1024,1024]{1,0:T(8,128)S(1)} %early_draft.3.refs_1_, ...), custom_call_target="tpu_custom_call" | custom-call | flops 536870912 | bytes 8388608 | tf_op jit(solution)/shard_map/last_draft/pallas_call | solution.py:244
  82.3 7.0 %collective-permute-done.3.refs_0_.refs_13_ = bf16[256,1024]{1,0:T(8,128)(2,1)S(1)} collective-permute-done((bf16[256,1024]{1,0:T(8,128)(2,1)}, bf16[256,1024]{1,0:T(8,128)(2,1)S(1)}, u32[]{:S(2)}, u32[]{:S(2)}) %collective-permute-start.3) | collective-permute-done | bytes 524320 | tf_op jit(solution)/shard_map/ppermute | solution.py:495
  89.3 2.8 %last_draft.3 = (bf16[1024,1024]{1,0:T(8,128)(2,1)S(1)}, f32[8,1024]{1,0:T(8,128)S(1)}, f32[8,1024]{1,0:T(8,128)S(1)}, f32[8,1024]{1,0:T(8,128)S(1)}) custom-call(s32[1]{0:T(128)} %bitcast.2.at_ref, bf16[256,1024]{1,0:T(8,128)(2,1)S(1)} %collective-permute-done.3.refs_0_.refs_13_, f32[1024,1024]{1,0:T(8,128)S(1)} %early_draft.2.refs_1_, ...), custom_call_target="tpu_custom_call" | custom-call | flops 536870912 | bytes 8388608 | tf_op jit(solution)/shard_map/last_draft/pallas_call | solution.py:244
  108.1 9.1 %collective-permute-done.25 = bf16[256,1024]{1,0:T(8,128)(2,1)S(1)} collective-permute-done((bf16[256,1024]{1,0:T(8,128)(2,1)S(1)}, bf16[256,1024]{1,0:T(8,128)(2,1)S(1)}, u32[]{:S(2)}, u32[]{:S(2)}) %collective-permute-start.25) | collective-permute-done | bytes 524320 | tf_op jit(solution)/shard_map/ppermute | solution.py:495
  118.9 6.7 %hidden_grad.1 = bf16[1024,1024]{1,0:T(8,128)(2,1)S(1)} custom-call(s32[1]{0:T(128)} %bitcast.3.z_ref, bf16[1024,1024]{1,0:T(8,128)(2,1)S(1)} %get-tuple-element.70.refs_0_, bf16[1024,1024]{1,0:T(8,128)(2,1)S(1)} %get-tuple-element.71.refs_1_, bf16[256,1024]{1,0:T(8,128)(2,1)S(1)} %maximum_select_fusion.2.refs_0_.refs_2_, ...), custom_call_target="tpu_custom_call" | custom-call | flops 4294967296 | bytes 8388608 | tf_op jit(solution)/shard_map/hidden_grad/pallas_call | solution.py:286
  125.8 5.6 %collective-permute-start.18 = (f32[8,128]{1,0:T(8,128)S(1)}, f32[8,128]{1,0:T(8,128)S(1)}, u32[]{:S(2)}, u32[]{:S(2)}) collective-permute-start(f32[8,128]{1,0:T(8,128)S(1)} %get-tuple-element.69.refs_0_), channel_id=1, source_target_pairs={{0,8},{4,12},{8,16},{12,20},{16,24},{20,28},{24,0},{28,4},{1,9},{5... | collective-permute-start | bytes 12296 | tf_op jit(solution)/shard_map/ppermute | solution.py:495
  137.2 3.9 %collective-permute-start.28 = (bf16[256,1024]{1,0:T(8,128)(2,1)S(1)}, bf16[256,1024]{1,0:T(8,128)(2,1)S(1)}, u32[]{:S(2)}, u32[]{:S(2)}) collective-permute-start(bf16[256,1024]{1,0:T(8,128)(2,1)S(1)} %fusion.3), channel_id=1, source_target_pairs={{0,8},{4,12},{24,16},{28,20},{1,9},{5,13},{25,17},{29,21},{2,10},{... | collective-permute-start | bytes 1572872 | tf_op jit(solution)/shard_map/ppermute | solution.py:495
  142.5 3.0 %collective-permute-start.33 = (bf16[256,1024]{1,0:T(8,128)(2,1)S(1)}, bf16[256,1024]{1,0:T(8,128)(2,1)S(1)}, u32[]{:S(2)}, u32[]{:S(2)}) collective-permute-start(bf16[256,1024]{1,0:T(8,128)(2,1)S(1)} %fusion.6), channel_id=1, source_target_pairs={{0,8},{4,12},{24,16},{28,20},{1,9},{5,13},{25,17},{29,21},{2,10},{... | collective-permute-start | bytes 1572872 | tf_op jit(solution)/shard_map/ppermute | solution.py:495
  146.3 7.0 %collective-permute-done.28 = bf16[256,1024]{1,0:T(8,128)(2,1)S(1)} collective-permute-done((bf16[256,1024]{1,0:T(8,128)(2,1)S(1)}, bf16[256,1024]{1,0:T(8,128)(2,1)S(1)}, u32[]{:S(2)}, u32[]{:S(2)}) %collective-permute-start.28) | collective-permute-done | bytes 524320 | tf_op jit(solution)/shard_map/ppermute | solution.py:495
  159.3 5.3 %collective-permute-done.33 = bf16[256,1024]{1,0:T(8,128)(2,1)S(1)} collective-permute-done((bf16[256,1024]{1,0:T(8,128)(2,1)S(1)}, bf16[256,1024]{1,0:T(8,128)(2,1)S(1)}, u32[]{:S(2)}, u32[]{:S(2)}) %collective-permute-start.33) | collective-permute-done | bytes 524320 | tf_op jit(solution)/shard_map/ppermute | solution.py:495
  164.6 2.5 %collective-permute-start.24 = (bf16[512,256]{1,0:T(8,128)(2,1)S(1)}, bf16[512,256]{1,0:T(8,128)(2,1)S(1)}, u32[]{:S(2)}, u32[]{:S(2)}) collective-permute-start(bf16[512,256]{1,0:T(8,128)(2,1)S(1)} %get-tuple-element.82), channel_id=1, source_target_pairs={{0,3},{1,2},{2,1},{3,0},{4,7},{5,6},{6,5},{7,4},{8,11},{9,10},{10,... | collective-permute-start | bytes 786440 | tf_op jit(solution)/shard_map/ppermute | solution.py:498
  167.8 2.5 %collective-permute-start.32 = (bf16[256,1024]{1,0:T(8,128)(2,1)S(1)}, bf16[256,1024]{1,0:T(8,128)(2,1)S(1)}, u32[]{:S(2)}, u32[]{:S(2)}) collective-permute-start(bf16[256,1024]{1,0:T(8,128)(2,1)S(1)} %fusion.5), channel_id=1, source_target_pairs={{0,8},{4,12},{8,0},{12,4},{16,24},{20,28},{24,16},{28,20},{1,9},{5... | collective-permute-start | bytes 1572872 | tf_op jit(solution)/shard_map/ppermute | solution.py:495
  172.9 3.0 %collective-permute-done.27 = bf16[256,1024]{1,0:T(8,128)(2,1)S(1)} collective-permute-done((bf16[256,1024]{1,0:T(8,128)(2,1)S(1)}, bf16[256,1024]{1,0:T(8,128)(2,1)S(1)}, u32[]{:S(2)}, u32[]{:S(2)}) %collective-permute-start.27) | collective-permute-done | bytes 524320 | tf_op jit(solution)/shard_map/ppermute | solution.py:495
  176.7 7.5 %collective-permute-done.32 = bf16[256,1024]{1,0:T(8,128)(2,1)S(1)} collective-permute-done((bf16[256,1024]{1,0:T(8,128)(2,1)S(1)}, bf16[256,1024]{1,0:T(8,128)(2,1)S(1)}, u32[]{:S(2)}, u32[]{:S(2)}) %collective-permute-start.32) | collective-permute-done | bytes 524320 | tf_op jit(solution)/shard_map/ppermute | solution.py:495
  (99 shorter events, 62.0 us)
Async XLA Ops:
  6.9 65.8 %collective-permute-start.7 = (bf16[512,2048]{1,0:T(8,128)(2,1)}, bf16[512,2048]{1,0:T(8,128)(2,1)}, u32[]{:S(2)}, u32[]{:S(2)}) collective-permute-start(bf16[512,2048]{1,0:T(8,128)(2,1)} %slice_select_fusion), channel_id=1, source_target_pairs={{0,4},{4,0},{8,12},{12,8},{16,20},{20,16},{24,28},{28,24},{1,5},{5... | collective-permute-start | bytes 6291464 | tf_op jit(solution)/shard_map/ppermute | solution.py:492
  7.1 16.0 %collective-permute-start.10 = (bf16[256,1024]{1,0:T(8,128)(2,1)S(1)}, bf16[256,1024]{1,0:T(8,128)(2,1)}, u32[]{:S(2)}, u32[]{:S(2)}) collective-permute-start(bf16[256,1024]{1,0:T(8,128)(2,1)S(1)} %maximum_select_fusion.2.refs_0_.refs_2_), channel_id=1, source_target_pairs={{8,0},{12,4},{0,8},{4,12},{24,16},{28,20},{16,24},{20,28},{9,1},{1... | collective-permute-start | bytes 1572872 | tf_op jit(solution)/shard_map/ppermute | solution.py:495
  10.2 29.3 %collective-permute-start.6 = (bf16[512,1024]{1,0:T(8,128)(2,1)}, bf16[512,1024]{1,0:T(8,128)(2,1)}, u32[]{:S(2)}, u32[]{:S(2)}) collective-permute-start(bf16[512,1024]{1,0:T(8,128)(2,1)} %param.4), channel_id=1, source_target_pairs={{0,4},{4,0},{8,12},{12,8},{16,20},{20,16},{24,28},{28,24},{1,5},{5... | collective-permute-start | bytes 3145736 | tf_op jit(solution)/shard_map/ppermute | solution.py:492
  11.7 12.0 %collective-permute-start.13 = (bf16[256,1024]{1,0:T(8,128)(2,1)S(1)}, bf16[256,1024]{1,0:T(8,128)(2,1)}, u32[]{:S(2)}, u32[]{:S(2)}) collective-permute-start(bf16[256,1024]{1,0:T(8,128)(2,1)S(1)} %maximum_select_fusion.2.refs_0_.refs_2_), channel_id=1, source_target_pairs={{16,8},{20,12},{8,16},{12,20},{17,9},{21,13},{9,17},{13,21},{18,10... | collective-permute-start | bytes 1572872 | tf_op jit(solution)/shard_map/ppermute | solution.py:495
  13.4 20.3 %collective-permute-start.1 = (bf16[256,1024]{1,0:T(8,128)(2,1)S(1)}, bf16[256,1024]{1,0:T(8,128)(2,1)}, u32[]{:S(2)}, u32[]{:S(2)}) collective-permute-start(bf16[256,1024]{1,0:T(8,128)(2,1)S(1)} %maximum_select_fusion.1.refs_0_.refs_8_), channel_id=1, source_target_pairs={{8,0},{12,4},{0,8},{4,12},{24,16},{28,20},{16,24},{20,28},{9,1},{1... | collective-permute-start | bytes 1572872 | tf_op jit(solution)/shard_map/ppermute | solution.py:495
  23.1 12.0 %collective-permute-start.4 = (bf16[256,1024]{1,0:T(8,128)(2,1)S(1)}, bf16[256,1024]{1,0:T(8,128)(2,1)S(1)}, u32[]{:S(2)}, u32[]{:S(2)}) collective-permute-start(bf16[256,1024]{1,0:T(8,128)(2,1)S(1)} %maximum_select_fusion.1.refs_0_.refs_8_), channel_id=1, source_target_pairs={{16,8},{20,12},{8,16},{12,20},{17,9},{21,13},{9,17},{13,21},{18,10... | collective-permute-start | bytes 1572872 | tf_op jit(solution)/shard_map/ppermute | solution.py:495
  23.8 18.1 %collective-permute-start.11 = (bf16[256,1024]{1,0:T(8,128)(2,1)}, bf16[256,1024]{1,0:T(8,128)(2,1)}, u32[]{:S(2)}, u32[]{:S(2)}) collective-permute-start(bf16[256,1024]{1,0:T(8,128)(2,1)} %collective-permute-done.10.refs_1_.refs_3_), channel_id=1, source_target_pairs={{16,8},{20,12},{8,16},{12,20},{17,9},{21,13},{9,17},{13,21},{18,10... | collective-permute-start | bytes 1572872 | tf_op jit(solution)/shard_map/ppermute | solution.py:495
  35.9 21.5 %collective-permute-start.14 = (bf16[256,1024]{1,0:T(8,128)(2,1)}, bf16[256,1024]{1,0:T(8,128)(2,1)}, u32[]{:S(2)}, u32[]{:S(2)}) collective-permute-start(bf16[256,1024]{1,0:T(8,128)(2,1)} %collective-permute-done.13.refs_2_.refs_4_), channel_id=1, source_target_pairs={{8,0},{12,4},{16,24},{20,28},{9,1},{13,5},{17,25},{21,29},{10,2},{... | collective-permute-start | bytes 1572872 | tf_op jit(solution)/shard_map/ppermute | solution.py:495
  39.5 29.0 %collective-permute-start.5 = (bf16[256,1024]{1,0:T(8,128)(2,1)}, bf16[256,1024]{1,0:T(8,128)(2,1)S(1)}, u32[]{:S(2)}, u32[]{:S(2)}) collective-permute-start(bf16[256,1024]{1,0:T(8,128)(2,1)} %copy-done.1), channel_id=1, source_target_pairs={{8,0},{12,4},{16,24},{20,28},{9,1},{13,5},{17,25},{21,29},{10,2},{... | collective-permute-start | bytes 1572872 | tf_op jit(solution)/shard_map/ppermute | solution.py:495
  41.9 37.9 %collective-permute-start.12 = (bf16[256,1024]{1,0:T(8,128)(2,1)}, bf16[256,1024]{1,0:T(8,128)(2,1)S(1)}, u32[]{:S(2)}, u32[]{:S(2)}) collective-permute-start(bf16[256,1024]{1,0:T(8,128)(2,1)} %collective-permute-done.11.refs_4_.refs_6_), channel_id=1, source_target_pairs={{8,0},{12,4},{16,24},{20,28},{9,1},{13,5},{17,25},{21,29},{10,2},{... | collective-permute-start | bytes 1572872 | tf_op jit(solution)/shard_map/ppermute | solution.py:495
  43.2 46.0 %collective-permute-start.3 = (bf16[256,1024]{1,0:T(8,128)(2,1)}, bf16[256,1024]{1,0:T(8,128)(2,1)S(1)}, u32[]{:S(2)}, u32[]{:S(2)}) collective-permute-start(bf16[256,1024]{1,0:T(8,128)(2,1)} %collective-permute-done.2.refs_4_.refs_12_), channel_id=1, source_target_pairs={{8,0},{12,4},{16,24},{20,28},{9,1},{13,5},{17,25},{21,29},{10,2},{... | collective-permute-start | bytes 1572872 | tf_op jit(solution)/shard_map/ppermute | solution.py:495
  103.4 13.8 %collective-permute-start.25 = (bf16[256,1024]{1,0:T(8,128)(2,1)S(1)}, bf16[256,1024]{1,0:T(8,128)(2,1)S(1)}, u32[]{:S(2)}, u32[]{:S(2)}) collective-permute-start(bf16[256,1024]{1,0:T(8,128)(2,1)S(1)} %get-tuple-element.79), channel_id=1, source_target_pairs={{0,8},{4,12},{24,16},{28,20},{1,9},{5,13},{25,17},{29,21},{2,10},{... | collective-permute-start | bytes 1572872 | tf_op jit(solution)/shard_map/ppermute | solution.py:495
  106.8 34.3 %collective-permute-start.30 = (bf16[256,1024]{1,0:T(8,128)(2,1)S(1)}, bf16[256,1024]{1,0:T(8,128)(2,1)S(1)}, u32[]{:S(2)}, u32[]{:S(2)}) collective-permute-start(bf16[256,1024]{1,0:T(8,128)(2,1)S(1)} %get-tuple-element.68), channel_id=1, source_target_pairs={{0,8},{4,12},{24,16},{28,20},{1,9},{5,13},{25,17},{29,21},{2,10},{... | collective-permute-start | bytes 1572872 | tf_op jit(solution)/shard_map/ppermute | solution.py:495
  118.0 27.6 %collective-permute-start.26 = (bf16[256,1024]{1,0:T(8,128)(2,1)S(1)}, bf16[256,1024]{1,0:T(8,128)(2,1)S(1)}, u32[]{:S(2)}, u32[]{:S(2)}) collective-permute-start(bf16[256,1024]{1,0:T(8,128)(2,1)S(1)} %fusion.3), channel_id=1, source_target_pairs={{8,16},{12,20},{16,8},{20,12},{9,17},{13,21},{17,9},{21,13},{10,18... | collective-permute-start | bytes 1572872 | tf_op jit(solution)/shard_map/ppermute | solution.py:495
  125.7 29.1 %collective-permute-start.21 = (bf16[512,1024]{1,0:T(8,128)(2,1)S(1)}, bf16[512,1024]{1,0:T(8,128)(2,1)S(1)}, u32[]{:S(2)}, u32[]{:S(2)}) collective-permute-start(bf16[512,1024]{1,0:T(8,128)(2,1)S(1)} %slice.37), channel_id=1, source_target_pairs={{0,4},{4,0},{8,12},{12,8},{16,20},{20,16},{24,28},{28,24},{1,5},{5... | collective-permute-start | bytes 3145736 | tf_op jit(solution)/shard_map/ppermute | solution.py:492
  137.2 16.2 %collective-permute-start.28 = (bf16[256,1024]{1,0:T(8,128)(2,1)S(1)}, bf16[256,1024]{1,0:T(8,128)(2,1)S(1)}, u32[]{:S(2)}, u32[]{:S(2)}) collective-permute-start(bf16[256,1024]{1,0:T(8,128)(2,1)S(1)} %fusion.3), channel_id=1, source_target_pairs={{0,8},{4,12},{24,16},{28,20},{1,9},{5,13},{25,17},{29,21},{2,10},{... | collective-permute-start | bytes 1572872 | tf_op jit(solution)/shard_map/ppermute | solution.py:495
  141.8 15.2 %collective-permute-start.31 = (bf16[256,1024]{1,0:T(8,128)(2,1)S(1)}, bf16[256,1024]{1,0:T(8,128)(2,1)S(1)}, u32[]{:S(2)}, u32[]{:S(2)}) collective-permute-start(bf16[256,1024]{1,0:T(8,128)(2,1)S(1)} %fusion.6), channel_id=1, source_target_pairs={{8,16},{12,20},{16,8},{20,12},{9,17},{13,21},{17,9},{21,13},{10,18... | collective-permute-start | bytes 1572872 | tf_op jit(solution)/shard_map/ppermute | solution.py:495
  142.5 22.1 %collective-permute-start.33 = (bf16[256,1024]{1,0:T(8,128)(2,1)S(1)}, bf16[256,1024]{1,0:T(8,128)(2,1)S(1)}, u32[]{:S(2)}, u32[]{:S(2)}) collective-permute-start(bf16[256,1024]{1,0:T(8,128)(2,1)S(1)} %fusion.6), channel_id=1, source_target_pairs={{0,8},{4,12},{24,16},{28,20},{1,9},{5,13},{25,17},{29,21},{2,10},{... | collective-permute-start | bytes 1572872 | tf_op jit(solution)/shard_map/ppermute | solution.py:495
  146.3 29.6 %collective-permute-start.27 = (bf16[256,1024]{1,0:T(8,128)(2,1)S(1)}, bf16[256,1024]{1,0:T(8,128)(2,1)S(1)}, u32[]{:S(2)}, u32[]{:S(2)}) collective-permute-start(bf16[256,1024]{1,0:T(8,128)(2,1)S(1)} %fusion.2), channel_id=1, source_target_pairs={{0,8},{4,12},{8,0},{12,4},{16,24},{20,28},{24,16},{28,20},{1,9},{5... | collective-permute-start | bytes 1572872 | tf_op jit(solution)/shard_map/ppermute | solution.py:495
  154.1 21.7 %collective-permute-start.29 = (bf16[256,1024]{1,0:T(8,128)(2,1)S(1)}, bf16[256,1024]{1,0:T(8,128)(2,1)S(1)}, u32[]{:S(2)}, u32[]{:S(2)}) collective-permute-start(bf16[256,1024]{1,0:T(8,128)(2,1)S(1)} %fusion.4), channel_id=1, source_target_pairs={{8,16},{12,20},{16,8},{20,12},{9,17},{13,21},{17,9},{21,13},{10,18... | collective-permute-start | bytes 1572872 | tf_op jit(solution)/shard_map/ppermute | solution.py:495
  155.5 12.3 %collective-permute-start.22 = (bf16[512,256]{1,0:T(8,128)(2,1)S(1)}, bf16[512,256]{1,0:T(8,128)(2,1)S(1)}, u32[]{:S(2)}, u32[]{:S(2)}) collective-permute-start(bf16[512,256]{1,0:T(8,128)(2,1)S(1)} %get-tuple-element.81), channel_id=1, source_target_pairs={{0,1},{1,0},{2,3},{3,2},{4,5},{5,4},{6,7},{7,6},{8,9},{9,8},{10,11... | collective-permute-start | bytes 786440 | tf_op jit(solution)/shard_map/ppermute | solution.py:498
  157.1 13.3 %collective-permute-start.23 = (bf16[512,256]{1,0:T(8,128)(2,1)S(1)}, bf16[512,256]{1,0:T(8,128)(2,1)S(1)}, u32[]{:S(2)}, u32[]{:S(2)}) collective-permute-start(bf16[512,256]{1,0:T(8,128)(2,1)S(1)} %get-tuple-element.83), channel_id=1, source_target_pairs={{0,2},{1,3},{2,0},{3,1},{4,6},{5,7},{6,4},{7,5},{8,10},{9,11},{10,... | collective-permute-start | bytes 786440 | tf_op jit(solution)/shard_map/ppermute | solution.py:498
  167.8 16.5 %collective-permute-start.32 = (bf16[256,1024]{1,0:T(8,128)(2,1)S(1)}, bf16[256,1024]{1,0:T(8,128)(2,1)S(1)}, u32[]{:S(2)}, u32[]{:S(2)}) collective-permute-start(bf16[256,1024]{1,0:T(8,128)(2,1)S(1)} %fusion.5), channel_id=1, source_target_pairs={{0,8},{4,12},{8,0},{12,4},{16,24},{20,28},{24,16},{28,20},{1,9},{5... | collective-permute-start | bytes 1572872 | tf_op jit(solution)/shard_map/ppermute | solution.py:495
  170.3 13.9 %collective-permute-start.34 = (bf16[256,1024]{1,0:T(8,128)(2,1)S(1)}, bf16[256,1024]{1,0:T(8,128)(2,1)S(1)}, u32[]{:S(2)}, u32[]{:S(2)}) collective-permute-start(bf16[256,1024]{1,0:T(8,128)(2,1)S(1)} %fusion.7), channel_id=1, source_target_pairs={{8,16},{12,20},{16,8},{20,12},{9,17},{13,21},{17,9},{21,13},{10,18... | collective-permute-start | bytes 1572872 | tf_op jit(solution)/shard_map/ppermute | solution.py:495
  (17 other events, 95.8 us)

commit v7 on v6

--- a/solution.py
+++ b/solution.py
@@ -406,6 +406,44 @@
     )(index, *map(near, args))
 
 
+def finish_kernel(count, core_ref, *refs):
+    out_ref = refs[-1]
+    for k in range(2):
+
+        @pl.when(pl.program_id(0) == k)
+        def _(k=k):
+            terms = refs[k * count:(k + 1) * count]
+            out_ref[...] = sum(r[...].astype(f32) for r in terms)
+
+
+def finish_call(part, core, earlier, mine, other):
+    rows, piece = mine[0].shape
+    count = len(mine)
+    args = [near(x) for x in mine + other]
+    in_specs = [WHOLE] * len(args)
+    aliases = {}
+    if earlier is not None:
+        aliases = {1 + len(args): 0}
+        args.append(earlier)
+        in_specs.append(pl.BlockSpec(memory_space=pl.ANY))
+    return pl.pallas_call(
+        functools.partial(finish_kernel, count),
+        grid_spec=pltpu.PrefetchScalarGridSpec(
+            num_scalar_prefetch=1,
+            grid=(2,),
+            in_specs=in_specs,
+            out_specs=pl.BlockSpec(
+                (rows, piece), lambda i, s: (0, jnp.where(i == 0, s[0], 1 - s[0]) * PARTS + part)
+            ),
+        ),
+        out_shape=jax.ShapeDtypeStruct((rows, 2 * PARTS * piece), f32),
+        input_output_aliases=aliases,
+        compiler_params=params(8),
+        cost_estimate=cost(2 * rows * piece, 12 * rows * piece),
+        name="finish",
+    )(core, *args)
+
+
 def loss_kernel(scale, z_ref, *refs):
     planes, out_ref = [r[...] for r in refs[:-1]], refs[-1]
     nz = len(planes)
@@ -480,11 +518,9 @@
     row_of = {k: v * deep for k, v in row_of.items()}
     col_of = [(voc ^ v) * width for v in range(n_voc)]
     vocab_start = voc * share + core * half
-    keep_cols = [core * half + p * piece for p in range(PARTS)]
-    send_cols = [(1 - core) * half + p * piece for p in range(PARTS)]
-    (even, first_chip, ahead, row_of, col_of, vocab_start, keep_cols, send_cols), head, hidden, logits, ids = (
+    (even, first_chip, ahead, row_of, col_of, vocab_start), head, hidden, logits, ids = (
         lax.optimization_barrier(
-            ((even, first_chip, ahead, row_of, col_of, vocab_start, keep_cols, send_cols), head, hidden, logits, ids)
+            ((even, first_chip, ahead, row_of, col_of, vocab_start), head, hidden, logits, ids)
         )
     )
 
@@ -493,6 +529,11 @@
 
     def hop(x, pairs):
         return lax.ppermute(x, "tok", [(2 * a + k, 2 * b + k) for a, b in pairs for k in range(2)])
+
+    def cross_hop(x, pairs):
+        return lax.ppermute(
+            x, "tok", [(2 * a + k, 2 * b + 1 - k) for a, b in pairs for k in range(2)]
+        )
 
     def plane_swap(x, v):
         return lax.ppermute(x, "voc", [(w, w ^ v) for w in range(n_voc)])
@@ -505,12 +546,17 @@
         left, right = x[:, :half], x[:, half:]
         return jnp.where(even, right, left) if other else jnp.where(even, left, right)
 
+    keep, send = mine(head), mine(head, True)
     blocks = []
     for p in range(PARTS):
-        keep, send = (cut(head, 0, c[p], (own_rows, piece)) for c in (keep_cols, send_cols))
-        other = swap(send)
+        part = slice(p * piece, (p + 1) * piece)
+        other = swap(send[:, part])
         blocks.append(
-            jnp.where(even, jnp.concatenate([keep, other]), jnp.concatenate([other, keep]))
+            jnp.where(
+                even,
+                jnp.concatenate([keep[:, part], other]),
+                jnp.concatenate([other, keep[:, part]]),
+            )
         )
 
     came = [{("own", 0): b, ("even", 0): b, ("odd", 0): b} for b in blocks]
@@ -547,8 +593,10 @@
     bits = n_voc.bit_length() - 1
     done = 0
     while True:
-        few = min(1, bits - done)
-        got = [x] + [plane_swap(x, v << done) for v in range(1, 1 << few)]
+        few = min(2, bits - done)
+        peers = range((1 << few) - 1, 0, -1)
+        got = {v: plane_swap(x, v << done) for v in peers}
+        got = [x] + [got[v] for v in sorted(got)]
         done += few
         if done >= bits:
             break
@@ -588,19 +636,22 @@
                     msg = add(grad_rows(kind, s, p), back[other_kind[kind]]).astype(bf16)
                 elif kind == "even" or s == nz - 1:
                     msg = add(grad_rows(kind, s, p), *back.values()).astype(bf16)
+                if s == 1 and kind == "even" and p == PARTS - 1:
+                    low, high = msg[:own_rows], msg[own_rows:]
+                    straight = hop(jnp.where(even, low, high), pairs)
+                    across = cross_hop(jnp.where(even, high, low), pairs)
+                    continue
                 got[p][kind, s] = hop(msg, pairs)
-    keeps, gives = [], []
+    grad_head = None
     for p in range(PARTS):
         full = add(grad_rows("own", 0, p), got[p].get(("even", 1)), got[p].get(("odd", 1)))
         low, high = full[:own_rows], full[own_rows:]
-        keeps.append(jnp.where(even, low, high))
-        give = jnp.where(even, high, low).astype(bf16)
-        gives.append(swap(give).astype(f32))
-    grad_head = jnp.where(
-        even,
-        jnp.concatenate(keeps + gives, axis=1),
-        jnp.concatenate(gives + keeps, axis=1),
-    )
+        mine_terms = [jnp.where(even, low, high)]
+        other_terms = [swap(jnp.where(even, high, low).astype(bf16))]
+        if p == PARTS - 1:
+            mine_terms.append(straight)
+            other_terms.append(across)
+        grad_head = finish_call(p, ahead["core"], grad_head, mine_terms, other_terms)
 
     late, plane, _ = lax.optimization_barrier((slope, plane, msgs[-1]))
     planes = [hop(plane, [(a, (a + k) % nz) for a in range(nz)]) for k in range(1, nz)]

time: 189 us -> 188 us (level)
  the two profiles are of different devices: /device:TPU:0 before, /device:TPU:9 now
where the time goes in v7:
time: 188 us; the launch traced here: 187 us
  waiting for transfers between devices  72.1 us (38%)
  starting transfers between devices  61.6 us (33%)
  Pallas kernels  32.7 us (17%)
  other arithmetic  8.06 us (4%)
  matrix products  5.78 us (3%)
  local copies, waits for them, and re-layouts  5.39 us (3%)
    ppermute x23, waiting for transfers between devices, hop(): lax.ppermute(x, 'tok', [(2 * a + k, 2 * b + k) for a, b in pairs for k in...  65.1 us
    ppermute x23, starting transfers between devices, hop(): lax.ppermute(x, 'tok', [(2 * a + k, 2 * b + k) for a, b in pairs for k in...  41 us
    ppermute x9, starting transfers between devices, swap(): return lax.ppermute(x, 'tok', [(i, i ^ 1) for i in range(n_tok)])  10.1 us
    pallas_call x2, Pallas kernels, early_call(): pl.pallas_call(functools.partial(early_kernel, nz, len(blocks)), grid_spe...  8.69 us
    pallas_call x1, Pallas kernels, hidden_call(): pl.pallas_call(functools.partial(hidden_kernel, nz, count), grid_spec=plt...  7.06 us
    ppermute x1, starting transfers between devices, cross_hop(): lax.ppermute(x, 'tok', [(2 * a + k, 2 * b + 1 - k) for a, b in pairs for...  7.05 us
    dot_general x8, matrix products, dot(): lax.dot_general(a, b, (((1,), (0,)), ((), ())), preferred_element_type=f32)  5.78 us
    pallas_call x2, Pallas kernels, last_call(): pl.pallas_call(functools.partial(last_kernel, part, len(stats), tile), gr...  5.21 us
  transfers between devices with their start and end apart: 39, of which 17 were waited for; matrix products, arithmetic and copies ran while one was open for 9% of the time, Pallas kernels for 14%

profile of v7, /device:TPU:9, one launch (start us, length us, event | category | flops | bytes accessed | tf_op | source)
XLA Modules:
  0.0 186.9 jit_solution(17839618139970879914)
XLA Ops:
  2.8 3.8 %slice_select_fusion = bf16[512,2048]{1,0:T(8,128)(2,1)} fusion(bf16[512,4096]{1,0:T(8,128)(2,1)} %mine_ref, pred[]{:T(512)S(6)} %eq.8), kind=kLoop, calls=%fused_computation.1 | loop fusion | flops 1048576 | bytes 6291457 | tf_op jit(solution)/shard_map/jit(_where)/select_n | solution.py:547
  7.9 3.4 %collective-permute-done = bf16[128,1024]{1,0:T(8,128)(2,1)S(1)} collective-permute-done((bf16[128,1024]{1,0:T(8,128)(2,1)S(1)}, bf16[128,1024]{1,0:T(8,128)(2,1)S(1)}, u32[]{:S(2)}, u32[]{:S(2)}) %collective-permute-start) | collective-permute-done | bytes 262176 | tf_op jit(solution)/shard_map/ppermute | solution.py:528
  11.3 3.2 %collective-permute-start.13 = (bf16[256,1024]{1,0:T(8,128)(2,1)S(1)}, bf16[256,1024]{1,0:T(8,128)(2,1)}, u32[]{:S(2)}, u32[]{:S(2)}) collective-permute-start(bf16[256,1024]{1,0:T(8,128)(2,1)S(1)} %maximum_select_fusion.1.refs_0_.refs_2_), channel_id=1, source_target_pairs={{16,8},{20,12},{8,16},{12,20},{17,9},{21,13},{9,17},{13,21},{18,10... | collective-permute-start | bytes 1572872 | tf_op jit(solution)/shard_map/ppermute | solution.py:531
  14.7 5.2 %collective-permute-done.10.refs_1_.refs_3_ = bf16[256,1024]{1,0:T(8,128)(2,1)} collective-permute-done((bf16[256,1024]{1,0:T(8,128)(2,1)S(1)}, bf16[256,1024]{1,0:T(8,128)(2,1)}, u32[]{:S(2)}, u32[]{:S(2)}) %collective-permute-start.10) | collective-permute-done | bytes 524320 | tf_op jit(solution)/shard_map/ppermute | solution.py:531
  19.9 3.2 %collective-permute-start.4 = (bf16[256,1024]{1,0:T(8,128)(2,1)S(1)}, bf16[256,1024]{1,0:T(8,128)(2,1)S(1)}, u32[]{:S(2)}, u32[]{:S(2)}) collective-permute-start(bf16[256,1024]{1,0:T(8,128)(2,1)S(1)} %maximum_select_fusion.refs_0_.refs_8_), channel_id=1, source_target_pairs={{16,8},{20,12},{8,16},{12,20},{17,9},{21,13},{9,17},{13,21},{18,10... | collective-permute-start | bytes 1572872 | tf_op jit(solution)/shard_map/ppermute | solution.py:531
  23.1 3.5 %collective-permute-done.13.refs_2_.refs_4_ = bf16[256,1024]{1,0:T(8,128)(2,1)} collective-permute-done((bf16[256,1024]{1,0:T(8,128)(2,1)S(1)}, bf16[256,1024]{1,0:T(8,128)(2,1)}, u32[]{:S(2)}, u32[]{:S(2)}) %collective-permute-start.13) | collective-permute-done | bytes 524320 | tf_op jit(solution)/shard_map/ppermute | solution.py:531
  26.6 3.2 %collective-permute-start.11 = (bf16[256,1024]{1,0:T(8,128)(2,1)}, bf16[256,1024]{1,0:T(8,128)(2,1)}, u32[]{:S(2)}, u32[]{:S(2)}) collective-permute-start(bf16[256,1024]{1,0:T(8,128)(2,1)} %collective-permute-done.10.refs_1_.refs_3_), channel_id=1, source_target_pairs={{16,8},{20,12},{8,16},{12,20},{17,9},{21,13},{9,17},{13,21},{18,10... | collective-permute-start | bytes 1572872 | tf_op jit(solution)/shard_map/ppermute | solution.py:531
  31.1 3.2 %collective-permute-start.2 = (bf16[256,1024]{1,0:T(8,128)(2,1)}, bf16[256,1024]{1,0:T(8,128)(2,1)}, u32[]{:S(2)}, u32[]{:S(2)}) collective-permute-start(bf16[256,1024]{1,0:T(8,128)(2,1)} %collective-permute-done.1.refs_1_.refs_9_), channel_id=1, source_target_pairs={{16,8},{20,12},{8,16},{12,20},{17,9},{21,13},{9,17},{13,21},{18,10... | collective-permute-start | bytes 1572872 | tf_op jit(solution)/shard_map/ppermute | solution.py:531
  34.3 3.4 %collective-permute-done.4.refs_2_.refs_10_ = bf16[256,1024]{1,0:T(8,128)(2,1)S(1)} collective-permute-done((bf16[256,1024]{1,0:T(8,128)(2,1)S(1)}, bf16[256,1024]{1,0:T(8,128)(2,1)S(1)}, u32[]{:S(2)}, u32[]{:S(2)}) %collective-permute-start.4) | collective-permute-done | bytes 524320 | tf_op jit(solution)/shard_map/ppermute | solution.py:531
  45.4 3.7 %collective-permute-done.11.refs_4_.refs_6_ = bf16[256,1024]{1,0:T(8,128)(2,1)} collective-permute-done((bf16[256,1024]{1,0:T(8,128)(2,1)}, bf16[256,1024]{1,0:T(8,128)(2,1)}, u32[]{:S(2)}, u32[]{:S(2)}) %collective-permute-start.11) | collective-permute-done | bytes 524320 | tf_op jit(solution)/shard_map/ppermute | solution.py:531
  50.4 9.9 %collective-permute-done.2.refs_4_.refs_12_ = bf16[256,1024]{1,0:T(8,128)(2,1)} collective-permute-done((bf16[256,1024]{1,0:T(8,128)(2,1)}, bf16[256,1024]{1,0:T(8,128)(2,1)}, u32[]{:S(2)}, u32[]{:S(2)}) %collective-permute-start.2) | collective-permute-done | bytes 524320 | tf_op jit(solution)/shard_map/ppermute | solution.py:531
  63.1 4.4 %early_draft.3.refs_1_ = f32[1024,1024]{1,0:T(8,128)S(1)} custom-call(s32[1]{0:T(128)} %bitcast.3.z_ref, bf16[256,1024]{1,0:T(8,128)(2,1)S(1)} %maximum_select_fusion.1.refs_0_.refs_2_, bf16[256,1024]{1,0:T(8,128)(2,1)} %collective-permute-done.10.refs_1_.refs_3_, bf16[256,1024]{1,0:T(8,128)(2,1)} %collective-permute-done.13.refs_2_.refs_4_, ...), custom_call_target="tpu_custom_call" | custom-call | flops 2147483648 | bytes 6291456 | tf_op jit(solution)/shard_map/early_draft/pallas_call | solution.py:172
  67.6 4.3 %early_draft.2.refs_1_ = f32[1024,1024]{1,0:T(8,128)S(1)} custom-call(s32[1]{0:T(128)} %bitcast.3.z_ref, bf16[256,1024]{1,0:T(8,128)(2,1)S(1)} %maximum_select_fusion.refs_0_.refs_8_, bf16[256,1024]{1,0:T(8,128)(2,1)} %collective-permute-done.1.refs_1_.refs_9_, bf16[256,1024]{1,0:T(8,128)(2,1)S(1)} %copy-done.2, ...), custom_call_target="tpu_custom_call" | custom-call | flops 2147483648 | bytes 6291456 | tf_op jit(solution)/shard_map/early_draft/pallas_call | solution.py:172
  71.9 5.0 %target_exps.1 = (bf16[1024,2048]{1,0:T(8,128)(2,1)S(1)}, f32[1024,128]{1,0:T(8,128)S(1)}) custom-call(s32[1]{0:T(128)} %bitcast.core_ref, bf16[512,4096]{1,0:T(8,128)(2,1)S(1)} %copy-done, bf16[512,2048]{1,0:T(8,128)(2,1)} %collective-permute-done.7.came_ref, s32[1024,1]{1,0:T(8,128)S(1)} %broadcast_subtract_fusion.id_ref), custom_call_target="tpu_custom_call" | custom-call | flops 16777216 | bytes 8388608 | tf_op jit(solution)/shard_map/target_exps/pallas_call | solution.py:85
  79.4 4.4 %collective-permute-done.3.refs_0_.refs_13_ = bf16[256,1024]{1,0:T(8,128)(2,1)S(1)} collective-permute-done((bf16[256,1024]{1,0:T(8,128)(2,1)}, bf16[256,1024]{1,0:T(8,128)(2,1)S(1)}, u32[]{:S(2)}, u32[]{:S(2)}) %collective-permute-start.3) | collective-permute-done | bytes 524320 | tf_op jit(solution)/shard_map/ppermute | solution.py:531
  101.3 7.1 %hidden_grad.1 = bf16[1024,1024]{1,0:T(8,128)(2,1)S(1)} custom-call(s32[1]{0:T(128)} %bitcast.3.z_ref, bf16[1024,1024]{1,0:T(8,128)(2,1)S(1)} %get-tuple-element.62.refs_0_, bf16[1024,1024]{1,0:T(8,128)(2,1)S(1)} %get-tuple-element.63.refs_1_, bf16[256,1024]{1,0:T(8,128)(2,1)S(1)} %maximum_select_fusion.1.refs_0_.refs_2_, ...), custom_call_target="tpu_custom_call" | custom-call | flops 4294967296 | bytes 8388608 | tf_op jit(solution)/shard_map/hidden_grad/pallas_call | solution.py:286
  116.1 9.9 %collective-permute-done.19.refs_1_ = f32[8,128]{1,0:T(8,128)S(1)} collective-permute-done((f32[8,128]{1,0:T(8,128)S(1)}, f32[8,128]{1,0:T(8,128)S(1)}, u32[]{:S(2)}, u32[]{:S(2)}) %collective-permute-start.19) | collective-permute-done | bytes 4128 | tf_op jit(solution)/shard_map/ppermute | solution.py:531
  133.9 3.4 %collective-permute-start.29 = (bf16[256,1024]{1,0:T(8,128)(2,1)S(1)}, bf16[256,1024]{1,0:T(8,128)(2,1)S(1)}, u32[]{:S(2)}, u32[]{:S(2)}) collective-permute-start(bf16[256,1024]{1,0:T(8,128)(2,1)S(1)} %fusion.2), channel_id=1, source_target_pairs={{8,16},{12,20},{16,8},{20,12},{9,17},{13,21},{17,9},{21,13},{10,18... | collective-permute-start | bytes 1572872 | tf_op jit(solution)/shard_map/ppermute | solution.py:531
  139.6 3.6 %collective-permute-done.34 = bf16[256,1024]{1,0:T(8,128)(2,1)S(1)} collective-permute-done((bf16[256,1024]{1,0:T(8,128)(2,1)S(1)}, bf16[256,1024]{1,0:T(8,128)(2,1)S(1)}, u32[]{:S(2)}, u32[]{:S(2)}) %collective-permute-start.34) | collective-permute-done | bytes 524320 | tf_op jit(solution)/shard_map/ppermute | solution.py:531
  144.1 10.3 %collective-permute-done.29 = bf16[256,1024]{1,0:T(8,128)(2,1)S(1)} collective-permute-done((bf16[256,1024]{1,0:T(8,128)(2,1)S(1)}, bf16[256,1024]{1,0:T(8,128)(2,1)S(1)}, u32[]{:S(2)}, u32[]{:S(2)}) %collective-permute-start.29) | collective-permute-done | bytes 524320 | tf_op jit(solution)/shard_map/ppermute | solution.py:531
  156.3 3.1 %collective-permute-start.37 = (bf16[256,1024]{1,0:T(8,128)(2,1)S(1)}, bf16[256,1024]{1,0:T(8,128)(2,1)S(1)}, u32[]{:S(2)}, u32[]{:S(2)}) collective-permute-start(bf16[256,1024]{1,0:T(8,128)(2,1)S(1)} %fusion.6), channel_id=1, source_target_pairs={{8,16},{12,20},{16,8},{20,12},{9,17},{13,21},{17,9},{21,13},{10,18... | collective-permute-start | bytes 1572872 | tf_op jit(solution)/shard_map/ppermute | solution.py:531
  160.3 7.1 %collective-permute-start.32 = (bf16[128,1024]{1,0:T(8,128)(2,1)S(1)}, bf16[128,1024]{1,0:T(8,128)(2,1)S(1)}, u32[]{:S(2)}, u32[]{:S(2)}) collective-permute-start(bf16[128,1024]{1,0:T(8,128)(2,1)S(1)} %get-tuple-element.78), channel_id=1, source_target_pairs={{0,12},{4,8},{8,4},{12,0},{16,28},{20,24},{24,20},{28,16},{1,13},{... | collective-permute-start | bytes 786440 | tf_op jit(solution)/shard_map/ppermute | solution.py:534
  171.1 3.2 %collective-permute-start.38 = (bf16[128,1024]{1,0:T(8,128)(2,1)S(1)}, bf16[128,1024]{1,0:T(8,128)(2,1)S(1)}, u32[]{:S(2)}, u32[]{:S(2)}) collective-permute-start(bf16[128,1024]{1,0:T(8,128)(2,1)S(1)} %select_convert_fusion), channel_id=1, source_target_pairs={{0,4},{4,0},{8,12},{12,8},{16,20},{20,16},{24,28},{28,24},{1,5},{5... | collective-permute-start | bytes 786440 | tf_op jit(solution)/shard_map/ppermute | solution.py:528
  174.3 8.9 %collective-permute-done.28 = bf16[256,1024]{1,0:T(8,128)(2,1)S(1)} collective-permute-done((bf16[256,1024]{1,0:T(8,128)(2,1)S(1)}, bf16[256,1024]{1,0:T(8,128)(2,1)S(1)}, u32[]{:S(2)}, u32[]{:S(2)}) %collective-permute-start.28) | collective-permute-done | bytes 524320 | tf_op jit(solution)/shard_map/ppermute | solution.py:531
  (104 shorter events, 65.5 us)
Async XLA Ops:
  6.5 65.3 %collective-permute-start.7 = (bf16[512,2048]{1,0:T(8,128)(2,1)}, bf16[512,2048]{1,0:T(8,128)(2,1)}, u32[]{:S(2)}, u32[]{:S(2)}) collective-permute-start(bf16[512,2048]{1,0:T(8,128)(2,1)} %slice_select_fusion), channel_id=1, source_target_pairs={{0,4},{4,0},{8,12},{12,8},{16,20},{20,16},{24,28},{28,24},{1,5},{5... | collective-permute-start | bytes 6291464 | tf_op jit(solution)/shard_map/ppermute | solution.py:528
  7.4 35.6 %collective-permute-start.6 = (bf16[512,1024]{1,0:T(8,128)(2,1)}, bf16[512,1024]{1,0:T(8,128)(2,1)}, u32[]{:S(2)}, u32[]{:S(2)}) collective-permute-start(bf16[512,1024]{1,0:T(8,128)(2,1)} %param.4), channel_id=1, source_target_pairs={{0,4},{4,0},{8,12},{12,8},{16,20},{20,16},{24,28},{28,24},{1,5},{5... | collective-permute-start | bytes 3145736 | tf_op jit(solution)/shard_map/ppermute | solution.py:528
  11.3 15.3 %collective-permute-start.13 = (bf16[256,1024]{1,0:T(8,128)(2,1)S(1)}, bf16[256,1024]{1,0:T(8,128)(2,1)}, u32[]{:S(2)}, u32[]{:S(2)}) collective-permute-start(bf16[256,1024]{1,0:T(8,128)(2,1)S(1)} %maximum_select_fusion.1.refs_0_.refs_2_), channel_id=1, source_target_pairs={{16,8},{20,12},{8,16},{12,20},{17,9},{21,13},{9,17},{13,21},{18,10... | collective-permute-start | bytes 1572872 | tf_op jit(solution)/shard_map/ppermute | solution.py:531
  14.6 16.5 %collective-permute-start.1 = (bf16[256,1024]{1,0:T(8,128)(2,1)S(1)}, bf16[256,1024]{1,0:T(8,128)(2,1)}, u32[]{:S(2)}, u32[]{:S(2)}) collective-permute-start(bf16[256,1024]{1,0:T(8,128)(2,1)S(1)} %maximum_select_fusion.refs_0_.refs_8_), channel_id=1, source_target_pairs={{8,0},{12,4},{0,8},{4,12},{24,16},{28,20},{16,24},{20,28},{9,1},{1... | collective-permute-start | bytes 1572872 | tf_op jit(solution)/shard_map/ppermute | solution.py:531
  19.9 17.8 %collective-permute-start.4 = (bf16[256,1024]{1,0:T(8,128)(2,1)S(1)}, bf16[256,1024]{1,0:T(8,128)(2,1)S(1)}, u32[]{:S(2)}, u32[]{:S(2)}) collective-permute-start(bf16[256,1024]{1,0:T(8,128)(2,1)S(1)} %maximum_select_fusion.refs_0_.refs_8_), channel_id=1, source_target_pairs={{16,8},{20,12},{8,16},{12,20},{17,9},{21,13},{9,17},{13,21},{18,10... | collective-permute-start | bytes 1572872 | tf_op jit(solution)/shard_map/ppermute | solution.py:531
  26.6 22.5 %collective-permute-start.11 = (bf16[256,1024]{1,0:T(8,128)(2,1)}, bf16[256,1024]{1,0:T(8,128)(2,1)}, u32[]{:S(2)}, u32[]{:S(2)}) collective-permute-start(bf16[256,1024]{1,0:T(8,128)(2,1)} %collective-permute-done.10.refs_1_.refs_3_), channel_id=1, source_target_pairs={{16,8},{20,12},{8,16},{12,20},{17,9},{21,13},{9,17},{13,21},{18,10... | collective-permute-start | bytes 1572872 | tf_op jit(solution)/shard_map/ppermute | solution.py:531
  31.1 29.2 %collective-permute-start.2 = (bf16[256,1024]{1,0:T(8,128)(2,1)}, bf16[256,1024]{1,0:T(8,128)(2,1)}, u32[]{:S(2)}, u32[]{:S(2)}) collective-permute-start(bf16[256,1024]{1,0:T(8,128)(2,1)} %collective-permute-done.1.refs_1_.refs_9_), channel_id=1, source_target_pairs={{16,8},{20,12},{8,16},{12,20},{17,9},{21,13},{9,17},{13,21},{18,10... | collective-permute-start | bytes 1572872 | tf_op jit(solution)/shard_map/ppermute | solution.py:531
  38.5 24.6 %collective-permute-start.14 = (bf16[256,1024]{1,0:T(8,128)(2,1)}, bf16[256,1024]{1,0:T(8,128)(2,1)}, u32[]{:S(2)}, u32[]{:S(2)}) collective-permute-start(bf16[256,1024]{1,0:T(8,128)(2,1)} %collective-permute-done.13.refs_2_.refs_4_), channel_id=1, source_target_pairs={{8,0},{12,4},{16,24},{20,28},{9,1},{13,5},{17,25},{21,29},{10,2},{... | collective-permute-start | bytes 1572872 | tf_op jit(solution)/shard_map/ppermute | solution.py:531
  43.0 24.6 %collective-permute-start.5 = (bf16[256,1024]{1,0:T(8,128)(2,1)}, bf16[256,1024]{1,0:T(8,128)(2,1)S(1)}, u32[]{:S(2)}, u32[]{:S(2)}) collective-permute-start(bf16[256,1024]{1,0:T(8,128)(2,1)} %copy-done.1), channel_id=1, source_target_pairs={{8,0},{12,4},{16,24},{20,28},{9,1},{13,5},{17,25},{21,29},{10,2},{... | collective-permute-start | bytes 1572872 | tf_op jit(solution)/shard_map/ppermute | solution.py:531
  49.1 27.8 %collective-permute-start.12 = (bf16[256,1024]{1,0:T(8,128)(2,1)}, bf16[256,1024]{1,0:T(8,128)(2,1)S(1)}, u32[]{:S(2)}, u32[]{:S(2)}) collective-permute-start(bf16[256,1024]{1,0:T(8,128)(2,1)} %collective-permute-done.11.refs_4_.refs_6_), channel_id=1, source_target_pairs={{8,0},{12,4},{16,24},{20,28},{9,1},{13,5},{17,25},{21,29},{10,2},{... | collective-permute-start | bytes 1572872 | tf_op jit(solution)/shard_map/ppermute | solution.py:531
  60.3 23.5 %collective-permute-start.3 = (bf16[256,1024]{1,0:T(8,128)(2,1)}, bf16[256,1024]{1,0:T(8,128)(2,1)S(1)}, u32[]{:S(2)}, u32[]{:S(2)}) collective-permute-start(bf16[256,1024]{1,0:T(8,128)(2,1)} %collective-permute-done.2.refs_4_.refs_12_), channel_id=1, source_target_pairs={{8,0},{12,4},{16,24},{20,28},{9,1},{13,5},{17,25},{21,29},{10,2},{... | collective-permute-start | bytes 1572872 | tf_op jit(solution)/shard_map/ppermute | solution.py:531
  97.9 31.2 %collective-permute-start.33 = (bf16[256,1024]{1,0:T(8,128)(2,1)S(1)}, bf16[256,1024]{1,0:T(8,128)(2,1)S(1)}, u32[]{:S(2)}, u32[]{:S(2)}) collective-permute-start(bf16[256,1024]{1,0:T(8,128)(2,1)S(1)} %get-tuple-element.72), channel_id=1, source_target_pairs={{0,8},{4,12},{24,16},{28,20},{1,9},{5,13},{25,17},{29,21},{2,10},{... | collective-permute-start | bytes 1572872 | tf_op jit(solution)/shard_map/ppermute | solution.py:531
  108.4 30.1 %collective-permute-start.22 = (bf16[512,1024]{1,0:T(8,128)(2,1)S(1)}, bf16[512,1024]{1,0:T(8,128)(2,1)S(1)}, u32[]{:S(2)}, u32[]{:S(2)}) collective-permute-start(bf16[512,1024]{1,0:T(8,128)(2,1)S(1)} %slice.77), channel_id=1, source_target_pairs={{0,4},{4,0},{8,12},{12,8},{16,20},{20,16},{24,28},{28,24},{1,5},{5... | collective-permute-start | bytes 3145736 | tf_op jit(solution)/shard_map/ppermute | solution.py:528
  110.5 22.6 %collective-permute-start.26 = (bf16[256,1024]{1,0:T(8,128)(2,1)S(1)}, bf16[256,1024]{1,0:T(8,128)(2,1)S(1)}, u32[]{:S(2)}, u32[]{:S(2)}) collective-permute-start(bf16[256,1024]{1,0:T(8,128)(2,1)S(1)} %get-tuple-element.60), channel_id=1, source_target_pairs={{0,8},{4,12},{24,16},{28,20},{1,9},{5,13},{25,17},{29,21},{2,10},{... | collective-permute-start | bytes 1572872 | tf_op jit(solution)/shard_map/ppermute | solution.py:531
  113.2 14.7 %collective-permute-start.20 = (f32[8,128]{1,0:T(8,128)S(1)}, f32[8,128]{1,0:T(8,128)S(1)}, u32[]{:S(2)}, u32[]{:S(2)}) collective-permute-start(f32[8,128]{1,0:T(8,128)S(1)} %get-tuple-element.61.refs_0_), channel_id=1, source_target_pairs={{0,16},{4,20},{8,24},{12,28},{16,0},{20,4},{24,8},{28,12},{1,17},{... | collective-permute-start | bytes 12296 | tf_op jit(solution)/shard_map/ppermute | solution.py:531
  131.8 23.5 %collective-permute-start.36 = (bf16[256,1024]{1,0:T(8,128)(2,1)S(1)}, bf16[256,1024]{1,0:T(8,128)(2,1)S(1)}, u32[]{:S(2)}, u32[]{:S(2)}) collective-permute-start(bf16[256,1024]{1,0:T(8,128)(2,1)S(1)} %fusion.5), channel_id=1, source_target_pairs={{0,8},{4,12},{24,16},{28,20},{1,9},{5,13},{25,17},{29,21},{2,10},{... | collective-permute-start | bytes 1572872 | tf_op jit(solution)/shard_map/ppermute | solution.py:531
  133.9 20.5 %collective-permute-start.29 = (bf16[256,1024]{1,0:T(8,128)(2,1)S(1)}, bf16[256,1024]{1,0:T(8,128)(2,1)S(1)}, u32[]{:S(2)}, u32[]{:S(2)}) collective-permute-start(bf16[256,1024]{1,0:T(8,128)(2,1)S(1)} %fusion.2), channel_id=1, source_target_pairs={{8,16},{12,20},{16,8},{20,12},{9,17},{13,21},{17,9},{21,13},{10,18... | collective-permute-start | bytes 1572872 | tf_op jit(solution)/shard_map/ppermute | solution.py:531
  137.2 19.1 %collective-permute-start.27 = (bf16[256,1024]{1,0:T(8,128)(2,1)S(1)}, bf16[256,1024]{1,0:T(8,128)(2,1)S(1)}, u32[]{:S(2)}, u32[]{:S(2)}) collective-permute-start(bf16[256,1024]{1,0:T(8,128)(2,1)S(1)} %fusion.2), channel_id=1, source_target_pairs={{0,8},{4,12},{24,16},{28,20},{1,9},{5,13},{25,17},{29,21},{2,10},{... | collective-permute-start | bytes 1572872 | tf_op jit(solution)/shard_map/ppermute | solution.py:531
  139.2 21.0 %collective-permute-start.23 = (bf16[512,256]{1,0:T(8,128)(2,1)S(1)}, bf16[512,256]{1,0:T(8,128)(2,1)S(1)}, u32[]{:S(2)}, u32[]{:S(2)}) collective-permute-start(bf16[512,256]{1,0:T(8,128)(2,1)S(1)} %get-tuple-element.73), channel_id=1, source_target_pairs={{0,1},{1,0},{2,3},{3,2},{4,5},{5,4},{6,7},{7,6},{8,9},{9,8},{10,11... | collective-permute-start | bytes 786440 | tf_op jit(solution)/shard_map/ppermute | solution.py:539
  143.2 17.1 %collective-permute-start.24 = (bf16[512,256]{1,0:T(8,128)(2,1)S(1)}, bf16[512,256]{1,0:T(8,128)(2,1)S(1)}, u32[]{:S(2)}, u32[]{:S(2)}) collective-permute-start(bf16[512,256]{1,0:T(8,128)(2,1)S(1)} %get-tuple-element.75), channel_id=1, source_target_pairs={{0,2},{1,3},{2,0},{3,1},{4,6},{5,7},{6,4},{7,5},{8,10},{9,11},{10,... | collective-permute-start | bytes 786440 | tf_op jit(solution)/shard_map/ppermute | solution.py:539
  155.3 15.0 %collective-permute-start.35 = (bf16[256,1024]{1,0:T(8,128)(2,1)S(1)}, bf16[256,1024]{1,0:T(8,128)(2,1)S(1)}, u32[]{:S(2)}, u32[]{:S(2)}) collective-permute-start(bf16[256,1024]{1,0:T(8,128)(2,1)S(1)} %fusion.4), channel_id=1, source_target_pairs={{0,8},{4,12},{8,0},{12,4},{16,24},{20,28},{24,16},{28,20},{1,9},{5... | collective-permute-start | bytes 1572872 | tf_op jit(solution)/shard_map/ppermute | solution.py:531
  160.2 25.6 %collective-permute-start.30 = (bf16[128,1024]{1,0:T(8,128)(2,1)S(1)}, bf16[128,1024]{1,0:T(8,128)(2,1)S(1)}, u32[]{:S(2)}, u32[]{:S(2)}) collective-permute-start(bf16[128,1024]{1,0:T(8,128)(2,1)S(1)} %get-tuple-element.79), channel_id=1, source_target_pairs={{0,8},{4,12},{8,0},{12,4},{16,24},{20,28},{24,16},{28,20},{1,9},{5... | collective-permute-start | bytes 786440 | tf_op jit(solution)/shard_map/ppermute | solution.py:531
  160.3 25.6 %collective-permute-start.32 = (bf16[128,1024]{1,0:T(8,128)(2,1)S(1)}, bf16[128,1024]{1,0:T(8,128)(2,1)S(1)}, u32[]{:S(2)}, u32[]{:S(2)}) collective-permute-start(bf16[128,1024]{1,0:T(8,128)(2,1)S(1)} %get-tuple-element.78), channel_id=1, source_target_pairs={{0,12},{4,8},{8,4},{12,0},{16,28},{20,24},{24,20},{28,16},{1,13},{... | collective-permute-start | bytes 786440 | tf_op jit(solution)/shard_map/ppermute | solution.py:534
  167.4 15.8 %collective-permute-start.28 = (bf16[256,1024]{1,0:T(8,128)(2,1)S(1)}, bf16[256,1024]{1,0:T(8,128)(2,1)S(1)}, u32[]{:S(2)}, u32[]{:S(2)}) collective-permute-start(bf16[256,1024]{1,0:T(8,128)(2,1)S(1)} %fusion.1), channel_id=1, source_target_pairs={{8,16},{12,20},{16,8},{20,12},{9,17},{13,21},{17,9},{21,13},{10,18... | collective-permute-start | bytes 1572872 | tf_op jit(solution)/shard_map/ppermute | solution.py:531
  (19 other events, 125.3 us)

commit v8 on v7

--- a/solution.py
+++ b/solution.py
@@ -66,8 +66,9 @@
     return pltpu.CompilerParams(vmem_limit_bytes=size << 20)
 
 
-def target_kernel(own_tiles, core_ref, mine_ref, came_ref, id_ref, e_ref, stat_ref):
+def target_kernel(own_tiles, core_ref, mine_ref, came_ref, id_ref, e_ref, stat_ref, row_ref, turn_ref):
     step = pl.program_id(0)
+    steps = pl.num_programs(0)
     t = jnp.where(step < own_tiles, mine_ref[...], came_ref[...]).astype(f32)
     at = pl.ds(pl.multiple_of(step * t.shape[0], t.shape[0]), t.shape[0])
     top = jnp.max(t, axis=1, keepdims=True)
@@ -76,7 +77,14 @@
     total = jnp.sum(e, axis=1, keepdims=True)
     first = jnp.sum(e * t, axis=1, keepdims=True)
     ids = id_ref[...].astype(f32)
-    stat_ref[at, :] = lanes([top, total, first, ids], (t.shape[0], 128))
+    size = t.shape[0]
+    stat = lanes([top, total, first, ids], (size, 128))
+    stat_ref[at, :] = stat
+    row = lax.broadcasted_iota(jnp.int32, (8, size), 0)
+    rows = jnp.where(row < 3, stat.T[:8], 0.0)
+    row_ref[:, at] = rows
+    turned = lax.rem(step + steps // 2, steps) * size
+    turn_ref[:, pl.ds(pl.multiple_of(turned, size), size)] = rows
 
 
 def target_call(core, logits, came, ids, tile):
@@ -92,9 +100,14 @@
                 pl.BlockSpec((tile, half), lambda i, s: (jnp.maximum(i - own_tiles, 0), 0)),
                 pl.BlockSpec((tile, 1), lambda i, s: (i, 0)),
             ],
-            out_specs=[WHOLE, WHOLE],
+            out_specs=[WHOLE] * 4,
         ),
-        out_shape=[out((n, half), bf16), out((n, 128), f32)],
+        out_shape=[
+            out((n, half), bf16),
+            out((n, 128), f32),
+            out((8, n), f32),
+            out((8, n), f32),
+        ],
         compiler_params=params(16),
         cost_estimate=cost(8 * n * half, 4 * n * half, n * half),
         name="target_exps",
@@ -189,9 +202,9 @@
 
 
 def last_kernel(part, earlier, tile, at_ref, *refs):
-    w_ref, acc_ref, h_ref, e_ref, t_ref = refs[:5]
-    stat_refs = refs[5:5 + earlier]
-    outs = refs[5 + earlier:]
+    w_ref, acc_ref, h_ref, e_ref = refs[:4]
+    stat_refs = refs[4:4 + earlier]
+    outs = refs[4 + earlier:]
     n, piece = acc_ref.shape
     deep = w_ref.shape[0]
     block = pl.ds(pl.multiple_of(at_ref[0] * deep, deep), deep)
@@ -203,37 +216,30 @@
         e = jnp.exp(z - top)
         outs[0][at, :] = e.astype(bf16)
         total = jnp.sum(e, axis=1, keepdims=True)
-        e_t = e_ref[at, part * piece:(part + 1) * piece].astype(f32)
-        cross = jnp.sum(e_t * z, axis=1, keepdims=True)
-        t_stat = t_ref[at, :]
-        column = lax.broadcasted_iota(jnp.int32, z.shape, 1) + part * piece
-        id_col = t_stat[:, 3:4].astype(jnp.int32)
-        own = jnp.sum(jnp.where(column == id_col, z, 0.0), axis=1, keepdims=True)
-        stat = lanes([top, total, cross, own], like, 4 + 4 * part)
+        weight = e_ref[at, part * piece:(part + 1) * piece].astype(f32)
+        cross = jnp.sum(weight * z, axis=1, keepdims=True)
+        stat = lanes([top, total, cross], like, 4 * part)
         if part < PARTS - 1:
             outs[1][at, :] = stat
             continue
         send_ref, turn_ref, tops_ref = outs[1:]
-        stat = stat + t_stat
         for r in stat_refs:
             stat = stat + r[at, :]
         row = stat.T
-        row = [row[k:k + 1] for k in range(4 + 4 * PARTS)]
-        tops = row[4::4]
+        row = [row[k:k + 1] for k in range(4 * PARTS)]
+        tops = row[::4]
         all_top = functools.reduce(jnp.maximum, tops)
-        total = sum(row[5 + 4 * p] * jnp.exp(tops[p] - all_top) for p in range(PARTS))
-        cross, own = sum(row[6::4]), sum(row[7::4])
+        total = sum(row[1 + 4 * p] * jnp.exp(tops[p] - all_top) for p in range(PARTS))
         blank = jnp.zeros((1, tile), f32)
-        rows = [row[0], row[1], row[2] - cross, all_top, total, own, blank, blank]
+        rows = [blank] * 3 + [all_top, total, sum(row[2::4]), blank, blank]
         rows = jnp.concatenate(rows)
         send_ref[:, at] = rows
         turned = (k * tile + n // 2) % n
         turn_ref[:, turned:turned + tile] = rows
-        tops = [row[0]] + tops + [row[3]]
         tops_ref[:, at] = jnp.concatenate(tops + [blank] * (8 - len(tops)))
 
 
-def last_call(part, at, w, acc, hid, e_t, t_stat, stats, tile):
+def last_call(part, at, w, acc, hid, weight, stats, tile):
     n, piece = acc.shape
     out_shape = [out((n, piece), bf16)]
     if part < PARTS - 1:
@@ -246,14 +252,14 @@
         grid_spec=pltpu.PrefetchScalarGridSpec(
             num_scalar_prefetch=1,
             grid=(1,),
-            in_specs=[WHOLE] * (5 + len(stats)),
+            in_specs=[WHOLE] * (4 + len(stats)),
             out_specs=[WHOLE] * len(out_shape),
         ),
         out_shape=out_shape,
         compiler_params=params(10),
         cost_estimate=cost(2 * n * w.shape[0] * piece, 8 * n * piece, n * piece),
         name="last_draft",
-    )(at, near(w), near(acc), near(hid), near(e_t), near(t_stat), *map(near, stats))
+    )(at, near(w), near(acc), near(hid), near(weight), *map(near, stats))
 
 
 def hidden_kernel(nz, count, z_ref, *refs):
@@ -337,60 +343,83 @@
     )(*map(near, rows))
 
 
+def weight_kernel(peers, tile, *refs):
+    local_ref, e_ref, stat_ref, w_ref, row_ref = refs[peers:]
+    got = [r[...] for r in refs[:peers]]
+    while len(got) > 1:
+        got = [fold_rows(got[j], got[j + 1]) for j in range(0, len(got), 2)]
+    s = got[0]
+    n = s.shape[1]
+    inv = 1.0 / s[1:2]
+    row = s[2:3] * inv - s[0:1] - jnp.log(s[1:2])
+    row_ref[...] = jnp.broadcast_to(row, row_ref.shape)
+    gain = jnp.exp(local_ref[0:1, :] - s[0:1]) * inv
+    gain = jnp.concatenate([gain, jnp.zeros((127, n), f32)]).T[:, 0:1]
+    id_col = stat_ref[:, 3:4].astype(jnp.int32)
+    for first in range(0, e_ref.shape[1], tile):
+        at = slice(first, first + tile)
+        value = e_ref[:, at].astype(f32) * gain
+        column = lax.broadcasted_iota(jnp.int32, value.shape, 1) + first
+        w_ref[:, at] = jnp.where(column == id_col, value + ce_weight, value).astype(bf16)
+
+
+def weight_call(got, local, e_t, t_stat, tile):
+    n, half = e_t.shape
+    args = [*got, local, e_t, t_stat]
+    return pl.pallas_call(
+        functools.partial(weight_kernel, len(got), tile),
+        in_specs=[WHOLE] * len(args),
+        out_specs=[WHOLE, WHOLE],
+        out_shape=[out((n, half), bf16), out((8, n), f32)],
+        compiler_params=params(16),
+        cost_estimate=cost(4 * n * half, 4 * n * half),
+        name="weights",
+    )(*map(near, args))
+
+
 def slope_kernel(part, peers, tile, idx_ref, *refs):
     if peers:
-        tops_ref = refs[peers]
-        ez_ref, et_ref, ht_ref = refs[peers + 1:peers + 4]
-        slope_ref, msg_ref, coef_ref, loss_ref = refs[peers + 4:]
-
+        tops_ref, t_ref = refs[peers:peers + 2]
+        ez_ref, w_ref, ht_ref = refs[peers + 2:peers + 5]
+        slope_ref, msg_ref, coef_ref, loss_ref = refs[peers + 5:]
         got = [r[...] for r in refs[:peers]]
         while len(got) > 1:
             got = [fold_rows(got[j], got[j + 1]) for j in range(0, len(got), 2)]
         s = got[0]
-        t_inv = 1.0 / s[1:2]
-        lse_t = s[0:1] + jnp.log(s[1:2])
+        n = s.shape[1]
         lse_z = s[3:4] + jnp.log(s[4:5])
-        n = s.shape[1]
-        per_token = s[2:3] * t_inv - lse_t + (1.0 + ce_weight) * lse_z - ce_weight * s[5:6]
+        per_token = t_ref[0:1, :] - s[5:6] + (1.0 + ce_weight) * lse_z
         plane = jnp.sum(per_token[:, :n // 2], axis=1, keepdims=True) + jnp.sum(
             per_token[:, n // 2:], axis=1, keepdims=True
         )
         loss_ref[...] = jnp.broadcast_to(plane, loss_ref.shape)
         z_inv = (1.0 + ce_weight) / s[4:5]
         tops = tops_ref[...]
-        rows = [jnp.exp(tops[0:1] - s[0:1]) * t_inv]
-        rows += [jnp.exp(tops[p + 1:p + 2] - s[3:4]) * z_inv for p in range(PARTS)]
-        rows += [tops[PARTS + 1:PARTS + 2]]
+        rows = [jnp.exp(tops[p:p + 1] - s[3:4]) * z_inv for p in range(PARTS)]
         rows += [jnp.zeros((128 - len(rows), n), f32)]
         coef_ref[...] = jnp.concatenate(rows).T
-
     else:
-        coef_ref, ez_ref, et_ref, ht_ref, slope_ref, msg_ref = refs
-    b = coef_ref[:, 0:1]
-    a = coef_ref[:, part + 1:part + 2]
-    id_col = coef_ref[:, PARTS + 1:PARTS + 2].astype(jnp.int32)
+        coef_ref, ez_ref, w_ref, ht_ref, slope_ref, msg_ref = refs
+    a = coef_ref[:, part:part + 1]
     deep, piece = msg_ref.shape
     rows = pl.ds(pl.multiple_of(idx_ref[0] * deep, deep), deep)
     for first in range(0, piece, tile):
         at = slice(first, first + tile)
-        e_t = et_ref[:, part * piece + first:part * piece + first + tile]
-        value = ez_ref[:, at].astype(f32) * a - e_t.astype(f32) * b
-        column = lax.broadcasted_iota(jnp.int32, value.shape, 1) + (part * piece + first)
-        value = jnp.where(column == id_col, value - ce_weight, value)
-        slope = value.astype(bf16)
+        weight = w_ref[:, part * piece + first:part * piece + first + tile]
+        slope = (ez_ref[:, at].astype(f32) * a - weight.astype(f32)).astype(bf16)
         slope_ref[:, at] = slope
         msg_ref[:, at] = dot(ht_ref[rows, :], slope).astype(bf16)
 
 
-def slope_call(part, index, head_args, e_z, e_t, hid_t, deep, tile):
+def slope_call(part, index, head_args, e_z, weight, hid_t, deep, tile):
     n, piece = e_z.shape
-    peers = len(head_args) - 1
+    peers = max(0, len(head_args) - 2)
     out_specs = [WHOLE, WHOLE]
     out_shape = [out((n, piece), bf16), out((deep, piece), bf16)]
     if peers:
         out_specs += [WHOLE, WHOLE]
         out_shape += [out((n, 128), f32), out((8, 128), f32)]
-    args = [*head_args, e_z, e_t, hid_t]
+    args = [*head_args, e_z, weight, hid_t]
     return pl.pallas_call(
         functools.partial(slope_kernel, part, peers, tile),
         grid_spec=pltpu.PrefetchScalarGridSpec(
@@ -573,7 +602,24 @@
     tgt = mine(logits, True)
     tgt = swap(tgt)
     local = jnp.concatenate([ids, swap(ids)]) - vocab_start
-    e_t, t_stat = target_call(ahead["core"], logits, tgt, local[:, None], tile)
+    e_t, t_stat, t_rows, t_turned = target_call(ahead["core"], logits, tgt, local[:, None], tile)
+
+    def exchange(rows, turned):
+        x = fold_call([rows, swap(turned)])
+        bits = n_voc.bit_length() - 1
+        done = 0
+        while True:
+            few = min(2, bits - done)
+            peers = range((1 << few) - 1, 0, -1)
+            got = {v: plane_swap(x, v << done) for v in peers}
+            got = [x] + [got[v] for v in sorted(got)]
+            done += few
+            if done >= bits:
+                return got
+            x = fold_call(got)
+
+    got = exchange(t_rows, t_turned)
+    weight, t_row = weight_call(got, t_rows, e_t, t_stat, wide)
 
     stats, e_z = [], []
     order = arrivals(nz)
@@ -583,30 +629,19 @@
         acc = early_call(nz, ahead["z"], whole[p][:len(early)], hid, tile)
         w = whole[p][len(early):]
         w = w[0] if len(w) == 1 else jnp.where(first_chip, w[0], w[1])
-        outs = last_call(p, ahead["last"], w, acc, hid, e_t, t_stat, stats, tile)
+        outs = last_call(p, ahead["last"], w, acc, hid, weight, stats, tile)
         e_z.append(outs[0])
         if p < PARTS - 1:
             stats.append(outs[1])
     mine_rows, turned, tops = outs[1:]
 
-    x = fold_call([mine_rows, swap(turned)])
-    bits = n_voc.bit_length() - 1
-    done = 0
-    while True:
-        few = min(2, bits - done)
-        peers = range((1 << few) - 1, 0, -1)
-        got = {v: plane_swap(x, v << done) for v in peers}
-        got = [x] + [got[v] for v in sorted(got)]
-        done += few
-        if done >= bits:
-            break
-        x = fold_call(got)
+    got = exchange(mine_rows, turned)
 
     msgs, slope = [], []
     for p in range(PARTS):
-        head_args = got + [tops] if p == 0 else [coef]
+        head_args = got + [tops, t_row] if p == 0 else [coef]
         outs = slope_call(
-            p, ahead["first"], head_args, e_z[p], e_t, hid_t, deep, wide
+            p, ahead["first"], head_args, e_z[p], weight, hid_t, deep, wide
         )
         slope.append(outs[0])
         msgs.append(outs[1])

time: 188 us -> 190 us (1.011)
  the two profiles are of different devices: /device:TPU:9 before, /device:TPU:0 now
where the time goes in v8:
time: 190 us; the launch traced here: 187 us
  waiting for transfers between devices  78.5 us (41%)
  starting transfers between devices  55.3 us (29%)
  Pallas kernels  31.6 us (17%)
  local copies, waits for them, and re-layouts  7.56 us (4%)
  other arithmetic  6.93 us (4%)
  matrix products  5.77 us (3%)
    ppermute x23, waiting for transfers between devices, hop(): lax.ppermute(x, 'tok', [(2 * a + k, 2 * b + k) for a, b in pairs for k in...  62.3 us
    ppermute x23, starting transfers between devices, hop(): lax.ppermute(x, 'tok', [(2 * a + k, 2 * b + k) for a, b in pairs for k in...  42.5 us
    ppermute x9, starting transfers between devices, plane_swap(): return lax.ppermute(x, 'voc', [(w, w ^ v) for w in range(n_voc)])  10.9 us
    pallas_call x2, Pallas kernels, early_call(): pl.pallas_call(functools.partial(early_kernel, nz, len(blocks)), grid_spe...  8.11 us
    ppermute x9, waiting for transfers between devices, plane_swap(): return lax.ppermute(x, 'voc', [(w, w ^ v) for w in range(n_voc)])  7.02 us
    pallas_call x1, Pallas kernels, hidden_call(): pl.pallas_call(functools.partial(hidden_kernel, nz, count), grid_spec=plt...  6.74 us
    ppermute x10, waiting for transfers between devices, swap(): return lax.ppermute(x, 'tok', [(i, i ^ 1) for i in range(n_tok)])  6.41 us
    dot_general x8, matrix products, dot(): lax.dot_general(a, b, (((1,), (0,)), ((), ())), preferred_element_type=f32)  5.77 us
  transfers between devices with their start and end apart: 43, of which 21 were waited for; matrix products, arithmetic and copies ran while one was open for 7% of the time, Pallas kernels for 14%

profile of v8, /device:TPU:0, one launch (start us, length us, event | category | flops | bytes accessed | tf_op | source)
XLA Modules:
  0.0 187.0 jit_solution(10336849317629854403)
XLA Ops:
  0.7 3.8 %slice_select_fusion = bf16[512,2048]{1,0:T(8,128)(2,1)} fusion(bf16[512,4096]{1,0:T(8,128)(2,1)} %mine_ref, pred[]{:T(512)S(6)} %eq.8), kind=kLoop, calls=%fused_computation.1 | loop fusion | flops 1048576 | bytes 6291457 | tf_op jit(solution)/shard_map/jit(_where)/select_n | solution.py:576
  5.3 4.1 %collective-permute-done.13 = bf16[128,1024]{1,0:T(8,128)(2,1)S(1)} collective-permute-done((bf16[128,1024]{1,0:T(8,128)(2,1)S(1)}, bf16[128,1024]{1,0:T(8,128)(2,1)S(1)}, u32[]{:S(2)}, u32[]{:S(2)}) %collective-permute-start.13) | collective-permute-done | bytes 262176 | tf_op jit(solution)/shard_map/ppermute | solution.py:557
  9.6 3.0 %collective-permute-start.14 = (bf16[256,1024]{1,0:T(8,128)(2,1)S(1)}, bf16[256,1024]{1,0:T(8,128)(2,1)}, u32[]{:S(2)}, u32[]{:S(2)}) collective-permute-start(bf16[256,1024]{1,0:T(8,128)(2,1)S(1)} %maximum_select_fusion.1.refs_0_.refs_2_), channel_id=1, source_target_pairs={{8,0},{12,4},{0,8},{4,12},{24,16},{28,20},{16,24},{20,28},{9,1},{1... | collective-permute-start | bytes 1572872 | tf_op jit(solution)/shard_map/ppermute | solution.py:560
  15.7 3.6 %collective-permute-start.1 = (bf16[256,1024]{1,0:T(8,128)(2,1)S(1)}, bf16[256,1024]{1,0:T(8,128)(2,1)}, u32[]{:S(2)}, u32[]{:S(2)}) collective-permute-start(bf16[256,1024]{1,0:T(8,128)(2,1)S(1)} %maximum_select_fusion.refs_0_.refs_8_), channel_id=1, source_target_pairs={{8,0},{12,4},{0,8},{4,12},{24,16},{28,20},{16,24},{20,28},{9,1},{1... | collective-permute-start | bytes 1572872 | tf_op jit(solution)/shard_map/ppermute | solution.py:560
  19.4 6.1 %collective-permute-done.14.refs_1_.refs_3_ = bf16[256,1024]{1,0:T(8,128)(2,1)} collective-permute-done((bf16[256,1024]{1,0:T(8,128)(2,1)S(1)}, bf16[256,1024]{1,0:T(8,128)(2,1)}, u32[]{:S(2)}, u32[]{:S(2)}) %collective-permute-start.14) | collective-permute-done | bytes 524320 | tf_op jit(solution)/shard_map/ppermute | solution.py:560
  27.6 8.5 %collective-permute-done.1.refs_1_.refs_9_ = bf16[256,1024]{1,0:T(8,128)(2,1)} collective-permute-done((bf16[256,1024]{1,0:T(8,128)(2,1)S(1)}, bf16[256,1024]{1,0:T(8,128)(2,1)}, u32[]{:S(2)}, u32[]{:S(2)}) %collective-permute-start.1) | collective-permute-done | bytes 524320 | tf_op jit(solution)/shard_map/ppermute | solution.py:560
  50.7 5.3 %target_exps.1 = (bf16[1024,2048]{1,0:T(8,128)(2,1)S(1)}, f32[1024,128]{1,0:T(8,128)S(1)}, f32[8,1024]{1,0:T(8,128)S(1)}, f32[8,1024]{1,0:T(8,128)S(1)}) custom-call(s32[1]{0:T(128)} %bitcast.core_ref, bf16[512,4096]{1,0:T(8,128)(2,1)S(1)} %copy-done, bf16[512,2048]{1,0:T(8,128)(2,1)} %collective-permute-done.7.came_ref, ...), custom_call_target="tpu_custom_call" | custom-call | flops 16777216 | bytes 8388608 | tf_op jit(solution)/shard_map/target_exps/pallas_call | solution.py:93
  56.1 3.2 %collective-permute-done.18.refs_3_.refs_5_ = bf16[256,1024]{1,0:T(8,128)(2,1)} collective-permute-done((bf16[256,1024]{1,0:T(8,128)(2,1)}, bf16[256,1024]{1,0:T(8,128)(2,1)}, u32[]{:S(2)}, u32[]{:S(2)}) %collective-permute-start.18) | collective-permute-done | bytes 524320 | tf_op jit(solution)/shard_map/ppermute | solution.py:560
  59.3 4.1 %early_draft.3.refs_1_ = f32[1024,1024]{1,0:T(8,128)S(1)} custom-call(s32[1]{0:T(128)} %bitcast.3.z_ref, bf16[256,1024]{1,0:T(8,128)(2,1)S(1)} %maximum_select_fusion.1.refs_0_.refs_2_, bf16[256,1024]{1,0:T(8,128)(2,1)} %collective-permute-done.14.refs_1_.refs_3_, bf16[256,1024]{1,0:T(8,128)(2,1)} %collective-permute-done.17.refs_2_.refs_4_, ...), custom_call_target="tpu_custom_call" | custom-call | flops 2147483648 | bytes 6291456 | tf_op jit(solution)/shard_map/early_draft/pallas_call | solution.py:185
  66.6 3.9 %collective-permute-done.5.refs_3_.refs_11_ = bf16[256,1024]{1,0:T(8,128)(2,1)S(1)} collective-permute-done((bf16[256,1024]{1,0:T(8,128)(2,1)}, bf16[256,1024]{1,0:T(8,128)(2,1)S(1)}, u32[]{:S(2)}, u32[]{:S(2)}) %collective-permute-start.5) | collective-permute-done | bytes 524320 | tf_op jit(solution)/shard_map/ppermute | solution.py:560
  72.9 4.0 %early_draft.2.refs_1_ = f32[1024,1024]{1,0:T(8,128)S(1)} custom-call(s32[1]{0:T(128)} %bitcast.3.z_ref, bf16[256,1024]{1,0:T(8,128)(2,1)S(1)} %maximum_select_fusion.refs_0_.refs_8_, bf16[256,1024]{1,0:T(8,128)(2,1)} %collective-permute-done.1.refs_1_.refs_9_, bf16[256,1024]{1,0:T(8,128)(2,1)S(1)} %copy-done.2, ...), custom_call_target="tpu_custom_call" | custom-call | flops 2147483648 | bytes 6291456 | tf_op jit(solution)/shard_map/early_draft/pallas_call | solution.py:185
  79.0 2.7 %collective-permute-done.16.refs_0_.refs_7_ = bf16[256,1024]{1,0:T(8,128)(2,1)S(1)} collective-permute-done((bf16[256,1024]{1,0:T(8,128)(2,1)}, bf16[256,1024]{1,0:T(8,128)(2,1)S(1)}, u32[]{:S(2)}, u32[]{:S(2)}) %collective-permute-start.16) | collective-permute-done | bytes 524320 | tf_op jit(solution)/shard_map/ppermute | solution.py:560
  83.6 5.6 %collective-permute-done.3.refs_0_.refs_13_ = bf16[256,1024]{1,0:T(8,128)(2,1)S(1)} collective-permute-done((bf16[256,1024]{1,0:T(8,128)(2,1)}, bf16[256,1024]{1,0:T(8,128)(2,1)S(1)}, u32[]{:S(2)}, u32[]{:S(2)}) %collective-permute-start.3) | collective-permute-done | bytes 524320 | tf_op jit(solution)/shard_map/ppermute | solution.py:560
  102.0 4.5 %collective-permute-start.37 = (bf16[256,1024]{1,0:T(8,128)(2,1)S(1)}, bf16[256,1024]{1,0:T(8,128)(2,1)S(1)}, u32[]{:S(2)}, u32[]{:S(2)}) collective-permute-start(bf16[256,1024]{1,0:T(8,128)(2,1)S(1)} %get-tuple-element.80), channel_id=1, source_target_pairs={{0,8},{4,12},{24,16},{28,20},{1,9},{5,13},{25,17},{29,21},{2,10},{... | collective-permute-start | bytes 1572872 | tf_op jit(solution)/shard_map/ppermute | solution.py:560
  108.9 9.8 %collective-permute-done.37 = bf16[256,1024]{1,0:T(8,128)(2,1)S(1)} collective-permute-done((bf16[256,1024]{1,0:T(8,128)(2,1)S(1)}, bf16[256,1024]{1,0:T(8,128)(2,1)S(1)}, u32[]{:S(2)}, u32[]{:S(2)}) %collective-permute-start.37) | collective-permute-done | bytes 524320 | tf_op jit(solution)/shard_map/ppermute | solution.py:560
  120.4 6.7 %hidden_grad.1 = bf16[1024,1024]{1,0:T(8,128)(2,1)S(1)} custom-call(s32[1]{0:T(128)} %bitcast.3.z_ref, bf16[1024,1024]{1,0:T(8,128)(2,1)S(1)} %get-tuple-element.70.refs_0_, bf16[1024,1024]{1,0:T(8,128)(2,1)S(1)} %get-tuple-element.71.refs_1_, bf16[256,1024]{1,0:T(8,128)(2,1)S(1)} %maximum_select_fusion.1.refs_0_.refs_2_, ...), custom_call_target="tpu_custom_call" | custom-call | flops 4294967296 | bytes 8388608 | tf_op jit(solution)/shard_map/hidden_grad/pallas_call | solution.py:292
  127.3 5.8 %collective-permute-start.23 = (f32[8,128]{1,0:T(8,128)S(1)}, f32[8,128]{1,0:T(8,128)S(1)}, u32[]{:S(2)}, u32[]{:S(2)}) collective-permute-start(f32[8,128]{1,0:T(8,128)S(1)} %get-tuple-element.69.refs_0_), channel_id=1, source_target_pairs={{0,8},{4,12},{8,16},{12,20},{16,24},{20,28},{24,0},{28,4},{1,9},{5... | collective-permute-start | bytes 12296 | tf_op jit(solution)/shard_map/ppermute | solution.py:560
  138.8 3.9 %collective-permute-start.40 = (bf16[256,1024]{1,0:T(8,128)(2,1)S(1)}, bf16[256,1024]{1,0:T(8,128)(2,1)S(1)}, u32[]{:S(2)}, u32[]{:S(2)}) collective-permute-start(bf16[256,1024]{1,0:T(8,128)(2,1)S(1)} %fusion.5), channel_id=1, source_target_pairs={{0,8},{4,12},{24,16},{28,20},{1,9},{5,13},{25,17},{29,21},{2,10},{... | collective-permute-start | bytes 1572872 | tf_op jit(solution)/shard_map/ppermute | solution.py:560
  144.2 2.8 %collective-permute-start.31 = (bf16[256,1024]{1,0:T(8,128)(2,1)S(1)}, bf16[256,1024]{1,0:T(8,128)(2,1)S(1)}, u32[]{:S(2)}, u32[]{:S(2)}) collective-permute-start(bf16[256,1024]{1,0:T(8,128)(2,1)S(1)} %fusion.2), channel_id=1, source_target_pairs={{0,8},{4,12},{24,16},{28,20},{1,9},{5,13},{25,17},{29,21},{2,10},{... | collective-permute-start | bytes 1572872 | tf_op jit(solution)/shard_map/ppermute | solution.py:560
  147.9 7.2 %collective-permute-done.40 = bf16[256,1024]{1,0:T(8,128)(2,1)S(1)} collective-permute-done((bf16[256,1024]{1,0:T(8,128)(2,1)S(1)}, bf16[256,1024]{1,0:T(8,128)(2,1)S(1)}, u32[]{:S(2)}, u32[]{:S(2)}) %collective-permute-start.40) | collective-permute-done | bytes 524320 | tf_op jit(solution)/shard_map/ppermute | solution.py:560
  159.2 7.1 %collective-permute-done.31 = bf16[256,1024]{1,0:T(8,128)(2,1)S(1)} collective-permute-done((bf16[256,1024]{1,0:T(8,128)(2,1)S(1)}, bf16[256,1024]{1,0:T(8,128)(2,1)S(1)}, u32[]{:S(2)}, u32[]{:S(2)}) %collective-permute-start.31) | collective-permute-done | bytes 524320 | tf_op jit(solution)/shard_map/ppermute | solution.py:560
  167.7 2.5 %collective-permute-start.34 = (bf16[128,1024]{1,0:T(8,128)(2,1)S(1)}, bf16[128,1024]{1,0:T(8,128)(2,1)S(1)}, u32[]{:S(2)}, u32[]{:S(2)}) collective-permute-start(bf16[128,1024]{1,0:T(8,128)(2,1)S(1)} %get-tuple-element.87), channel_id=1, source_target_pairs={{0,8},{4,12},{8,0},{12,4},{16,24},{20,28},{24,16},{28,20},{1,9},{5... | collective-permute-start | bytes 786440 | tf_op jit(solution)/shard_map/ppermute | solution.py:560
  170.2 3.3 %collective-permute-done.29 = bf16[512,256]{1,0:T(8,128)(2,1)S(1)} collective-permute-done((bf16[512,256]{1,0:T(8,128)(2,1)S(1)}, bf16[512,256]{1,0:T(8,128)(2,1)S(1)}, u32[]{:S(2)}, u32[]{:S(2)}) %collective-permute-start.29) | collective-permute-done | bytes 262176 | tf_op jit(solution)/shard_map/ppermute | solution.py:568
  183.1 2.8 %collective-permute-done.36.refs_3_ = bf16[128,1024]{1,0:T(8,128)(2,1)S(1)} collective-permute-done((bf16[128,1024]{1,0:T(8,128)(2,1)S(1)}, bf16[128,1024]{1,0:T(8,128)(2,1)S(1)}, u32[]{:S(2)}, u32[]{:S(2)}) %collective-permute-start.36) | collective-permute-done | bytes 262176 | tf_op jit(solution)/shard_map/ppermute | solution.py:563
  (116 shorter events, 71.1 us)
Async XLA Ops:
  4.6 43.9 %collective-permute-start.7 = (bf16[512,2048]{1,0:T(8,128)(2,1)}, bf16[512,2048]{1,0:T(8,128)(2,1)}, u32[]{:S(2)}, u32[]{:S(2)}) collective-permute-start(bf16[512,2048]{1,0:T(8,128)(2,1)} %slice_select_fusion), channel_id=1, source_target_pairs={{0,4},{4,0},{8,12},{12,8},{16,20},{20,16},{24,28},{28,24},{1,5},{5... | collective-permute-start | bytes 6291464 | tf_op jit(solution)/shard_map/ppermute | solution.py:557
  9.6 15.9 %collective-permute-start.14 = (bf16[256,1024]{1,0:T(8,128)(2,1)S(1)}, bf16[256,1024]{1,0:T(8,128)(2,1)}, u32[]{:S(2)}, u32[]{:S(2)}) collective-permute-start(bf16[256,1024]{1,0:T(8,128)(2,1)S(1)} %maximum_select_fusion.1.refs_0_.refs_2_), channel_id=1, source_target_pairs={{8,0},{12,4},{0,8},{4,12},{24,16},{28,20},{16,24},{20,28},{9,1},{1... | collective-permute-start | bytes 1572872 | tf_op jit(solution)/shard_map/ppermute | solution.py:560
  12.6 29.5 %collective-permute-start.6 = (bf16[512,1024]{1,0:T(8,128)(2,1)}, bf16[512,1024]{1,0:T(8,128)(2,1)}, u32[]{:S(2)}, u32[]{:S(2)}) collective-permute-start(bf16[512,1024]{1,0:T(8,128)(2,1)} %param.4), channel_id=1, source_target_pairs={{0,4},{4,0},{8,12},{12,8},{16,20},{20,16},{24,28},{28,24},{1,5},{5... | collective-permute-start | bytes 3145736 | tf_op jit(solution)/shard_map/ppermute | solution.py:557
  14.1 12.0 %collective-permute-start.17 = (bf16[256,1024]{1,0:T(8,128)(2,1)S(1)}, bf16[256,1024]{1,0:T(8,128)(2,1)}, u32[]{:S(2)}, u32[]{:S(2)}) collective-permute-start(bf16[256,1024]{1,0:T(8,128)(2,1)S(1)} %maximum_select_fusion.1.refs_0_.refs_2_), channel_id=1, source_target_pairs={{16,8},{20,12},{8,16},{12,20},{17,9},{21,13},{9,17},{13,21},{18,10... | collective-permute-start | bytes 1572872 | tf_op jit(solution)/shard_map/ppermute | solution.py:560
  15.7 20.4 %collective-permute-start.1 = (bf16[256,1024]{1,0:T(8,128)(2,1)S(1)}, bf16[256,1024]{1,0:T(8,128)(2,1)}, u32[]{:S(2)}, u32[]{:S(2)}) collective-permute-start(bf16[256,1024]{1,0:T(8,128)(2,1)S(1)} %maximum_select_fusion.refs_0_.refs_8_), channel_id=1, source_target_pairs={{8,0},{12,4},{0,8},{4,12},{24,16},{28,20},{16,24},{20,28},{9,1},{1... | collective-permute-start | bytes 1572872 | tf_op jit(solution)/shard_map/ppermute | solution.py:560
  25.4 12.2 %collective-permute-start.4 = (bf16[256,1024]{1,0:T(8,128)(2,1)S(1)}, bf16[256,1024]{1,0:T(8,128)(2,1)S(1)}, u32[]{:S(2)}, u32[]{:S(2)}) collective-permute-start(bf16[256,1024]{1,0:T(8,128)(2,1)S(1)} %maximum_select_fusion.refs_0_.refs_8_), channel_id=1, source_target_pairs={{16,8},{20,12},{8,16},{12,20},{17,9},{21,13},{9,17},{13,21},{18,10... | collective-permute-start | bytes 1572872 | tf_op jit(solution)/shard_map/ppermute | solution.py:560
  26.1 18.2 %collective-permute-start.15 = (bf16[256,1024]{1,0:T(8,128)(2,1)}, bf16[256,1024]{1,0:T(8,128)(2,1)}, u32[]{:S(2)}, u32[]{:S(2)}) collective-permute-start(bf16[256,1024]{1,0:T(8,128)(2,1)} %collective-permute-done.14.refs_1_.refs_3_), channel_id=1, source_target_pairs={{16,8},{20,12},{8,16},{12,20},{17,9},{21,13},{9,17},{13,21},{18,10... | collective-permute-start | bytes 1572872 | tf_op jit(solution)/shard_map/ppermute | solution.py:560
  38.4 20.9 %collective-permute-start.18 = (bf16[256,1024]{1,0:T(8,128)(2,1)}, bf16[256,1024]{1,0:T(8,128)(2,1)}, u32[]{:S(2)}, u32[]{:S(2)}) collective-permute-start(bf16[256,1024]{1,0:T(8,128)(2,1)} %collective-permute-done.17.refs_2_.refs_4_), channel_id=1, source_target_pairs={{8,0},{12,4},{16,24},{20,28},{9,1},{13,5},{17,25},{21,29},{10,2},{... | collective-permute-start | bytes 1572872 | tf_op jit(solution)/shard_map/ppermute | solution.py:560
  42.0 28.4 %collective-permute-start.5 = (bf16[256,1024]{1,0:T(8,128)(2,1)}, bf16[256,1024]{1,0:T(8,128)(2,1)S(1)}, u32[]{:S(2)}, u32[]{:S(2)}) collective-permute-start(bf16[256,1024]{1,0:T(8,128)(2,1)} %copy-done.1), channel_id=1, source_target_pairs={{8,0},{12,4},{16,24},{20,28},{9,1},{13,5},{17,25},{21,29},{10,2},{... | collective-permute-start | bytes 1572872 | tf_op jit(solution)/shard_map/ppermute | solution.py:560
  44.4 37.2 %collective-permute-start.16 = (bf16[256,1024]{1,0:T(8,128)(2,1)}, bf16[256,1024]{1,0:T(8,128)(2,1)S(1)}, u32[]{:S(2)}, u32[]{:S(2)}) collective-permute-start(bf16[256,1024]{1,0:T(8,128)(2,1)} %collective-permute-done.15.refs_4_.refs_6_), channel_id=1, source_target_pairs={{8,0},{12,4},{16,24},{20,28},{9,1},{13,5},{17,25},{21,29},{10,2},{... | collective-permute-start | bytes 1572872 | tf_op jit(solution)/shard_map/ppermute | solution.py:560
  45.7 43.5 %collective-permute-start.3 = (bf16[256,1024]{1,0:T(8,128)(2,1)}, bf16[256,1024]{1,0:T(8,128)(2,1)S(1)}, u32[]{:S(2)}, u32[]{:S(2)}) collective-permute-start(bf16[256,1024]{1,0:T(8,128)(2,1)} %collective-permute-done.2.refs_4_.refs_12_), channel_id=1, source_target_pairs={{8,0},{12,4},{16,24},{20,28},{9,1},{13,5},{17,25},{21,29},{10,2},{... | collective-permute-start | bytes 1572872 | tf_op jit(solution)/shard_map/ppermute | solution.py:560
  63.5 13.4 %collective-permute-start.10 = (f32[8,1024]{1,0:T(8,128)S(1)}, f32[8,1024]{1,0:T(8,128)S(1)}, u32[]{:S(2)}, u32[]{:S(2)}) collective-permute-start(f32[8,1024]{1,0:T(8,128)S(1)} %fold.2.refs_0_), channel_id=1, source_target_pairs={{0,1},{1,0},{2,3},{3,2},{4,5},{5,4},{6,7},{7,6},{8,9},{9,8},{10,11... | collective-permute-start | bytes 98312 | tf_op jit(solution)/shard_map/ppermute | solution.py:568
  102.0 16.8 %collective-permute-start.37 = (bf16[256,1024]{1,0:T(8,128)(2,1)S(1)}, bf16[256,1024]{1,0:T(8,128)(2,1)S(1)}, u32[]{:S(2)}, u32[]{:S(2)}) collective-permute-start(bf16[256,1024]{1,0:T(8,128)(2,1)S(1)} %get-tuple-element.80), channel_id=1, source_target_pairs={{0,8},{4,12},{24,16},{28,20},{1,9},{5,13},{25,17},{29,21},{2,10},{... | collective-permute-start | bytes 1572872 | tf_op jit(solution)/shard_map/ppermute | solution.py:560
  107.6 35.2 %collective-permute-start.30 = (bf16[256,1024]{1,0:T(8,128)(2,1)S(1)}, bf16[256,1024]{1,0:T(8,128)(2,1)S(1)}, u32[]{:S(2)}, u32[]{:S(2)}) collective-permute-start(bf16[256,1024]{1,0:T(8,128)(2,1)S(1)} %get-tuple-element.68), channel_id=1, source_target_pairs={{0,8},{4,12},{24,16},{28,20},{1,9},{5,13},{25,17},{29,21},{2,10},{... | collective-permute-start | bytes 1572872 | tf_op jit(solution)/shard_map/ppermute | solution.py:560
  119.5 27.6 %collective-permute-start.38 = (bf16[256,1024]{1,0:T(8,128)(2,1)S(1)}, bf16[256,1024]{1,0:T(8,128)(2,1)S(1)}, u32[]{:S(2)}, u32[]{:S(2)}) collective-permute-start(bf16[256,1024]{1,0:T(8,128)(2,1)S(1)} %fusion.5), channel_id=1, source_target_pairs={{8,16},{12,20},{16,8},{20,12},{9,17},{13,21},{17,9},{21,13},{10,18... | collective-permute-start | bytes 1572872 | tf_op jit(solution)/shard_map/ppermute | solution.py:560
  127.2 29.2 %collective-permute-start.26 = (bf16[512,1024]{1,0:T(8,128)(2,1)S(1)}, bf16[512,1024]{1,0:T(8,128)(2,1)S(1)}, u32[]{:S(2)}, u32[]{:S(2)}) collective-permute-start(bf16[512,1024]{1,0:T(8,128)(2,1)S(1)} %slice.77), channel_id=1, source_target_pairs={{0,4},{4,0},{8,12},{12,8},{16,20},{20,16},{24,28},{28,24},{1,5},{5... | collective-permute-start | bytes 3145736 | tf_op jit(solution)/shard_map/ppermute | solution.py:557
  138.8 16.2 %collective-permute-start.40 = (bf16[256,1024]{1,0:T(8,128)(2,1)S(1)}, bf16[256,1024]{1,0:T(8,128)(2,1)S(1)}, u32[]{:S(2)}, u32[]{:S(2)}) collective-permute-start(bf16[256,1024]{1,0:T(8,128)(2,1)S(1)} %fusion.5), channel_id=1, source_target_pairs={{0,8},{4,12},{24,16},{28,20},{1,9},{5,13},{25,17},{29,21},{2,10},{... | collective-permute-start | bytes 1572872 | tf_op jit(solution)/shard_map/ppermute | solution.py:560
  143.5 14.3 %collective-permute-start.33 = (bf16[256,1024]{1,0:T(8,128)(2,1)S(1)}, bf16[256,1024]{1,0:T(8,128)(2,1)S(1)}, u32[]{:S(2)}, u32[]{:S(2)}) collective-permute-start(bf16[256,1024]{1,0:T(8,128)(2,1)S(1)} %fusion.2), channel_id=1, source_target_pairs={{8,16},{12,20},{16,8},{20,12},{9,17},{13,21},{17,9},{21,13},{10,18... | collective-permute-start | bytes 1572872 | tf_op jit(solution)/shard_map/ppermute | solution.py:560
  144.2 22.1 %collective-permute-start.31 = (bf16[256,1024]{1,0:T(8,128)(2,1)S(1)}, bf16[256,1024]{1,0:T(8,128)(2,1)S(1)}, u32[]{:S(2)}, u32[]{:S(2)}) collective-permute-start(bf16[256,1024]{1,0:T(8,128)(2,1)S(1)} %fusion.2), channel_id=1, source_target_pairs={{0,8},{4,12},{24,16},{28,20},{1,9},{5,13},{25,17},{29,21},{2,10},{... | collective-permute-start | bytes 1572872 | tf_op jit(solution)/shard_map/ppermute | solution.py:560
  147.8 29.7 %collective-permute-start.39 = (bf16[256,1024]{1,0:T(8,128)(2,1)S(1)}, bf16[256,1024]{1,0:T(8,128)(2,1)S(1)}, u32[]{:S(2)}, u32[]{:S(2)}) collective-permute-start(bf16[256,1024]{1,0:T(8,128)(2,1)S(1)} %fusion.4), channel_id=1, source_target_pairs={{0,8},{4,12},{8,0},{12,4},{16,24},{20,28},{24,16},{28,20},{1,9},{5... | collective-permute-start | bytes 1572872 | tf_op jit(solution)/shard_map/ppermute | solution.py:560
  155.8 21.8 %collective-permute-start.41 = (bf16[256,1024]{1,0:T(8,128)(2,1)S(1)}, bf16[256,1024]{1,0:T(8,128)(2,1)S(1)}, u32[]{:S(2)}, u32[]{:S(2)}) collective-permute-start(bf16[256,1024]{1,0:T(8,128)(2,1)S(1)} %fusion.6), channel_id=1, source_target_pairs={{8,16},{12,20},{16,8},{20,12},{9,17},{13,21},{17,9},{21,13},{10,18... | collective-permute-start | bytes 1572872 | tf_op jit(solution)/shard_map/ppermute | solution.py:560
  157.8 12.4 %collective-permute-start.28 = (bf16[512,256]{1,0:T(8,128)(2,1)S(1)}, bf16[512,256]{1,0:T(8,128)(2,1)S(1)}, u32[]{:S(2)}, u32[]{:S(2)}) collective-permute-start(bf16[512,256]{1,0:T(8,128)(2,1)S(1)} %get-tuple-element.83), channel_id=1, source_target_pairs={{0,2},{1,3},{2,0},{3,1},{4,6},{5,7},{6,4},{7,5},{8,10},{9,11},{10,... | collective-permute-start | bytes 786440 | tf_op jit(solution)/shard_map/ppermute | solution.py:568
  167.7 15.4 %collective-permute-start.34 = (bf16[128,1024]{1,0:T(8,128)(2,1)S(1)}, bf16[128,1024]{1,0:T(8,128)(2,1)S(1)}, u32[]{:S(2)}, u32[]{:S(2)}) collective-permute-start(bf16[128,1024]{1,0:T(8,128)(2,1)S(1)} %get-tuple-element.87), channel_id=1, source_target_pairs={{0,8},{4,12},{8,0},{12,4},{16,24},{20,28},{24,16},{28,20},{1,9},{5... | collective-permute-start | bytes 786440 | tf_op jit(solution)/shard_map/ppermute | solution.py:560
  170.2 15.7 %collective-permute-start.36 = (bf16[128,1024]{1,0:T(8,128)(2,1)S(1)}, bf16[128,1024]{1,0:T(8,128)(2,1)S(1)}, u32[]{:S(2)}, u32[]{:S(2)}) collective-permute-start(bf16[128,1024]{1,0:T(8,128)(2,1)S(1)} %get-tuple-element.86), channel_id=1, source_target_pairs={{0,12},{4,8},{8,4},{12,0},{16,28},{20,24},{24,20},{28,16},{1,13},{... | collective-permute-start | bytes 786440 | tf_op jit(solution)/shard_map/ppermute | solution.py:563
  (24 other events, 136.5 us)
